TPU v7x, 128 devices: a whole 4x4x4 slice. The times are simulated.
128 devices in a mesh: expert: 64 (over x, y, z), dp: 2 (over core).
Axes of the slice: x: 4, y: 4, z: 4, core: 2. Of those that a mesh axis runs over, the one named last changes fastest.
Arguments:
- tokens: bfloat16 [12288, 4096], P(('expert', 'dp')), may hold values from -6 to 6
- w_gate: bfloat16 [128, 4096, 768], P(('expert', 'dp')), may hold values from -0.09375 to 0.09375
- w_up: bfloat16 [128, 4096, 768], P(('expert', 'dp')), may hold values from -0.09375 to 0.09375
- w_down: bfloat16 [128, 768, 4096], P(('expert', 'dp')), may hold values from -0.21875 to 0.21875
- route_ids: int32 [12288, 8], P(('expert', 'dp')), may hold values from 0 to 127, all different within a row
- route_gates: float32 [12288, 8], P(('expert', 'dp')), may hold values from 0.05 to 0.4
- hot_experts: int32 [1], replicated, may hold values from 0 to 127
Outputs:
- mixed: bfloat16 [12288, 4096], P(('expert', 'dp'))
Inputs may be any that keep to these rules, and one draw needn't show every extreme that they name: `route_ids`: each row names 8 different experts.
All inputs are finite; a program needn't handle non-finite values.
Results may differ from a plain program's by a relative error of at most 0.007.
Values may be sent and summed in bfloat16 or wider, within the bound.
A program may use at most 192 MiB of HBM per device.

v0:
```python
import jax
import jax.numpy as jnp
from jax import lax
from jax.sharding import PartitionSpec as P

CAP = 6


def expert_ffn(in_rows, gate_w, up_w, down_w):
    gate_val = jnp.dot(in_rows, gate_w, preferred_element_type=jnp.float32)
    up_val = jnp.dot(in_rows, up_w, preferred_element_type=jnp.float32)
    hidden = (jax.nn.silu(gate_val) * up_val).astype(jnp.bfloat16)
    return jnp.dot(hidden, down_w, preferred_element_type=jnp.float32).astype(jnp.bfloat16)


def on_device(tokens, w_gate, w_up, w_down, route_ids, route_gates, hot_experts):
    feat_width = tokens.shape[1]
    tok_rows = tokens.shape[0]
    top_k = route_ids.shape[1]
    n_dp = lax.axis_size("dp")
    experts = lax.axis_size("expert") * n_dp
    hot_id = hot_experts[0]
    me = lax.axis_index("expert") * n_dp + lax.axis_index("dp")
    own = (w_gate[0], w_up[0], w_down[0])

    with jax.named_scope("hot_weight_broadcast"):
        is_root = me == hot_id
        hot_w = tuple(
            lax.psum(jnp.where(is_root, w, jnp.zeros_like(w)), ("expert", "dp")) for w in own
        )

    with jax.named_scope("routing"):
        flat_ids = route_ids.reshape(-1)
        labels = lax.iota(jnp.int32, experts)
        onehot = (flat_ids[:, None] == labels[None, :]).astype(jnp.int32)
        rank_of = jnp.sum(onehot * (jnp.cumsum(onehot, axis=0) - 1), axis=1)
        is_kept = (flat_ids != hot_id) & (rank_of < CAP)
        slot_of = jnp.where(is_kept, flat_ids * CAP + rank_of, experts * CAP)
        slots = lax.iota(jnp.int32, experts * CAP)
        hit = slot_of[None, :] == slots[:, None]
        dispatch = jnp.any(hit.reshape(experts * CAP, tok_rows, top_k), axis=2)

    with jax.named_scope("dispatch"):
        outgoing = jnp.dot(
            dispatch.astype(tokens.dtype), tokens, preferred_element_type=jnp.float32
        ).astype(tokens.dtype)
        to_send = outgoing.reshape(experts, CAP * feat_width)
        arrived = lax.all_to_all(to_send, ("expert", "dp"), 0, 0, tiled=True)

    with jax.named_scope("expert_ffn"):
        results = expert_ffn(arrived.reshape(-1, feat_width), *own)

    with jax.named_scope("return"):
        come_back = lax.all_to_all(
            results.reshape(experts, CAP * feat_width), ("expert", "dp"), 0, 0, tiled=True
        )
        returned = come_back.reshape(experts * CAP, feat_width)

    with jax.named_scope("combine"):
        gate_flat = route_gates.reshape(-1)
        cold_weight = jnp.where(is_kept, gate_flat, jnp.zeros_like(gate_flat))
        weight_of_slot = jnp.where(hit, cold_weight[None, :], 0.0)
        combine = jnp.sum(weight_of_slot.reshape(experts * CAP, tok_rows, top_k), axis=2).T
        cold_sum = jnp.dot(
            combine,
            returned.astype(jnp.float32),
            precision=lax.Precision.HIGHEST,
            preferred_element_type=jnp.float32,
        )

    with jax.named_scope("hot_expert"):
        hot_out = expert_ffn(tokens, *hot_w)
        hot_weight = jnp.sum(
            jnp.where(route_ids == hot_id, route_gates, jnp.zeros_like(route_gates)), axis=1
        )
        combined = cold_sum + hot_weight[:, None] * hot_out.astype(jnp.float32)
    return combined.astype(jnp.bfloat16)


def solution(mesh):
    in_specs = (
        P(("expert", "dp"), None),
        P(("expert", "dp"), None, None),
        P(("expert", "dp"), None, None),
        P(("expert", "dp"), None, None),
        P(("expert", "dp"), None),
        P(("expert", "dp"), None),
        P(),
    )
    out_specs = P(("expert", "dp"), None)
    return jax.shard_map(
        on_device, mesh=mesh, in_specs=in_specs, out_specs=out_specs, check_vma=False
    )
```

profile of v0, /device:TPU:0, one launch (start us, length us, event | category | flops | bytes accessed | tf_op | source)
XLA Modules:
  0.0 559.9 jit_solution(3620452224844530923)
XLA Ops:
  10.8 4.5 convolution_convert_fusion
  15.2 23.8 %all_to_all.16 = bf16[128,1,24576]{2,1,0:T(2,128)(2,1)} reshape(bf16[768,4096]{1,0:T(8,128)(2,1)} %convolution_convert_fusion) | data formatting | bytes 12582912 | tf_op jit(solution)/shard_map/dispatch/all_to_all | solution.py:48
  39.4 38.9 %reduce.2 = bf16[128,24576]{1,0:T(8,128)(2,1)} reduce(bf16[128,1,24576]{2,1,0:T(2,128)(2,1)} %all_to_all.16, bf16[]{:T(256)} %broadcast.85), dimensions={1}, to_apply=%all_to_all.16.reduce_sub_computation | reduce | bytes 12582914 | tf_op jit(solution)/shard_map/dispatch/all_to_all | solution.py:48
  78.3 9.4 %reshape.90 = bf16[128,2,12288]{2,1,0:T(2,128)(2,1)} reshape(bf16[128,24576]{1,0:T(8,128)(2,1)} %reduce.2) | data formatting | bytes 12582912
  87.7 11.6 %all-to-all-start = ((bf16[128,2,12288]{2,1,0:T(2,128)(2,1)}), bf16[128,2,12288]{2,1,0:T(2,128)(2,1)}, u32[]{:S(2)}, u32[]{:S(2)}) async-start(bf16[128,2,12288]{2,1,0:T(2,128)(2,1)} %reshape.90), calls=%async_computation | async-start | bytes 12582912 | tf_op jit(solution)/shard_map/dispatch/all_to_all | solution.py:48
  99.4 5.9 %bitcast_select_fusion = bf16[768,4096]{1,0:T(8,128)(2,1)} fusion(bf16[1,768,4096]{2,1,0:T(8,128)(2,1)} %param.10, pred[]{:T(512)S(6)} %eq.59), kind=kLoop, calls=%fused_computation.2 | loop fusion | flops 3145728 | bytes 12582913 | tf_op jit(solution)/shard_map/hot_weight_broadcast/jit(_where)/select_n | solution.py:29
  105.3 9.9 %bitcast_select_fusion.1 = (bf16[4096,768]{1,0:T(8,128)(2,1)}, bf16[4096,768]{1,0:T(8,128)(2,1)}) fusion(bf16[1,4096,768]{2,1,0:T(8,128)(2,1)} %param.9, pred[]{:T(512)S(6)} %eq.59, bf16[1,4096,768]{2,1,0:T(8,128)(2,1)} %param.8), kind=kLoop, calls=%fused_computation.4 | loop fusion | flops 6291456 | bytes 25165824 | tf_op jit(solution)/shard_map/hot_weight_broadcast/jit(_where)/select_n | solution.py:29
  115.1 65.2 %all-to-all-done = bf16[128,2,12288]{2,1,0:T(2,128)(2,1)} async-done(((bf16[128,2,12288]{2,1,0:T(2,128)(2,1)}), bf16[128,2,12288]{2,1,0:T(2,128)(2,1)}, u32[]{:S(2)}, u32[]{:S(2)}) %all-to-all-start) | async-done | bytes 6291488 | tf_op jit(solution)/shard_map/dispatch/all_to_all | solution.py:48
  180.4 34.5 %reshape.91 = bf16[128,1,24576]{2,1,0:T(2,128)(2,1)} reshape(bf16[128,2,12288]{2,1,0:T(2,128)(2,1)} %all-to-all-done) | data formatting | bytes 12582912
  214.8 38.3 %reduce = bf16[128,24576]{1,0:T(8,128)(2,1)} reduce(bf16[128,1,24576]{2,1,0:T(2,128)(2,1)} %reshape.91, bf16[]{:T(256)} %constant.43), dimensions={1}, to_apply=%all_to_all.13.reduce_sub_computation | reduce | bytes 12582914 | tf_op jit(solution)/shard_map/dispatch/all_to_all | solution.py:48
  253.2 11.2 %reshape.86 = bf16[768,4096]{1,0:T(8,128)(2,1)} reshape(bf16[128,24576]{1,0:T(8,128)(2,1)} %reduce) | data formatting | bytes 12582912 | tf_op jit(solution)/shard_map/expert_ffn/reshape | solution.py:51
  264.4 9.1 %fusion.3 = f32[768,768]{1,0:T(8,128)S(1)} fusion(bf16[768,4096]{1,0:T(8,128)(2,1)} %reshape.86, bf16[1,4096,768]{2,1,0:T(8,128)(2,1)} %param.8), kind=kOutput, calls=%fused_computation.8 | convolution fusion | flops 4831838208 | bytes 14942208 | tf_op jit(solution)/shard_map/expert_ffn/dot_general | solution.py:10
  273.5 8.0 %multiply_convert_fusion = bf16[768,768]{1,0:T(8,128)(2,1)S(1)} fusion(f32[768,768]{1,0:T(8,128)S(1)} %fusion.3, bf16[768,4096]{1,0:T(8,128)(2,1)S(1)} %copy-done.1, bf16[1,4096,768]{2,1,0:T(8,128)(2,1)} %param.9), kind=kOutput, calls=%fused_computation.15 | convolution fusion | flops 4835377152 | bytes 16121856 | tf_op jit(solution)/shard_map/expert_ffn/dot_general | solution.py:11
  281.6 7.1 %convolution_convert_fusion.1 = bf16[768,4096]{1,0:T(8,128)(2,1)} fusion(bf16[768,768]{1,0:T(8,128)(2,1)S(1)} %multiply_convert_fusion, bf16[1,768,4096]{2,1,0:T(8,128)(2,1)S(1)} %bitcast.50), kind=kOutput, calls=%fused_computation.1 | convolution fusion | flops 4834983936 | bytes 13762560 | tf_op jit(solution)/shard_map/expert_ffn/dot_general | solution.py:13
  288.7 23.9 %all_to_all.17 = bf16[128,1,24576]{2,1,0:T(2,128)(2,1)} reshape(bf16[768,4096]{1,0:T(8,128)(2,1)} %convolution_convert_fusion.1) | data formatting | bytes 12582912 | tf_op jit(solution)/shard_map/return/all_to_all | solution.py:54
  312.5 38.8 %reduce.3 = bf16[128,24576]{1,0:T(8,128)(2,1)} reduce(bf16[128,1,24576]{2,1,0:T(2,128)(2,1)} %all_to_all.17, bf16[]{:T(256)} %broadcast.85), dimensions={1}, to_apply=%all_to_all.17.reduce_sub_computation | reduce | bytes 12582914 | tf_op jit(solution)/shard_map/return/all_to_all | solution.py:54
  351.4 9.7 %reshape.92 = bf16[128,2,12288]{2,1,0:T(2,128)(2,1)} reshape(bf16[128,24576]{1,0:T(8,128)(2,1)} %reduce.3) | data formatting | bytes 12582912
  361.1 7.8 %all-to-all-start.1 = ((bf16[128,2,12288]{2,1,0:T(2,128)(2,1)}), bf16[128,2,12288]{2,1,0:T(2,128)(2,1)}, u32[]{:S(2)}, u32[]{:S(2)}) async-start(bf16[128,2,12288]{2,1,0:T(2,128)(2,1)} %reshape.92), calls=%async_computation.1 | async-start | bytes 12582912 | tf_op jit(solution)/shard_map/return/all_to_all | solution.py:54
  369.8 81.9 %all-reduce.3.cloned.1.call-done = (bf16[768,4096]{1,0:T(8,128)(2,1)}, bf16[4096,768]{1,0:T(8,128)(2,1)}, bf16[4096,768]{1,0:T(8,128)(2,1)}) async-done(((bf16[768,4096]{1,0:T(8,128)(2,1)}, bf16[4096,768]{1,0:T(8,128)(2,1)}, bf16[4096,768]{1,0:T(8,128)(2,1)}), (bf16[768,4096]{1,0:T(8,128)(2,1)}, bf16[4096,768]{1,0:T(8,128)(2,1)}, bf16[4096,768]{1,0:T(8,128)(2,1)})) %all-reduce.3.cloned.1.call-update) | async-done | bytes 18874384 | tf_op jit(solution)/shard_map/hot_weight_broadcast/psum | solution.py:29
  455.6 7.1 %fusion.7 = f32[96,4096]{1,0:T(8,128)S(1)} fusion(bf16[768,4096]{1,0:T(8,128)(2,1)} %get-tuple-element.5, bf16[96,4096]{1,0:T(8,128)(2,1)S(1)} %copy-done, bf16[4096,768]{1,0:T(8,128)(2,1)} %get-tuple-element.6, f32[96]{0:T(128)S(1)} %get-tuple-element.9, f32[96,768]{1,0:T(8,128)S(1)} %convolution_bitcast_fusion.1), kind=kOutput, calls=%fused_computation.14 | convolution fusion | flops 1209581568 | bytes 15237504 | tf_op jit(solution)/shard_map/hot_expert/dot_general | solution.py:13
  462.8 33.8 %reshape.93 = bf16[128,1,24576]{2,1,0:T(2,128)(2,1)} reshape(bf16[128,2,12288]{2,1,0:T(2,128)(2,1)} %all-to-all-done.1) | data formatting | bytes 12582912
  496.6 38.3 %reduce.1 = bf16[128,24576]{1,0:T(8,128)(2,1)} reduce(bf16[128,1,24576]{2,1,0:T(2,128)(2,1)} %reshape.93, bf16[]{:T(256)} %constant.43), dimensions={1}, to_apply=%all_to_all.15.reduce_sub_computation | reduce | bytes 12582914 | tf_op jit(solution)/shard_map/return/all_to_all | solution.py:54
  534.9 11.1 %reshape.87 = bf16[768,4096]{1,0:T(8,128)(2,1)} reshape(bf16[128,24576]{1,0:T(8,128)(2,1)} %reduce.1) | data formatting | bytes 12582912 | tf_op jit(solution)/shard_map/return/reshape | solution.py:57
  546.0 6.8 %fusion.5 = bf16[96,4096]{1,0:T(8,128)(2,1)} fusion(f32[96,4096]{1,0:T(8,128)S(1)} %fusion.7, f32[768,96]{0,1:T(8,128)S(1)} %select_reduce_fusion, bf16[768,4096]{1,0:T(8,128)(2,1)} %reshape.87), kind=kOutput, calls=%fused_computation.11 | convolution fusion | flops 3624665088 | bytes 8945664 | tf_op jit(solution)/shard_map/combine/dot_general | solution.py:64
  (36 shorter events, 8.9 us)
Async XLA Ops:
  6.5 4.2 copy-start
  87.7 92.7 %all-to-all-start = ((bf16[128,2,12288]{2,1,0:T(2,128)(2,1)}), bf16[128,2,12288]{2,1,0:T(2,128)(2,1)}, u32[]{:S(2)}, u32[]{:S(2)}) async-start(bf16[128,2,12288]{2,1,0:T(2,128)(2,1)} %reshape.90), calls=%async_computation | async-start | bytes 12582912 | tf_op jit(solution)/shard_map/dispatch/all_to_all | solution.py:48
  99.3 352.4 %all-reduce.3.cloned.1.call-start = ((), (), s32[]{:S(2)}) async-start(), calls=%async_computation.2 | async-start | bytes 37748736 | tf_op jit(solution)/shard_map/hot_weight_broadcast/psum | solution.py:29
  253.2 28.4 %slice-start = ((s8[6291456]{0:T(1024)(128)(4,1)}), s8[2097152]{0:T(1024)(128)(4,1)S(1)}, s32[]{:S(2)}) async-start(s8[6291456]{0:T(1024)(128)(4,1)} %bitcast.49), calls=%async_computation.3 | async-start | bytes 4194304
  264.4 9.1 %copy-start.1 = (bf16[768,4096]{1,0:T(8,128)(2,1)S(1)}, bf16[768,4096]{1,0:T(8,128)(2,1)}, u32[]{:S(2)}) copy-start(bf16[768,4096]{1,0:T(8,128)(2,1)} %reshape.86) | copy-start | bytes 18874372
  264.4 17.2 %slice-start.1 = ((s8[6291456]{0:T(1024)(128)(4,1)}), s8[4194304]{0:T(1024)(128)(4,1)S(1)}, s32[]{:S(2)}) async-start(s8[6291456]{0:T(1024)(128)(4,1)} %bitcast.49), calls=%async_computation.4 | async-start | bytes 8388608
  361.1 7.8 %copy-start.2 = (s32[96,8]{0,1:T(8,128)S(1)}, s32[96,8]{0,1:T(8,128)}, u32[]{:S(2)}) copy-start(s32[96,8]{0,1:T(8,128)} %param.11) | copy-start | bytes 9220
  361.1 7.8 %copy-start.3 = (f32[96,8]{0,1:T(8,128)S(1)}, f32[96,8]{0,1:T(8,128)}, u32[]{:S(2)}) copy-start(f32[96,8]{0,1:T(8,128)} %param.12) | copy-start | bytes 9220
  361.1 101.7 %all-to-all-start.1 = ((bf16[128,2,12288]{2,1,0:T(2,128)(2,1)}), bf16[128,2,12288]{2,1,0:T(2,128)(2,1)}, u32[]{:S(2)}, u32[]{:S(2)}) async-start(bf16[128,2,12288]{2,1,0:T(2,128)(2,1)} %reshape.92), calls=%async_computation.1 | async-start | bytes 12582912 | tf_op jit(solution)/shard_map/return/all_to_all | solution.py:54
Sparse Core Ops, SparseCore 0:
  115.3 336.3 all-reduce.2
where the time goes:
time: 571 us; the launch traced here: 560 us
  other arithmetic  173 us (30%)
  local copies, waits for them, and re-layouts  159 us (28%)
  waiting for transfers between devices  147 us (26%)
  matrix products  46.5 us (8%)
  starting transfers between devices  19.5 us (3%)
  between operations  14.5 us (3%)
    unnamed x17, local copies, waits for them, and re-layouts  88.2 us
    psum x1, waiting for transfers between devices, on_device(): lax.psum(jnp.where(is_root, w, jnp.zeros_like(w)), ('expert', 'dp'))  81.9 us
    all_to_all x2, other arithmetic, on_device(): arrived = lax.all_to_all(to_send, ('expert', 'dp'), 0, 0, tiled=True)  77.2 us
    all_to_all x2, other arithmetic, on_device(): lax.all_to_all(results.reshape(experts, CAP * feat_width), ('expert', 'dp...  77.2 us
    all_to_all x1, waiting for transfers between devices, on_device(): arrived = lax.all_to_all(to_send, ('expert', 'dp'), 0, 0, tiled=True)  65.2 us
    all_to_all x2, local copies, waits for them, and re-layouts, on_device(): arrived = lax.all_to_all(to_send, ('expert', 'dp'), 0, 0, tiled=True)  24.2 us
    all_to_all x1, local copies, waits for them, and re-layouts, on_device(): lax.all_to_all(results.reshape(experts, CAP * feat_width), ('expert', 'dp...  23.9 us
    select_n x2, other arithmetic, on_device(): jnp.where(is_root, w, jnp.zeros_like(w))  15.8 us
  transfers between devices with their start and end apart: 3, of which 2 were waited for; matrix products, arithmetic and copies ran while one was open for 33% of the time, Pallas kernels for 0%

commit v1 on v0

--- a/solution.py
+++ b/solution.py
@@ -1,9 +1,71 @@
+import functools
 import jax
 import jax.numpy as jnp
 from jax import lax
 from jax.sharding import PartitionSpec as P
+from jax.experimental import pallas as pl
+from jax.experimental.pallas import tpu as pltpu
+
 
 CAP = 6
+MESH = pl.DeviceIdType.MESH
+
+
+def a2a_kernel(n_dp, x_ref, y_ref, send_sem, recv_sem, local_sem):
+    n = x_ref.shape[0]
+    me = lax.axis_index("expert") * n_dp + lax.axis_index("dp")
+
+    def peer_copy(src, dst, slot, peer):
+        return pltpu.make_async_remote_copy(
+            src_ref=x_ref.at[src],
+            dst_ref=y_ref.at[dst],
+            send_sem=send_sem.at[slot],
+            recv_sem=recv_sem.at[slot],
+            device_id=(peer // n_dp, peer % n_dp),
+            device_id_type=MESH,
+        )
+
+    local = pltpu.make_async_copy(x_ref.at[me], y_ref.at[me], local_sem)
+    local.start()
+
+    def start(k, carry):
+        peer = lax.rem(me + k, n)
+        pltpu.make_async_remote_copy(
+            src_ref=x_ref.at[peer],
+            dst_ref=y_ref.at[me],
+            send_sem=send_sem.at[peer],
+            recv_sem=recv_sem.at[me],
+            device_id=(peer // n_dp, peer % n_dp),
+            device_id_type=MESH,
+        ).start()
+        return carry
+
+    lax.fori_loop(1, n, start, 0)
+
+    def finish(k, carry):
+        peer = lax.rem(me + k, n)
+        peer_copy(peer, peer, peer, peer).wait_send()
+        peer_copy(peer, peer, peer, peer).wait_recv()
+        return carry
+
+    lax.fori_loop(1, n, finish, 0)
+    local.wait()
+
+
+def all_to_all_slabs(x, n_dp):
+    n = x.shape[0]
+    return pl.pallas_call(
+        functools.partial(a2a_kernel, n_dp),
+        out_shape=jax.ShapeDtypeStruct(x.shape, x.dtype),
+        in_specs=[pl.BlockSpec(memory_space=pl.ANY)],
+        out_specs=pl.BlockSpec(memory_space=pl.ANY),
+        scratch_shapes=[
+            pltpu.SemaphoreType.DMA((n,)),
+            pltpu.SemaphoreType.DMA((n,)),
+            pltpu.SemaphoreType.DMA(()),
+        ],
+        compiler_params=pltpu.CompilerParams(has_side_effects=True),
+    )(x)
 
 
 def expert_ffn(in_rows, gate_w, up_w, down_w):
@@ -44,16 +106,13 @@
         outgoing = jnp.dot(
             dispatch.astype(tokens.dtype), tokens, preferred_element_type=jnp.float32
         ).astype(tokens.dtype)
-        to_send = outgoing.reshape(experts, CAP * feat_width)
-        arrived = lax.all_to_all(to_send, ("expert", "dp"), 0, 0, tiled=True)
+        arrived = all_to_all_slabs(outgoing.reshape(experts, CAP, feat_width), n_dp)
 
     with jax.named_scope("expert_ffn"):
         results = expert_ffn(arrived.reshape(-1, feat_width), *own)
 
     with jax.named_scope("return"):
-        come_back = lax.all_to_all(
-            results.reshape(experts, CAP * feat_width), ("expert", "dp"), 0, 0, tiled=True
-        )
+        come_back = all_to_all_slabs(results.reshape(experts, CAP, feat_width), n_dp)
         returned = come_back.reshape(experts * CAP, feat_width)
 
     with jax.named_scope("combine"):

time: 571 us -> 664 us (1.16)
  the two profiles are of different devices: /device:TPU:0 before, /device:TPU:1 now
where the time goes in v1:
time: 664 us; the launch traced here: 663 us
  Pallas kernels  446 us (67%)
  waiting for transfers between devices  95.3 us (14%)
  matrix products  46.7 us (7%)
  local copies, waits for them, and re-layouts  42.6 us (6%)
  other arithmetic  17.9 us (3%)
  between operations  14.3 us (2%)
    pallas_call x2, Pallas kernels, all_to_all_slabs(): pl.pallas_call(functools.partial(a2a_kernel, n_dp), out_shape=jax.ShapeDt...  446 us
    psum x1, waiting for transfers between devices, on_device(): lax.psum(jnp.where(is_root, w, jnp.zeros_like(w)), ('expert', 'dp'))  95.3 us
    select_n x2, other arithmetic, on_device(): jnp.where(is_root, w, jnp.zeros_like(w))  15.7 us
    dot_general x2, matrix products, expert_ffn(): jnp.dot(hidden, down_w, preferred_element_type=jnp.float32)  14.1 us
  transfers between devices with their start and end apart: 1, of which 1 were waited for; matrix products, arithmetic and copies ran while one was open for 11% of the time, Pallas kernels for 67%

profile of v1, /device:TPU:1, one launch (start us, length us, event | category | flops | bytes accessed | tf_op | source)
XLA Modules:
  0.0 663.0 jit_solution(5596524427408404416)
XLA Ops:
  7.3 5.8 bitcast_select_fusion
  13.0 10.0 %bitcast_select_fusion.1 = (bf16[4096,768]{1,0:T(8,128)(2,1)}, bf16[4096,768]{1,0:T(8,128)(2,1)}) fusion(bf16[1,4096,768]{2,1,0:T(8,128)(2,1)} %param.9, pred[]{:T(512)S(6)} %eq.59, bf16[1,4096,768]{2,1,0:T(8,128)(2,1)} %param.8), kind=kLoop, calls=%fused_computation.4 | loop fusion | flops 6291456 | bytes 25165824 | tf_op jit(solution)/shard_map/hot_weight_broadcast/jit(_where)/select_n | solution.py:91
  23.0 0.7 copy-done.2
  23.7 0.1 copy.34
  24.0 0.1 copy.36
  24.1 0.2 fusion.13
  24.5 0.3 fusion.15
  24.9 0.1 copy.40
  25.0 0.8 fusion.8
  25.8 4.6 convolution_convert_fusion
  30.4 10.2 %reshape.82.x_ref = bf16[128,6,4096]{2,1,0:T(8,128)(2,1)} reshape(bf16[768,4096]{1,0:T(8,128)(2,1)} %convolution_convert_fusion) | data formatting | bytes 12582912 | tf_op jit(solution)/shard_map/dispatch/reshape | solution.py:109
  40.6 190.0 %dispatch.1 = bf16[128,6,4096]{2,1,0:T(8,128)(2,1)} custom-call(bf16[128,6,4096]{2,1,0:T(8,128)(2,1)} %reshape.82.x_ref), custom_call_target="tpu_custom_call" | custom-call | tf_op jit(solution)/shard_map/dispatch/pallas_call | solution.py:57
  230.6 10.5 %reshape.83 = bf16[768,4096]{1,0:T(8,128)(2,1)} reshape(bf16[128,6,4096]{2,1,0:T(8,128)(2,1)} %dispatch.1) | data formatting | bytes 12582912 | tf_op jit(solution)/shard_map/expert_ffn/reshape | solution.py:112
  241.1 9.2 %fusion.3 = f32[768,768]{1,0:T(8,128)S(1)} fusion(bf16[768,4096]{1,0:T(8,128)(2,1)} %reshape.83, bf16[1,4096,768]{2,1,0:T(8,128)(2,1)} %param.8), kind=kOutput, calls=%fused_computation.8 | convolution fusion | flops 4831838208 | bytes 14942208 | tf_op jit(solution)/shard_map/expert_ffn/dot_general | solution.py:72
  250.3 8.2 %multiply_convert_fusion = bf16[768,768]{1,0:T(8,128)(2,1)S(1)} fusion(f32[768,768]{1,0:T(8,128)S(1)} %fusion.3, bf16[768,4096]{1,0:T(8,128)(2,1)S(1)} %copy-done.1, bf16[1,4096,768]{2,1,0:T(8,128)(2,1)} %param.9), kind=kOutput, calls=%fused_computation.15 | convolution fusion | flops 4835377152 | bytes 16121856 | tf_op jit(solution)/shard_map/expert_ffn/dot_general | solution.py:73
  258.5 6.9 %convolution_convert_fusion.1 = bf16[768,4096]{1,0:T(8,128)(2,1)} fusion(bf16[768,768]{1,0:T(8,128)(2,1)S(1)} %multiply_convert_fusion, bf16[1,768,4096]{2,1,0:T(8,128)(2,1)S(1)} %bitcast.50), kind=kOutput, calls=%fused_computation.1 | convolution fusion | flops 4834983936 | bytes 13762560 | tf_op jit(solution)/shard_map/expert_ffn/dot_general | solution.py:75
  265.5 10.1 %reshape.84.x_ref = bf16[128,6,4096]{2,1,0:T(8,128)(2,1)} reshape(bf16[768,4096]{1,0:T(8,128)(2,1)} %convolution_convert_fusion.1) | data formatting | bytes 12582912 | tf_op jit(solution)/shard_map/return/reshape | solution.py:115
  275.6 256.2 %return.1 = bf16[128,6,4096]{2,1,0:T(8,128)(2,1)} custom-call(bf16[128,6,4096]{2,1,0:T(8,128)(2,1)} %reshape.84.x_ref), custom_call_target="tpu_custom_call" | custom-call | tf_op jit(solution)/shard_map/return/pallas_call | solution.py:57
  531.8 10.3 %reshape.85 = bf16[768,4096]{1,0:T(8,128)(2,1)} reshape(bf16[128,6,4096]{2,1,0:T(8,128)(2,1)} %return.1) | data formatting | bytes 12582912 | tf_op jit(solution)/shard_map/return/reshape | solution.py:116
  542.2 0.8 select_reduce_fusion
  543.0 95.3 %all-reduce.3.cloned.1.call-done = (bf16[768,4096]{1,0:T(8,128)(2,1)}, bf16[4096,768]{1,0:T(8,128)(2,1)}, bf16[4096,768]{1,0:T(8,128)(2,1)}) async-done(((bf16[768,4096]{1,0:T(8,128)(2,1)}, bf16[4096,768]{1,0:T(8,128)(2,1)}, bf16[4096,768]{1,0:T(8,128)(2,1)}), (bf16[768,4096]{1,0:T(8,128)(2,1)}, bf16[4096,768]{1,0:T(8,128)(2,1)}, bf16[4096,768]{1,0:T(8,128)(2,1)})) %all-reduce.3.cloned.1.call-update) | async-done | bytes 18874384 | tf_op jit(solution)/shard_map/hot_weight_broadcast/psum | solution.py:91
  638.3 3.9 convolution_bitcast_fusion.1
  642.2 7.1 %fusion.7 = f32[96,4096]{1,0:T(8,128)S(1)} fusion(bf16[768,4096]{1,0:T(8,128)(2,1)} %get-tuple-element.5, bf16[96,4096]{1,0:T(8,128)(2,1)S(1)} %copy-done, bf16[4096,768]{1,0:T(8,128)(2,1)} %get-tuple-element.6, f32[96]{0:T(128)S(1)} %get-tuple-element.9, f32[96,768]{1,0:T(8,128)S(1)} %convolution_bitcast_fusion.1), kind=kOutput, calls=%fused_computation.14 | convolution fusion | flops 1209581568 | bytes 15237504 | tf_op jit(solution)/shard_map/hot_expert/dot_general | solution.py:75
  649.3 6.8 %fusion.5 = bf16[96,4096]{1,0:T(8,128)(2,1)} fusion(f32[96,4096]{1,0:T(8,128)S(1)} %fusion.7, f32[768,96]{0,1:T(8,128)S(1)} %select_reduce_fusion, bf16[768,4096]{1,0:T(8,128)(2,1)} %reshape.85), kind=kOutput, calls=%fused_computation.11 | convolution fusion | flops 3624665088 | bytes 8945664 | tf_op jit(solution)/shard_map/combine/dot_general | solution.py:123
  (25 shorter events, 0.6 us)
Async XLA Ops:
  6.5 19.3 %copy-start = (bf16[96,4096]{1,0:T(8,128)(2,1)S(1)}, bf16[96,4096]{1,0:T(8,128)(2,1)}, u32[]{:S(2)}) copy-start(bf16[96,4096]{1,0:T(8,128)(2,1)} %param.7) | copy-start | bytes 2359300
  6.5 631.7 %all-reduce.3.cloned.1.call-start = ((), (), s32[]{:S(2)}) async-start(), calls=%async_computation | async-start | bytes 37748736 | tf_op jit(solution)/shard_map/hot_weight_broadcast/psum | solution.py:91
  23.0 0.7 copy-start.2
  230.6 27.9 %slice-start = ((s8[6291456]{0:T(1024)(128)(4,1)}), s8[2097152]{0:T(1024)(128)(4,1)S(1)}, s32[]{:S(2)}) async-start(s8[6291456]{0:T(1024)(128)(4,1)} %bitcast.49), calls=%async_computation.1 | async-start | bytes 4194304
  241.1 9.2 %copy-start.1 = (bf16[768,4096]{1,0:T(8,128)(2,1)S(1)}, bf16[768,4096]{1,0:T(8,128)(2,1)}, u32[]{:S(2)}) copy-start(bf16[768,4096]{1,0:T(8,128)(2,1)} %reshape.83) | copy-start | bytes 18874372
  241.1 17.4 %slice-start.1 = ((s8[6291456]{0:T(1024)(128)(4,1)}), s8[4194304]{0:T(1024)(128)(4,1)S(1)}, s32[]{:S(2)}) async-start(s8[6291456]{0:T(1024)(128)(4,1)} %bitcast.49), calls=%async_computation.2 | async-start | bytes 8388608
  531.8 10.3 %copy-start.3 = (f32[96,8]{0,1:T(8,128)S(1)}, f32[96,8]{0,1:T(8,128)}, u32[]{:S(2)}) copy-start(f32[96,8]{0,1:T(8,128)} %param.12) | copy-start | bytes 9220
Sparse Core Ops, SparseCore 0:
  23.1 615.0 all-reduce.2

commit v2 on v1

--- a/solution.py
+++ b/solution.py
@@ -76,7 +76,6 @@
 
 
 def on_device(tokens, w_gate, w_up, w_down, route_ids, route_gates, hot_experts):
-    feat_width = tokens.shape[1]
     tok_rows = tokens.shape[0]
     top_k = route_ids.shape[1]
     n_dp = lax.axis_size("dp")
@@ -85,42 +84,49 @@
     me = lax.axis_index("expert") * n_dp + lax.axis_index("dp")
     own = (w_gate[0], w_up[0], w_down[0])
 
+    with jax.named_scope("routing"):
+        flat_ids = route_ids.reshape(-1)
+        labels = lax.iota(jnp.int32, experts)
+        onehot = (flat_ids[:, None] == labels[None, :]).astype(jnp.int32)
+        rank_of = jnp.sum(onehot * (jnp.cumsum(onehot, axis=0) - 1), axis=1)
+        is_kept = (flat_ids != hot_id) & (rank_of < CAP)
+        slot_rank = lax.iota(jnp.int32, CAP)
+        hit = (flat_ids[None, None, :] == labels[:, None, None]) & (
+            rank_of[None, None, :] == slot_rank[None, :, None]
+        ) & is_kept[None, None, :]
+        dispatch = jnp.any(hit.reshape(experts, CAP, tok_rows, top_k), axis=3)
+
+    with jax.named_scope("dispatch"):
+        outgoing = jnp.einsum(
+            "esp,pd->esd", dispatch.astype(tokens.dtype), tokens,
+            preferred_element_type=jnp.float32,
+        ).astype(tokens.dtype)
+        arrived = lax.all_to_all(outgoing, ("expert", "dp"), 0, 0, tiled=True)
+
     with jax.named_scope("hot_weight_broadcast"):
         is_root = me == hot_id
         hot_w = tuple(
             lax.psum(jnp.where(is_root, w, jnp.zeros_like(w)), ("expert", "dp")) for w in own
         )
 
-    with jax.named_scope("routing"):
-        flat_ids = route_ids.reshape(-1)
-        labels = lax.iota(jnp.int32, experts)
-        onehot = (flat_ids[:, None] == labels[None, :]).astype(jnp.int32)
-        rank_of = jnp.sum(onehot * (jnp.cumsum(onehot, axis=0) - 1), axis=1)
-        is_kept = (flat_ids != hot_id) & (rank_of < CAP)
-        slot_of = jnp.where(is_kept, flat_ids * CAP + rank_of, experts * CAP)
-        slots = lax.iota(jnp.int32, experts * CAP)
-        hit = slot_of[None, :] == slots[:, None]
-        dispatch = jnp.any(hit.reshape(experts * CAP, tok_rows, top_k), axis=2)
-
-    with jax.named_scope("dispatch"):
-        outgoing = jnp.dot(
-            dispatch.astype(tokens.dtype), tokens, preferred_element_type=jnp.float32
-        ).astype(tokens.dtype)
-        arrived = all_to_all_slabs(outgoing.reshape(experts, CAP, feat_width), n_dp)
-
     with jax.named_scope("expert_ffn"):
-        results = expert_ffn(arrived.reshape(-1, feat_width), *own)
+        gate_val = jnp.einsum("esd,dh->esh", arrived, own[0], preferred_element_type=jnp.float32)
+        up_val = jnp.einsum("esd,dh->esh", arrived, own[1], preferred_element_type=jnp.float32)
+        hidden = (jax.nn.silu(gate_val) * up_val).astype(jnp.bfloat16)
+        results = jnp.einsum(
+            "esh,hd->esd", hidden, own[2], preferred_element_type=jnp.float32
+        ).astype(jnp.bfloat16)
 
     with jax.named_scope("return"):
-        come_back = all_to_all_slabs(results.reshape(experts, CAP, feat_width), n_dp)
-        returned = come_back.reshape(experts * CAP, feat_width)
+        returned = lax.all_to_all(results, ("expert", "dp"), 0, 0, tiled=True)
 
     with jax.named_scope("combine"):
         gate_flat = route_gates.reshape(-1)
         cold_weight = jnp.where(is_kept, gate_flat, jnp.zeros_like(gate_flat))
-        weight_of_slot = jnp.where(hit, cold_weight[None, :], 0.0)
-        combine = jnp.sum(weight_of_slot.reshape(experts * CAP, tok_rows, top_k), axis=2).T
-        cold_sum = jnp.dot(
+        weight_of_slot = jnp.where(hit, cold_weight[None, None, :], 0.0)
+        combine = jnp.sum(weight_of_slot.reshape(experts, CAP, tok_rows, top_k), axis=3)
+        cold_sum = jnp.einsum(
+            "esp,esd->pd",
             combine,
             returned.astype(jnp.float32),
             precision=lax.Precision.HIGHEST,

time: 664 us -> 462 us (0.70)
  Pallas kernels: 446 us -> 0 us
  waiting for transfers between devices: 95.3 us -> 310 us
  local copies, waits for them, and re-layouts: 42.6 us -> 15 us
  starting transfers between devices: 0.01 us -> 24.9 us
  matrix products: 46.7 us -> 69 us
    pallas_call x2 -> x0, Pallas kernels: 446 us -> none  [all_to_all_slabs(): pl.pallas_call(functools.partial(a2a_kernel, n_dp), out_shape=jax.ShapeDt...]
    psum x1, waiting for transfers between devices: 95.3 us -> 218 us  [on_device(): lax.psum(jnp.where(is_root, w, jnp.zeros_like(w)), ('expert', 'dp'))]
    all_to_all x0 -> x2, waiting for transfers between devices: none -> 92.3 us  [the longest x1 92.3 us: on_device(): arrived = lax.all_to_all(outgoing, ('expert', 'dp'), 0, 0, tiled=True)]
    reshape x4 -> x0, local copies, waits for them, and re-layouts: 41.1 us -> none  [the longest x1 10.5 us: on_device(): results = expert_ffn(arrived.reshape(-1, feat_width), *own)]
    dot_general x3 -> x5, matrix products: 19.5 us -> 58 us  [the longest x1 18.4 us: on_device(): jnp.einsum('esd,dh->esh', arrived, own[0], preferred_element_type=jnp.flo...]
    all_to_all x0 -> x2, starting transfers between devices: none -> 24.4 us  [the longest x1 12.4 us: on_device(): returned = lax.all_to_all(results, ('expert', 'dp'), 0, 0, tiled=True)]
    convert_element_type x0 -> x2, local copies, waits for them, and re-layouts: none -> 13.4 us  [the longest x1 6.72 us: on_device(): outgoing = jnp.einsum('esp,pd->esd', dispatch.astype(tokens.dtype), token...]
    dot_general x2 -> x1, matrix products: 13.1 us -> 3.91 us  [expert_ffn(): gate_val = jnp.dot(in_rows, gate_w, preferred_element_type=jnp.float32)]
  transfers between devices with their start and end apart: 1 -> 3, of which waited for: 1 -> 2; matrix products, arithmetic and copies ran while one was open for 11% -> 17% of each run, Pallas kernels for 67% -> 0%
where the time goes in v2:
time: 462 us; the launch traced here: 456 us
  waiting for transfers between devices  310 us (67%)
  matrix products  69 us (15%)
  starting transfers between devices  24.9 us (5%)
  other arithmetic  22.3 us (5%)
  local copies, waits for them, and re-layouts  15 us (3%)
  between operations  14.5 us (3%)
    psum x1, waiting for transfers between devices, on_device(): lax.psum(jnp.where(is_root, w, jnp.zeros_like(w)), ('expert', 'dp'))  218 us
    all_to_all x1, waiting for transfers between devices, on_device(): arrived = lax.all_to_all(outgoing, ('expert', 'dp'), 0, 0, tiled=True)  92.3 us
    dot_general x1, matrix products, on_device(): jnp.einsum('esd,dh->esh', arrived, own[0], preferred_element_type=jnp.flo...  18.4 us
    dot_general x1, matrix products, on_device(): jnp.einsum('esd,dh->esh', arrived, own[1], preferred_element_type=jnp.flo...  18.1 us
    select_n x3, other arithmetic, on_device(): jnp.where(is_root, w, jnp.zeros_like(w))  15 us
    dot_general x1, matrix products, on_device(): jnp.einsum('esp,esd->pd', combine, returned.astype(jnp.float32), precisio...  14.4 us
    all_to_all x1, starting transfers between devices, on_device(): returned = lax.all_to_all(results, ('expert', 'dp'), 0, 0, tiled=True)  12.4 us
    all_to_all x1, starting transfers between devices, on_device(): arrived = lax.all_to_all(outgoing, ('expert', 'dp'), 0, 0, tiled=True)  12 us
  transfers between devices with their start and end apart: 3, of which 2 were waited for; matrix products, arithmetic and copies ran while one was open for 17% of the time, Pallas kernels for 0%

profile of v2, /device:TPU:1, one launch (start us, length us, event | category | flops | bytes accessed | tf_op | source)
XLA Modules:
  0.0 455.9 jit_solution(11663155562628726604)
XLA Ops:
  6.5 0.9 copy.55
  7.7 0.2 fusion.28
  8.1 0.3 fusion.30
  8.6 0.2 iota_compare_fusion.3
  9.4 0.7 broadcast_select_fusion
  10.3 2.9 fusion.20
  13.1 1.8 convolution_convert_fusion
  15.0 6.7 %copy.63 = bf16[128,6,4096]{2,1,0:T(8,128)(2,1)} copy(bf16[128,6,4096]{2,0,1:T(8,128)(2,1)S(1)} %convolution_convert_fusion) | data formatting | bytes 12582912 | tf_op jit(solution)/shard_map/dispatch/convert_element_type | solution.py:103
  21.7 12.0 %all-to-all-start = ((bf16[128,6,4096]{2,1,0:T(8,128)(2,1)}), bf16[128,6,4096]{2,1,0:T(8,128)(2,1)}, u32[]{:S(2)}, u32[]{:S(2)}) async-start(bf16[128,6,4096]{2,1,0:T(8,128)(2,1)} %copy.63), calls=%async_computation | async-start | bytes 16777216 | tf_op jit(solution)/shard_map/dispatch/all_to_all | solution.py:104
  33.7 0.5 all-reduce.3.cloned.1.call-start
  34.2 5.9 %bitcast_select_fusion = bf16[768,4096]{1,0:T(8,128)(2,1)} fusion(bf16[1,768,4096]{2,1,0:T(8,128)(2,1)} %param.10, pred[]{:T(512)S(6)} %eq.86), kind=kLoop, calls=%fused_computation.3 | loop fusion | flops 3145728 | bytes 12582913 | tf_op jit(solution)/shard_map/hot_weight_broadcast/jit(_where)/select_n | solution.py:109
  40.1 6.1 %bitcast_select_fusion.1 = bf16[4096,768]{1,0:T(8,128)(2,1)} fusion(bf16[1,4096,768]{2,1,0:T(8,128)(2,1)} %param.9, pred[]{:T(512)S(6)} %eq.86), kind=kLoop, calls=%fused_computation.6 | loop fusion | flops 3145728 | bytes 12582913 | tf_op jit(solution)/shard_map/hot_weight_broadcast/jit(_where)/select_n | solution.py:109
  46.2 3.1 bitcast_select_fusion.2
  49.3 92.3 %all-to-all-done = bf16[128,6,4096]{2,1,0:T(8,128)(2,1)} async-done(((bf16[128,6,4096]{2,1,0:T(8,128)(2,1)}), bf16[128,6,4096]{2,1,0:T(8,128)(2,1)}, u32[]{:S(2)}, u32[]{:S(2)}) %all-to-all-start) | async-done | bytes 6291488 | tf_op jit(solution)/shard_map/dispatch/all_to_all | solution.py:104
  141.6 18.1 %fusion.1 = f32[128,6,768]{2,0,1:T(8,128)S(1)} fusion(bf16[1,4096,768]{2,1,0:T(8,128)(2,1)} %param.9, bf16[128,6,4096]{2,1,0:T(8,128)(2,1)} %all-to-all-done), kind=kOutput, calls=%fused_computation.4 | convolution fusion | flops 4831838208 | bytes 14942208 | tf_op jit(solution)/shard_map/expert_ffn/esd,dh->esh/dot_general | solution.py:114
  159.6 18.4 %multiply_convert_fusion = bf16[128,6,768]{2,0,1:T(8,128)(2,1)S(1)} fusion(f32[128,6,768]{2,0,1:T(8,128)S(1)} %fusion.1, bf16[1,4096,768]{2,1,0:T(8,128)(2,1)} %param.8, bf16[128,6,4096]{2,1,0:T(8,128)(2,1)} %all-to-all-done), kind=kOutput, calls=%fused_computation.20 | convolution fusion | flops 4835377152 | bytes 16121856 | tf_op jit(solution)/shard_map/expert_ffn/esd,dh->esh/dot_general | solution.py:113
  178.1 5.2 %convolution_convert_fusion.1 = bf16[128,6,4096]{2,0,1:T(8,128)(2,1)S(1)} fusion(bf16[128,6,768]{2,0,1:T(8,128)(2,1)S(1)} %multiply_convert_fusion, bf16[1,768,4096]{2,1,0:T(8,128)(2,1)S(1)} %bitcast.59), kind=kOutput, calls=%fused_computation.1 | convolution fusion | flops 4834983936 | bytes 13762560 | tf_op jit(solution)/shard_map/expert_ffn/esh,hd->esd/dot_general | solution.py:116
  183.4 6.7 %copy.66 = bf16[128,6,4096]{2,1,0:T(8,128)(2,1)} copy(bf16[128,6,4096]{2,0,1:T(8,128)(2,1)S(1)} %convolution_convert_fusion.1) | data formatting | bytes 12582912 | tf_op jit(solution)/shard_map/expert_ffn/convert_element_type | solution.py:118
  190.1 12.4 %all-to-all-start.1 = ((bf16[128,6,4096]{2,1,0:T(8,128)(2,1)}), bf16[128,6,4096]{2,1,0:T(8,128)(2,1)}, u32[]{:S(2)}, u32[]{:S(2)}) async-start(bf16[128,6,4096]{2,1,0:T(8,128)(2,1)} %copy.66), calls=%async_computation.1 | async-start | bytes 16777216 | tf_op jit(solution)/shard_map/return/all_to_all | solution.py:121
  202.6 2.9 select_reduce_fusion
  205.5 217.9 %all-reduce.3.cloned.1.call-done = (bf16[768,4096]{1,0:T(8,128)(2,1)}, bf16[4096,768]{1,0:T(8,128)(2,1)}, bf16[4096,768]{1,0:T(8,128)(2,1)}) async-done(((bf16[768,4096]{1,0:T(8,128)(2,1)}, bf16[4096,768]{1,0:T(8,128)(2,1)}, bf16[4096,768]{1,0:T(8,128)(2,1)}), (bf16[768,4096]{1,0:T(8,128)(2,1)}, bf16[4096,768]{1,0:T(8,128)(2,1)}, bf16[4096,768]{1,0:T(8,128)(2,1)})) %all-reduce.3.cloned.1.call-update) | async-done | bytes 18874384 | tf_op jit(solution)/shard_map/hot_weight_broadcast/psum | solution.py:109
  423.4 3.9 convolution_bitcast_fusion.1
  427.3 7.1 %fusion.17 = f32[96,4096]{1,0:T(8,128)S(1)} fusion(bf16[768,4096]{1,0:T(8,128)(2,1)} %get-tuple-element.5, bf16[96,4096]{1,0:T(8,128)(2,1)S(1)} %copy-done, bf16[4096,768]{1,0:T(8,128)(2,1)} %get-tuple-element.6, f32[96]{0:T(128)S(1)} %get-tuple-element.10, f32[96,768]{1,0:T(8,128)S(1)} %convolution_bitcast_fusion.1), kind=kOutput, calls=%fused_computation.17 | convolution fusion | flops 1209581568 | bytes 15237504 | tf_op jit(solution)/shard_map/hot_expert/dot_general | solution.py:75
  434.5 14.4 %fusion.13 = bf16[96,4096]{1,0:T(8,128)(2,1)} fusion(f32[96,4096]{1,0:T(8,128)S(1)} %fusion.17, f32[128,6,96]{0,2,1:T(8,128)S(1)} %select_reduce_fusion, bf16[128,6,4096]{2,1,0:T(8,128)(2,1)} %all-to-all-done.1), kind=kOutput, calls=%fused_computation.14 | convolution fusion | flops 3624665088 | bytes 8945664 | tf_op jit(solution)/shard_map/combine/esp,esd->pd/dot_general | solution.py:128
  (26 shorter events, 0.9 us)
Async XLA Ops:
  6.5 6.6 %copy-start = (bf16[96,4096]{1,0:T(8,128)(2,1)S(1)}, bf16[96,4096]{1,0:T(8,128)(2,1)}, u32[]{:S(2)}) copy-start(bf16[96,4096]{1,0:T(8,128)(2,1)} %param.7) | copy-start | bytes 2359300
  21.7 119.8 %all-to-all-start = ((bf16[128,6,4096]{2,1,0:T(8,128)(2,1)}), bf16[128,6,4096]{2,1,0:T(8,128)(2,1)}, u32[]{:S(2)}, u32[]{:S(2)}) async-start(bf16[128,6,4096]{2,1,0:T(8,128)(2,1)} %copy.63), calls=%async_computation | async-start | bytes 16777216 | tf_op jit(solution)/shard_map/dispatch/all_to_all | solution.py:104
  33.7 389.7 %all-reduce.3.cloned.1.call-start = ((), (), s32[]{:S(2)}) async-start(), calls=%async_computation.2 | async-start | bytes 37748736 | tf_op jit(solution)/shard_map/hot_weight_broadcast/psum | solution.py:109
  34.2 12.0 %slice-start = ((s8[6291456]{0:T(1024)(128)(4,1)}), s8[4194304]{0:T(1024)(128)(4,1)S(1)}, s32[]{:S(2)}) async-start(s8[6291456]{0:T(1024)(128)(4,1)} %bitcast.56), calls=%async_computation.3 | async-start | bytes 8388608
  40.1 6.1 %slice-start.1 = ((s8[6291456]{0:T(1024)(128)(4,1)}), s8[2097152]{0:T(1024)(128)(4,1)S(1)}, s32[]{:S(2)}) async-start(s8[6291456]{0:T(1024)(128)(4,1)} %bitcast.56), calls=%async_computation.4 | async-start | bytes 4194304
  141.6 36.5 %slice-start.2 = ((s8[6291456]{0:T(1024)(128)(4,1)}), s8[4194304]{0:T(1024)(128)(4,1)S(1)}, s32[]{:S(2)}) async-start(s8[6291456]{0:T(1024)(128)(4,1)} %bitcast.58), calls=%async_computation.5 | async-start | bytes 8388608
  159.6 18.5 %slice-start.3 = ((s8[6291456]{0:T(1024)(128)(4,1)}), s8[2097152]{0:T(1024)(128)(4,1)S(1)}, s32[]{:S(2)}) async-start(s8[6291456]{0:T(1024)(128)(4,1)} %bitcast.58), calls=%async_computation.6 | async-start | bytes 4194304
  190.1 244.4 %all-to-all-start.1 = ((bf16[128,6,4096]{2,1,0:T(8,128)(2,1)}), bf16[128,6,4096]{2,1,0:T(8,128)(2,1)}, u32[]{:S(2)}, u32[]{:S(2)}) async-start(bf16[128,6,4096]{2,1,0:T(8,128)(2,1)} %copy.66), calls=%async_computation.1 | async-start | bytes 16777216 | tf_op jit(solution)/shard_map/return/all_to_all | solution.py:121
Sparse Core Ops, SparseCore 0:
  49.4 373.9 all-reduce.2

commit v3 on v2

--- a/solution.py
+++ b/solution.py
@@ -104,10 +104,29 @@
         arrived = lax.all_to_all(outgoing, ("expert", "dp"), 0, 0, tiled=True)
 
     with jax.named_scope("hot_weight_broadcast"):
-        is_root = me == hot_id
-        hot_w = tuple(
-            lax.psum(jnp.where(is_root, w, jnp.zeros_like(w)), ("expert", "dp")) for w in own
+        core = lax.axis_index("dp")
+        partner = me + 1 - 2 * core
+        half = own[0].shape[1] // 2
+        split_g = own[0].reshape(own[0].shape[0], 2, half)
+        split_u = own[1].reshape(own[1].shape[0], 2, half)
+        split_d = own[2].reshape(2, half, own[2].shape[1])
+        mine = (
+            jnp.where(core == 0, split_g[:, 0], split_g[:, 1]),
+            jnp.where(core == 0, split_u[:, 0], split_u[:, 1]),
+            jnp.where(core == 0, split_d[0], split_d[1]),
         )
+        theirs = (
+            jnp.where(core == 0, split_g[:, 1], split_g[:, 0]),
+            jnp.where(core == 0, split_u[:, 1], split_u[:, 0]),
+            jnp.where(core == 0, split_d[1], split_d[0]),
+        )
+        swap = [(0, 1), (1, 0)]
+        from_partner = tuple(lax.ppermute(w, "dp", swap) for w in theirs)
+        held = tuple(
+            jnp.where(me == hot_id, a, jnp.where(partner == hot_id, b, jnp.zeros_like(a)))
+            for a, b in zip(mine, from_partner)
+        )
+        hot_w = tuple(lax.psum(w, "expert") for w in held)
 
     with jax.named_scope("expert_ffn"):
         gate_val = jnp.einsum("esd,dh->esh", arrived, own[0], preferred_element_type=jnp.float32)
@@ -134,7 +153,14 @@
         )
 
     with jax.named_scope("hot_expert"):
-        hot_out = expert_ffn(tokens, *hot_w)
+        pair = jnp.concatenate([tokens, lax.ppermute(tokens, "dp", swap)], axis=0)
+        gate_val = jnp.dot(pair, hot_w[0], preferred_element_type=jnp.float32)
+        up_val = jnp.dot(pair, hot_w[1], preferred_element_type=jnp.float32)
+        hidden = (jax.nn.silu(gate_val) * up_val).astype(jnp.bfloat16)
+        partial = jnp.dot(hidden, hot_w[2], preferred_element_type=jnp.float32)
+        hot_out = (
+            partial[:tok_rows] + lax.ppermute(partial[tok_rows:], "dp", swap)
+        ).astype(jnp.bfloat16)
         hot_weight = jnp.sum(
             jnp.where(route_ids == hot_id, route_gates, jnp.zeros_like(route_gates)), axis=1
         )

time: 462 us -> 450 us (0.974)
  waiting for transfers between devices: 310 us -> 264 us
  local copies, waits for them, and re-layouts: 15 us -> 33.7 us
  other arithmetic: 22.3 us -> 33.2 us
    psum x1, waiting for transfers between devices: 218 us -> 161 us  [on_device(): hot_w = tuple((lax.psum(w, 'expert') for w in held))]
    unnamed x11 -> x22, local copies, waits for them, and re-layouts: 0.88 us -> 17.6 us
    select_n x3 -> x6, other arithmetic: 15 us -> 25.1 us  [the longest x3 10.6 us: on_device(): jnp.where(me == hot_id, a, jnp.where(partner == hot_id, b, jnp.zeros_like...]
    all_to_all x1, waiting for transfers between devices: 92.3 us -> 102 us  [on_device(): arrived = lax.all_to_all(outgoing, ('expert', 'dp'), 0, 0, tiled=True)]
    ppermute x0 -> x5, starting transfers between devices: none -> 5.52 us  [the longest x1 2.37 us: on_device(): lax.ppermute(partial[tok_rows:], 'dp', swap)]
  transfers between devices with their start and end apart: 3 -> 8, of which waited for: 2 -> 3; matrix products, arithmetic and copies ran while one was open for 17% -> 24% of each run, Pallas kernels for 0% -> 0%
where the time goes in v3:
time: 450 us; the launch traced here: 442 us
  waiting for transfers between devices  264 us (59%)
  matrix products  68 us (15%)
  local copies, waits for them, and re-layouts  33.7 us (7%)
  other arithmetic  33.2 us (7%)
  starting transfers between devices  28.2 us (6%)
  between operations  14.6 us (3%)
    psum x1, waiting for transfers between devices, on_device(): hot_w = tuple((lax.psum(w, 'expert') for w in held))  161 us
    all_to_all x1, waiting for transfers between devices, on_device(): arrived = lax.all_to_all(outgoing, ('expert', 'dp'), 0, 0, tiled=True)  102 us
    dot_general x1, matrix products, on_device(): jnp.einsum('esd,dh->esh', arrived, own[0], preferred_element_type=jnp.flo...  18.9 us
    dot_general x1, matrix products, on_device(): jnp.einsum('esd,dh->esh', arrived, own[1], preferred_element_type=jnp.flo...  18.4 us
    unnamed x22, local copies, waits for them, and re-layouts  17.6 us
    dot_general x1, matrix products, on_device(): jnp.einsum('esp,esd->pd', combine, returned.astype(jnp.float32), precisio...  14.6 us
    all_to_all x1, starting transfers between devices, on_device(): returned = lax.all_to_all(results, ('expert', 'dp'), 0, 0, tiled=True)  11.7 us
    all_to_all x1, starting transfers between devices, on_device(): arrived = lax.all_to_all(outgoing, ('expert', 'dp'), 0, 0, tiled=True)  10.7 us
  transfers between devices with their start and end apart: 8, of which 3 were waited for; matrix products, arithmetic and copies ran while one was open for 24% of the time, Pallas kernels for 0%

profile of v3, /device:TPU:1, one launch (start us, length us, event | category | flops | bytes accessed | tf_op | source)
XLA Modules:
  0.0 441.9 jit_solution(14577127374547748899)
XLA Ops:
  6.5 8.6 %copy.98 = bf16[1,4096,768]{1,2,0:T(8,128)(2,1)} copy(bf16[1,4096,768]{2,1,0:T(8,128)(2,1)} %param.9) | data formatting | bytes 12582912 | tf_op args[2]
  15.2 4.8 %select_bitcast_fusion.1 = bf16[4096,384]{0,1:T(8,128)(2,1)} fusion(pred[]{:T(512)S(6)} %eq.102, bf16[4096,2,384]{0,2,1:T(8,128)(2,1)} %bitcast.54), kind=kLoop, calls=%fused_computation.16 | loop fusion | flops 1572864 | bytes 9437185 | tf_op jit(solution)/shard_map/hot_weight_broadcast/jit(_where)/select_n | solution.py:120
  21.4 8.7 %copy.97 = bf16[1,4096,768]{1,2,0:T(8,128)(2,1)} copy(bf16[1,4096,768]{2,1,0:T(8,128)(2,1)} %param.8) | data formatting | bytes 12582912 | tf_op args[1]
  30.2 4.9 %select_bitcast_fusion.2 = bf16[4096,384]{0,1:T(8,128)(2,1)} fusion(pred[]{:T(512)S(6)} %eq.102, bf16[4096,2,384]{0,2,1:T(8,128)(2,1)} %bitcast.56), kind=kLoop, calls=%fused_computation.17 | loop fusion | flops 1572864 | bytes 9437185 | tf_op jit(solution)/shard_map/hot_weight_broadcast/jit(_where)/select_n | solution.py:119
  35.0 4.9 %select_bitcast_fusion = bf16[384,4096]{1,0:T(8,128)(2,1)} fusion(pred[]{:T(512)S(6)} %eq.102, bf16[1,768,4096]{2,1,0:T(8,128)(2,1)} %param.10), kind=kLoop, calls=%fused_computation.15 | loop fusion | flops 1572864 | bytes 9437185 | tf_op jit(solution)/shard_map/hot_weight_broadcast/jit(_where)/select_n | solution.py:121
  43.1 2.9 fusion.12
  47.9 6.7 %copy.92 = bf16[128,6,4096]{2,1,0:T(8,128)(2,1)} copy(bf16[128,6,4096]{2,0,1:T(8,128)(2,1)S(1)} %convolution_convert_fusion) | data formatting | bytes 12582912 | tf_op jit(solution)/shard_map/dispatch/convert_element_type | solution.py:103
  54.6 10.7 %all-to-all-start = ((bf16[128,6,4096]{2,1,0:T(8,128)(2,1)}), bf16[128,6,4096]{2,1,0:T(8,128)(2,1)}, u32[]{:S(2)}, u32[]{:S(2)}) async-start(bf16[128,6,4096]{2,1,0:T(8,128)(2,1)} %copy.92), calls=%async_computation | async-start | bytes 16777216 | tf_op jit(solution)/shard_map/dispatch/all_to_all | solution.py:104
  65.7 4.3 bitcast_select_fusion.1
  70.0 4.3 bitcast_select_fusion.2
  74.3 1.9 bitcast_select_fusion
  76.3 101.5 %all-to-all-done = bf16[128,6,4096]{2,1,0:T(8,128)(2,1)} async-done(((bf16[128,6,4096]{2,1,0:T(8,128)(2,1)}), bf16[128,6,4096]{2,1,0:T(8,128)(2,1)}, u32[]{:S(2)}, u32[]{:S(2)}) %all-to-all-start) | async-done | bytes 6291488 | tf_op jit(solution)/shard_map/dispatch/all_to_all | solution.py:104
  177.8 18.4 %fusion.1 = f32[128,6,768]{2,0,1:T(8,128)S(1)} fusion(bf16[1,4096,768]{2,1,0:T(8,128)(2,1)} %param.9, bf16[128,6,4096]{2,1,0:T(8,128)(2,1)} %all-to-all-done), kind=kOutput, calls=%fused_computation.3 | convolution fusion | flops 4831838208 | bytes 14942208 | tf_op jit(solution)/shard_map/expert_ffn/esd,dh->esh/dot_general | solution.py:133
  196.2 18.9 %multiply_convert_fusion = bf16[128,6,768]{2,0,1:T(8,128)(2,1)S(1)} fusion(f32[128,6,768]{2,0,1:T(8,128)S(1)} %fusion.1, bf16[1,4096,768]{2,1,0:T(8,128)(2,1)} %param.8, bf16[128,6,4096]{2,1,0:T(8,128)(2,1)} %all-to-all-done), kind=kOutput, calls=%fused_computation.18 | convolution fusion | flops 4835377152 | bytes 16121856 | tf_op jit(solution)/shard_map/expert_ffn/esd,dh->esh/dot_general | solution.py:132
  215.2 5.5 %convolution_convert_fusion.1 = bf16[128,6,4096]{2,0,1:T(8,128)(2,1)S(1)} fusion(bf16[128,6,768]{2,0,1:T(8,128)(2,1)S(1)} %multiply_convert_fusion, bf16[1,768,4096]{2,1,0:T(8,128)(2,1)S(1)} %bitcast.61), kind=kOutput, calls=%fused_computation.1 | convolution fusion | flops 4834983936 | bytes 13762560 | tf_op jit(solution)/shard_map/expert_ffn/esh,hd->esd/dot_general | solution.py:135
  220.6 6.7 %copy.95 = bf16[128,6,4096]{2,1,0:T(8,128)(2,1)} copy(bf16[128,6,4096]{2,0,1:T(8,128)(2,1)S(1)} %convolution_convert_fusion.1) | data formatting | bytes 12582912 | tf_op jit(solution)/shard_map/expert_ffn/convert_element_type | solution.py:137
  227.4 11.7 %all-to-all-start.1 = ((bf16[128,6,4096]{2,1,0:T(8,128)(2,1)}), bf16[128,6,4096]{2,1,0:T(8,128)(2,1)}, u32[]{:S(2)}, u32[]{:S(2)}) async-start(bf16[128,6,4096]{2,1,0:T(8,128)(2,1)} %copy.95), calls=%async_computation.1 | async-start | bytes 16777216 | tf_op jit(solution)/shard_map/return/all_to_all | solution.py:140
  240.4 1.9 collective-permute-done
  242.3 160.9 %all-reduce.3.cloned.1.call-done = (bf16[384,4096]{1,0:T(8,128)(2,1)}, bf16[4096,384]{0,1:T(8,128)(2,1)}, bf16[4096,384]{0,1:T(8,128)(2,1)}) async-done(((bf16[384,4096]{1,0:T(8,128)(2,1)}, bf16[4096,384]{0,1:T(8,128)(2,1)}, bf16[4096,384]{0,1:T(8,128)(2,1)}), (bf16[384,4096]{1,0:T(8,128)(2,1)}, bf16[4096,384]{0,1:T(8,128)(2,1)}, bf16[4096,384]{0,1:T(8,128)(2,1)})) %all-reduce.3.cloned.1.call-update) | async-done | bytes 9437200 | tf_op jit(solution)/shard_map/hot_weight_broadcast/psum | solution.py:129
  403.2 3.1 fusion.28
  406.2 5.7 %fusion.23 = f32[192,4096]{1,0:T(8,128)S(1)} fusion(bf16[384,4096]{1,0:T(8,128)(2,1)} %get-tuple-element.5, f32[192,384]{1,0:T(8,128)S(1)} %fusion.28, bf16[192,4096]{1,0:T(8,128)(2,1)} %copy-done, bf16[4096,384]{0,1:T(8,128)(2,1)} %get-tuple-element.6), kind=kOutput, calls=%fused_computation.37 | convolution fusion | flops 1208401920 | bytes 11304960 | tf_op jit(solution)/shard_map/hot_expert/dot_general | solution.py:160
  413.2 2.4 collective-permute-start.4
  416.3 3.9 select_reduce_fusion
  420.2 14.6 %add_convert_fusion = bf16[96,4096]{1,0:T(8,128)(2,1)} fusion(f32[96,4096]{1,0:T(8,128)} %collective-permute-done.4, f32[192,4096]{1,0:T(8,128)S(1)} %fusion.23, f32[96]{0:T(128)} %get-tuple-element.10, f32[128,6,96]{0,2,1:T(8,128)S(1)} %select_reduce_fusion, bf16[128,6,4096]{2,1,0:T(8,128)(2,1)} %all-to-all-done.1), kind=kOutput, calls=%fused_computation.24 | convolution fusion | flops 3626237952 | bytes 10518912 | tf_op jit(solution)/shard_map/combine/esp,esd->pd/dot_general | solution.py:147
  (52 shorter events, 9.5 us)
Async XLA Ops:
  20.0 45.7 %collective-permute-start.2 = (bf16[4096,384]{0,1:T(8,128)(2,1)}, bf16[4096,384]{0,1:T(8,128)(2,1)}, u32[]{:S(2)}, u32[]{:S(2)}) collective-permute-start(bf16[4096,384]{0,1:T(8,128)(2,1)} %select_bitcast_fusion.1), channel_id=1, source_target_pairs={{0,1},{1,0},{2,3},{3,2},{4,5},{5,4},{6,7},{7,6},{8,9},{9,8},{10,11... | collective-permute-start | bytes 9437192 | tf_op jit(solution)/shard_map/hot_weight_broadcast/ppermute | solution.py:124
  35.0 5.4 %copy-start.3 = (s32[96,8]{0,1:T(8,128)S(1)}, s32[96,8]{0,1:T(8,128)}, u32[]{:S(2)}) copy-start(s32[96,8]{0,1:T(8,128)} %param.11) | copy-start | bytes 9220
  35.0 35.0 %collective-permute-start.1 = (bf16[4096,384]{0,1:T(8,128)(2,1)}, bf16[4096,384]{0,1:T(8,128)(2,1)}, u32[]{:S(2)}, u32[]{:S(2)}) collective-permute-start(bf16[4096,384]{0,1:T(8,128)(2,1)} %select_bitcast_fusion.2), channel_id=1, source_target_pairs={{0,1},{1,0},{2,3},{3,2},{4,5},{5,4},{6,7},{7,6},{8,9},{9,8},{10,11... | collective-permute-start | bytes 9437192 | tf_op jit(solution)/shard_map/hot_weight_broadcast/ppermute | solution.py:124
  39.9 2.4 copy-start.4
  39.9 6.1 %copy-start.1 = (bf16[96,4096]{1,0:T(8,128)(2,1)S(1)}, bf16[96,4096]{1,0:T(8,128)(2,1)}, u32[]{:S(2)}) copy-start(bf16[96,4096]{1,0:T(8,128)(2,1)} %param.7) | copy-start | bytes 2359300
  39.9 34.4 %collective-permute-start.3 = (bf16[384,4096]{1,0:T(8,128)(2,1)}, bf16[384,4096]{1,0:T(8,128)(2,1)}, u32[]{:S(2)}, u32[]{:S(2)}) collective-permute-start(bf16[384,4096]{1,0:T(8,128)(2,1)} %select_bitcast_fusion), channel_id=1, source_target_pairs={{0,1},{1,0},{2,3},{3,2},{4,5},{5,4},{6,7},{7,6},{8,9},{9,8},{10,11... | collective-permute-start | bytes 9437192 | tf_op jit(solution)/shard_map/hot_weight_broadcast/ppermute | solution.py:124
  43.0 4.9 %copy-start.2 = (pred[6,96,8]{2,1,0:T(8,128)(4,1)}, pred[6,96,8]{2,1,0:T(8,128)(4,1)S(1)}, u32[]{:S(2)}) copy-start(pred[6,96,8]{2,1,0:T(8,128)(4,1)S(1)} %iota_compare_fusion.4) | copy-start | bytes 13828
  54.6 19.7 %slice-start = ((s8[6291456]{0:T(1024)(128)(4,1)}), s8[2097152]{0:T(1024)(128)(4,1)S(1)}, s32[]{:S(2)}) async-start(s8[6291456]{0:T(1024)(128)(4,1)} %bitcast.58), calls=%async_computation.3 | async-start | bytes 4194304
  54.6 123.2 %all-to-all-start = ((bf16[128,6,4096]{2,1,0:T(8,128)(2,1)}), bf16[128,6,4096]{2,1,0:T(8,128)(2,1)}, u32[]{:S(2)}, u32[]{:S(2)}) async-start(bf16[128,6,4096]{2,1,0:T(8,128)(2,1)} %copy.92), calls=%async_computation | async-start | bytes 16777216 | tf_op jit(solution)/shard_map/dispatch/all_to_all | solution.py:104
  65.3 337.9 %all-reduce.3.cloned.1.call-start = ((), (), s32[]{:S(2)}) async-start(), calls=%async_computation.2 | async-start | bytes 18874368 | tf_op jit(solution)/shard_map/hot_weight_broadcast/psum | solution.py:129
  65.6 8.7 %slice-start.1 = ((s8[6291456]{0:T(1024)(128)(4,1)}), s8[4194304]{0:T(1024)(128)(4,1)S(1)}, s32[]{:S(2)}) async-start(s8[6291456]{0:T(1024)(128)(4,1)} %bitcast.58), calls=%async_computation.4 | async-start | bytes 8388608
  177.8 37.3 %slice-start.2 = ((s8[6291456]{0:T(1024)(128)(4,1)}), s8[4194304]{0:T(1024)(128)(4,1)S(1)}, s32[]{:S(2)}) async-start(s8[6291456]{0:T(1024)(128)(4,1)} %bitcast.60), calls=%async_computation.5 | async-start | bytes 8388608
  196.2 18.9 %slice-start.3 = ((s8[6291456]{0:T(1024)(128)(4,1)}), s8[2097152]{0:T(1024)(128)(4,1)S(1)}, s32[]{:S(2)}) async-start(s8[6291456]{0:T(1024)(128)(4,1)} %bitcast.60), calls=%async_computation.6 | async-start | bytes 4194304
  227.4 192.8 %all-to-all-start.1 = ((bf16[128,6,4096]{2,1,0:T(8,128)(2,1)}), bf16[128,6,4096]{2,1,0:T(8,128)(2,1)}, u32[]{:S(2)}, u32[]{:S(2)}) async-start(bf16[128,6,4096]{2,1,0:T(8,128)(2,1)} %copy.95), calls=%async_computation.1 | async-start | bytes 16777216 | tf_op jit(solution)/shard_map/return/all_to_all | solution.py:140
  239.1 3.1 collective-permute-start
  242.3 164.0 %copy-start = (bf16[192,4096]{1,0:T(8,128)(2,1)}, bf16[192,4096]{1,0:T(8,128)(2,1)S(1)}, u32[]{:S(2)}) copy-start(bf16[192,4096]{1,0:T(8,128)(2,1)S(1)} %constant_dynamic-update-slice_fusion) | copy-start | bytes 4718596
  413.2 7.0 %collective-permute-start.4 = (f32[96,4096]{1,0:T(8,128)}, f32[96,4096]{1,0:T(8,128)}, u32[]{:S(2)}, u32[]{:S(2)}) collective-permute-start(f32[96,4096]{1,0:T(8,128)} %slice.54), channel_id=1, source_target_pairs={{0,1},{1,0},{2,3},{3,2},{4,5},{5,4},{6,7},{7,6},{8,9},{9,8},{10,11... | collective-permute-start | bytes 4718600 | tf_op jit(solution)/shard_map/hot_expert/ppermute | solution.py:162
Sparse Core Ops, SparseCore 0:
  76.4 326.7 all-reduce.2

commit v4 on v3

--- a/solution.py
+++ b/solution.py
@@ -84,25 +84,6 @@
     me = lax.axis_index("expert") * n_dp + lax.axis_index("dp")
     own = (w_gate[0], w_up[0], w_down[0])
 
-    with jax.named_scope("routing"):
-        flat_ids = route_ids.reshape(-1)
-        labels = lax.iota(jnp.int32, experts)
-        onehot = (flat_ids[:, None] == labels[None, :]).astype(jnp.int32)
-        rank_of = jnp.sum(onehot * (jnp.cumsum(onehot, axis=0) - 1), axis=1)
-        is_kept = (flat_ids != hot_id) & (rank_of < CAP)
-        slot_rank = lax.iota(jnp.int32, CAP)
-        hit = (flat_ids[None, None, :] == labels[:, None, None]) & (
-            rank_of[None, None, :] == slot_rank[None, :, None]
-        ) & is_kept[None, None, :]
-        dispatch = jnp.any(hit.reshape(experts, CAP, tok_rows, top_k), axis=3)
-
-    with jax.named_scope("dispatch"):
-        outgoing = jnp.einsum(
-            "esp,pd->esd", dispatch.astype(tokens.dtype), tokens,
-            preferred_element_type=jnp.float32,
-        ).astype(tokens.dtype)
-        arrived = lax.all_to_all(outgoing, ("expert", "dp"), 0, 0, tiled=True)
-
     with jax.named_scope("hot_weight_broadcast"):
         core = lax.axis_index("dp")
         partner = me + 1 - 2 * core
@@ -126,7 +107,27 @@
             jnp.where(me == hot_id, a, jnp.where(partner == hot_id, b, jnp.zeros_like(a)))
             for a, b in zip(mine, from_partner)
         )
+        held, tokens = lax.optimization_barrier((held, tokens))
         hot_w = tuple(lax.psum(w, "expert") for w in held)
+
+    with jax.named_scope("routing"):
+        flat_ids = route_ids.reshape(-1)
+        labels = lax.iota(jnp.int32, experts)
+        onehot = (flat_ids[:, None] == labels[None, :]).astype(jnp.int32)
+        rank_of = jnp.sum(onehot * (jnp.cumsum(onehot, axis=0) - 1), axis=1)
+        is_kept = (flat_ids != hot_id) & (rank_of < CAP)
+        slot_rank = lax.iota(jnp.int32, CAP)
+        hit = (flat_ids[None, None, :] == labels[:, None, None]) & (
+            rank_of[None, None, :] == slot_rank[None, :, None]
+        ) & is_kept[None, None, :]
+        dispatch = jnp.any(hit.reshape(experts, CAP, tok_rows, top_k), axis=3)
+
+    with jax.named_scope("dispatch"):
+        outgoing = jnp.einsum(
+            "esp,pd->esd", dispatch.astype(tokens.dtype), tokens,
+            preferred_element_type=jnp.float32,
+        ).astype(tokens.dtype)
+        arrived = lax.all_to_all(outgoing, ("expert", "dp"), 0, 0, tiled=True)
 
     with jax.named_scope("expert_ffn"):
         gate_val = jnp.einsum("esd,dh->esh", arrived, own[0], preferred_element_type=jnp.float32)
@@ -144,13 +145,11 @@
         cold_weight = jnp.where(is_kept, gate_flat, jnp.zeros_like(gate_flat))
         weight_of_slot = jnp.where(hit, cold_weight[None, None, :], 0.0)
         combine = jnp.sum(weight_of_slot.reshape(experts, CAP, tok_rows, top_k), axis=3)
+        combine_hi = combine.astype(jnp.bfloat16)
+        combine_lo = (combine - combine_hi.astype(jnp.float32)).astype(jnp.bfloat16)
         cold_sum = jnp.einsum(
-            "esp,esd->pd",
-            combine,
-            returned.astype(jnp.float32),
-            precision=lax.Precision.HIGHEST,
-            preferred_element_type=jnp.float32,
-        )
+            "esp,esd->pd", combine_hi, returned, preferred_element_type=jnp.float32
+        ) + jnp.einsum("esp,esd->pd", combine_lo, returned, preferred_element_type=jnp.float32)
 
     with jax.named_scope("hot_expert"):
         pair = jnp.concatenate([tokens, lax.ppermute(tokens, "dp", swap)], axis=0)

time: 450 us -> 472 us (1.049)
  waiting for transfers between devices: 264 us -> 277 us
  matrix products: 68 us -> 75.8 us
    all_to_all x1, waiting for transfers between devices: 102 us -> 113 us  [on_device(): arrived = lax.all_to_all(outgoing, ('expert', 'dp'), 0, 0, tiled=True)]
    dot_general x1 -> x2, matrix products: 14.6 us -> 22.2 us  [the longest x1 11.9 us: on_device(): jnp.einsum('esp,esd->pd', combine_hi, returned, preferred_element_type=jn...]
    unnamed x22 -> x30, local copies, waits for them, and re-layouts: 17.6 us -> 19.6 us
  transfers between devices with their start and end apart: 8 -> 8, of which waited for: 3 -> 3; matrix products, arithmetic and copies ran while one was open for 24% -> 23% of each run, Pallas kernels for 0% -> 0%
where the time goes in v4:
time: 472 us; the launch traced here: 463 us
  waiting for transfers between devices  277 us (59%)
  matrix products  75.8 us (16%)
  local copies, waits for them, and re-layouts  35.7 us (8%)
  other arithmetic  32 us (7%)
  starting transfers between devices  28.3 us (6%)
  between operations  14.8 us (3%)
    psum x1, waiting for transfers between devices, on_device(): hot_w = tuple((lax.psum(w, 'expert') for w in held))  162 us
    all_to_all x1, waiting for transfers between devices, on_device(): arrived = lax.all_to_all(outgoing, ('expert', 'dp'), 0, 0, tiled=True)  113 us
    unnamed x30, local copies, waits for them, and re-layouts  19.6 us
    dot_general x1, matrix products, on_device(): jnp.einsum('esd,dh->esh', arrived, own[0], preferred_element_type=jnp.flo...  18.3 us
    dot_general x1, matrix products, on_device(): jnp.einsum('esd,dh->esh', arrived, own[1], preferred_element_type=jnp.flo...  18 us
    dot_general x1, matrix products, on_device(): jnp.einsum('esp,esd->pd', combine_hi, returned, preferred_element_type=jn...  11.9 us
    all_to_all x1, starting transfers between devices, on_device(): returned = lax.all_to_all(results, ('expert', 'dp'), 0, 0, tiled=True)  11.7 us
    all_to_all x1, starting transfers between devices, on_device(): arrived = lax.all_to_all(outgoing, ('expert', 'dp'), 0, 0, tiled=True)  10.7 us
  transfers between devices with their start and end apart: 8, of which 3 were waited for; matrix products, arithmetic and copies ran while one was open for 23% of the time, Pallas kernels for 0%

profile of v4, /device:TPU:1, one launch (start us, length us, event | category | flops | bytes accessed | tf_op | source)
XLA Modules:
  0.0 463.3 jit_solution(13555475964506094337)
XLA Ops:
  6.5 8.5 %copy.94 = bf16[1,4096,768]{1,2,0:T(8,128)(2,1)} copy(bf16[1,4096,768]{2,1,0:T(8,128)(2,1)} %param.8) | data formatting | bytes 12582912 | tf_op args[1]
  15.1 4.8 %select_bitcast_fusion.2 = bf16[4096,384]{0,1:T(8,128)(2,1)} fusion(pred[]{:T(512)S(6)} %eq.101, bf16[4096,2,384]{0,2,1:T(8,128)(2,1)} %bitcast.59), kind=kLoop, calls=%fused_computation.19 | loop fusion | flops 1572864 | bytes 9437185 | tf_op jit(solution)/shard_map/hot_weight_broadcast/jit(_where)/select_n | solution.py:100
  21.3 8.7 %copy.95 = bf16[1,4096,768]{1,2,0:T(8,128)(2,1)} copy(bf16[1,4096,768]{2,1,0:T(8,128)(2,1)} %param.9) | data formatting | bytes 12582912 | tf_op args[2]
  30.0 4.8 %select_bitcast_fusion.1 = bf16[4096,384]{0,1:T(8,128)(2,1)} fusion(pred[]{:T(512)S(6)} %eq.101, bf16[4096,2,384]{0,2,1:T(8,128)(2,1)} %bitcast.61), kind=kLoop, calls=%fused_computation.18 | loop fusion | flops 1572864 | bytes 9437185 | tf_op jit(solution)/shard_map/hot_weight_broadcast/jit(_where)/select_n | solution.py:101
  34.8 4.8 %select_bitcast_fusion = bf16[384,4096]{1,0:T(8,128)(2,1)} fusion(pred[]{:T(512)S(6)} %eq.101, bf16[1,768,4096]{2,1,0:T(8,128)(2,1)} %param.10), kind=kLoop, calls=%fused_computation.17 | loop fusion | flops 1572864 | bytes 9437185 | tf_op jit(solution)/shard_map/hot_weight_broadcast/jit(_where)/select_n | solution.py:102
  44.8 2.9 fusion.10
  47.8 4.3 bitcast_select_fusion.2
  52.1 2.0 bitcast_select_fusion.1
  57.4 3.0 convolution_convert_fusion
  60.4 6.7 %copy.98 = bf16[128,6,4096]{2,1,0:T(8,128)(2,1)} copy(bf16[128,6,4096]{2,0,1:T(8,128)(2,1)S(1)} %convolution_convert_fusion) | data formatting | bytes 12582912 | tf_op jit(solution)/shard_map/dispatch/convert_element_type | solution.py:129
  67.2 10.7 %all-to-all-start = ((bf16[128,6,4096]{2,1,0:T(8,128)(2,1)}), bf16[128,6,4096]{2,1,0:T(8,128)(2,1)}, u32[]{:S(2)}, u32[]{:S(2)}) async-start(bf16[128,6,4096]{2,1,0:T(8,128)(2,1)} %copy.98), calls=%async_computation | async-start | bytes 16777216 | tf_op jit(solution)/shard_map/dispatch/all_to_all | solution.py:130
  78.6 112.9 %all-to-all-done = bf16[128,6,4096]{2,1,0:T(8,128)(2,1)} async-done(((bf16[128,6,4096]{2,1,0:T(8,128)(2,1)}), bf16[128,6,4096]{2,1,0:T(8,128)(2,1)}, u32[]{:S(2)}, u32[]{:S(2)}) %all-to-all-start) | async-done | bytes 6291488 | tf_op jit(solution)/shard_map/dispatch/all_to_all | solution.py:130
  191.5 18.0 %fusion.1 = f32[128,6,768]{2,0,1:T(8,128)S(1)} fusion(bf16[1,4096,768]{2,1,0:T(8,128)(2,1)} %param.9, bf16[128,6,4096]{2,1,0:T(8,128)(2,1)} %all-to-all-done), kind=kOutput, calls=%fused_computation.3 | convolution fusion | flops 4831838208 | bytes 14942208 | tf_op jit(solution)/shard_map/expert_ffn/esd,dh->esh/dot_general | solution.py:134
  209.5 18.3 %multiply_convert_fusion = bf16[128,6,768]{2,0,1:T(8,128)(2,1)S(1)} fusion(f32[128,6,768]{2,0,1:T(8,128)S(1)} %fusion.1, bf16[1,4096,768]{2,1,0:T(8,128)(2,1)} %param.8, bf16[128,6,4096]{2,1,0:T(8,128)(2,1)} %all-to-all-done), kind=kOutput, calls=%fused_computation.20 | convolution fusion | flops 4835377152 | bytes 16121856 | tf_op jit(solution)/shard_map/expert_ffn/esd,dh->esh/dot_general | solution.py:133
  227.9 5.5 %convolution_convert_fusion.1 = bf16[128,6,4096]{2,0,1:T(8,128)(2,1)S(1)} fusion(bf16[128,6,768]{2,0,1:T(8,128)(2,1)S(1)} %multiply_convert_fusion, bf16[1,768,4096]{2,1,0:T(8,128)(2,1)S(1)} %bitcast.68), kind=kOutput, calls=%fused_computation.1 | convolution fusion | flops 4834983936 | bytes 13762560 | tf_op jit(solution)/shard_map/expert_ffn/esh,hd->esd/dot_general | solution.py:136
  233.4 6.7 %copy.101 = bf16[128,6,4096]{2,1,0:T(8,128)(2,1)} copy(bf16[128,6,4096]{2,0,1:T(8,128)(2,1)S(1)} %convolution_convert_fusion.1) | data formatting | bytes 12582912 | tf_op jit(solution)/shard_map/expert_ffn/convert_element_type | solution.py:138
  240.2 11.7 %all-to-all-start.1 = ((bf16[128,6,4096]{2,1,0:T(8,128)(2,1)}), bf16[128,6,4096]{2,1,0:T(8,128)(2,1)}, u32[]{:S(2)}, u32[]{:S(2)}) async-start(bf16[128,6,4096]{2,1,0:T(8,128)(2,1)} %copy.101), calls=%async_computation.1 | async-start | bytes 16777216 | tf_op jit(solution)/shard_map/return/all_to_all | solution.py:141
  255.0 161.7 %all-reduce.3.cloned.1.call-done = (bf16[384,4096]{1,0:T(8,128)(2,1)}, bf16[4096,384]{0,1:T(8,128)(2,1)}, bf16[4096,384]{0,1:T(8,128)(2,1)}) async-done(((bf16[384,4096]{1,0:T(8,128)(2,1)}, bf16[4096,384]{0,1:T(8,128)(2,1)}, bf16[4096,384]{0,1:T(8,128)(2,1)}), (bf16[384,4096]{1,0:T(8,128)(2,1)}, bf16[4096,384]{0,1:T(8,128)(2,1)}, bf16[4096,384]{0,1:T(8,128)(2,1)})) %all-reduce.3.cloned.1.call-update) | async-done | bytes 9437200 | tf_op jit(solution)/shard_map/hot_weight_broadcast/psum | solution.py:111
  416.8 3.1 fusion.32
  419.9 5.7 %fusion.21 = f32[192,4096]{1,0:T(8,128)S(1)} fusion(bf16[384,4096]{1,0:T(8,128)(2,1)} %get-tuple-element.13, f32[192,384]{1,0:T(8,128)S(1)} %fusion.32, bf16[192,4096]{1,0:T(8,128)(2,1)} %copy-done, bf16[4096,384]{0,1:T(8,128)(2,1)} %get-tuple-element.14), kind=kOutput, calls=%fused_computation.40 | convolution fusion | flops 1208401920 | bytes 11304960 | tf_op jit(solution)/shard_map/hot_expert/dot_general | solution.py:159
  426.8 2.4 collective-permute-start.4
  429.9 3.9 select_reduce_fusion
  433.8 10.3 %convolution_bitcast_fusion = f32[96,4096]{1,0:T(8,128)S(1)} fusion(bf16[128,6,4096]{2,1,0:T(8,128)(2,1)} %all-to-all-done.1, f32[128,6,96]{0,2,1:T(8,128)S(1)} %select_reduce_fusion), kind=kOutput, calls=%fused_computation.7 | convolution fusion | flops 604274688 | bytes 8159232 | tf_op jit(solution)/shard_map/combine/esp,esd->pd/dot_general | solution.py:152
  444.2 11.9 %add_convert_fusion = bf16[96,4096]{1,0:T(8,128)(2,1)} fusion(f32[96,4096]{1,0:T(8,128)} %collective-permute-done.4, f32[192,4096]{1,0:T(8,128)S(1)} %fusion.21, f32[96]{0:T(128)S(1)} %copy-done.6, f32[96,4096]{1,0:T(8,128)S(1)} %convolution_bitcast_fusion, bf16[128,6,4096]{2,1,0:T(8,128)(2,1)} %all-to-all-done.1, f32[128,6,96]{0,2,1:T(8,128)S(1)} %select_reduce_fusion), kind=kOutput, calls=%fused_computation.26 | convolution fusion | flops 606806016 | bytes 12091776 | tf_op jit(solution)/shard_map/combine/esp,esd->pd/dot_general | solution.py:150
  (62 shorter events, 15.1 us)
Async XLA Ops:
  19.9 27.9 %collective-permute-start = (bf16[4096,384]{0,1:T(8,128)(2,1)}, bf16[4096,384]{0,1:T(8,128)(2,1)}, u32[]{:S(2)}, u32[]{:S(2)}) collective-permute-start(bf16[4096,384]{0,1:T(8,128)(2,1)} %select_bitcast_fusion.2), channel_id=1, source_target_pairs={{0,1},{1,0},{2,3},{3,2},{4,5},{5,4},{6,7},{7,6},{8,9},{9,8},{10,11... | collective-permute-start | bytes 9437192 | tf_op jit(solution)/shard_map/hot_weight_broadcast/ppermute | solution.py:105
  34.8 5.3 %copy-start.4 = (s32[96,8]{0,1:T(8,128)S(1)}, s32[96,8]{0,1:T(8,128)}, u32[]{:S(2)}) copy-start(s32[96,8]{0,1:T(8,128)} %param.11) | copy-start | bytes 9220
  34.8 17.3 %collective-permute-start.1 = (bf16[4096,384]{0,1:T(8,128)(2,1)}, bf16[4096,384]{0,1:T(8,128)(2,1)}, u32[]{:S(2)}, u32[]{:S(2)}) collective-permute-start(bf16[4096,384]{0,1:T(8,128)(2,1)} %select_bitcast_fusion.1), channel_id=1, source_target_pairs={{0,1},{1,0},{2,3},{3,2},{4,5},{5,4},{6,7},{7,6},{8,9},{9,8},{10,11... | collective-permute-start | bytes 9437192 | tf_op jit(solution)/shard_map/hot_weight_broadcast/ppermute | solution.py:105
  39.6 4.2 copy-start.5
  39.6 14.5 %collective-permute-start.2 = (bf16[384,4096]{1,0:T(8,128)(2,1)}, bf16[384,4096]{1,0:T(8,128)(2,1)S(1)}, u32[]{:S(2)}, u32[]{:S(2)}) collective-permute-start(bf16[384,4096]{1,0:T(8,128)(2,1)} %select_bitcast_fusion), channel_id=1, source_target_pairs={{0,1},{1,0},{2,3},{3,2},{4,5},{5,4},{6,7},{7,6},{8,9},{9,8},{10,11... | collective-permute-start | bytes 9437192 | tf_op jit(solution)/shard_map/hot_weight_broadcast/ppermute | solution.py:105
  41.4 0.8 copy-start.2
  44.6 7.5 %copy-start.3 = (pred[6,96,8]{2,1,0:T(8,128)(4,1)}, pred[6,96,8]{2,1,0:T(8,128)(4,1)S(1)}, u32[]{:S(2)}) copy-start(pred[6,96,8]{2,1,0:T(8,128)(4,1)S(1)} %iota_compare_fusion.4) | copy-start | bytes 13828
  44.7 7.5 %slice-start = ((s8[6291456]{0:T(1024)(128)(4,1)}), s8[4194304]{0:T(1024)(128)(4,1)S(1)}, s32[]{:S(2)}) async-start(s8[6291456]{0:T(1024)(128)(4,1)} %bitcast.62), calls=%async_computation.3 | async-start | bytes 8388608
  47.7 4.4 slice-start.1
  47.7 6.4 %slice-start.2 = ((s8[6291456]{0:T(1024)(128)(4,1)}), s8[4194304]{0:T(1024)(128)(4,1)S(1)}, s32[]{:S(2)}) async-start(s8[6291456]{0:T(1024)(128)(4,1)} %bitcast.65), calls=%async_computation.5 | async-start | bytes 8388608
  52.1 3.4 slice-start.3
  67.2 124.3 %all-to-all-start = ((bf16[128,6,4096]{2,1,0:T(8,128)(2,1)}), bf16[128,6,4096]{2,1,0:T(8,128)(2,1)}, u32[]{:S(2)}, u32[]{:S(2)}) async-start(bf16[128,6,4096]{2,1,0:T(8,128)(2,1)} %copy.98), calls=%async_computation | async-start | bytes 16777216 | tf_op jit(solution)/shard_map/dispatch/all_to_all | solution.py:130
  77.8 338.9 %all-reduce.3.cloned.1.call-start = ((), (), s32[]{:S(2)}) async-start(), calls=%async_computation.2 | async-start | bytes 18874368 | tf_op jit(solution)/shard_map/hot_weight_broadcast/psum | solution.py:111
  191.5 36.4 %slice-start.4 = ((s8[6291456]{0:T(1024)(128)(4,1)}), s8[4194304]{0:T(1024)(128)(4,1)S(1)}, s32[]{:S(2)}) async-start(s8[6291456]{0:T(1024)(128)(4,1)} %bitcast.67), calls=%async_computation.7 | async-start | bytes 8388608
  209.5 18.4 %slice-start.5 = ((s8[6291456]{0:T(1024)(128)(4,1)}), s8[2097152]{0:T(1024)(128)(4,1)S(1)}, s32[]{:S(2)}) async-start(s8[6291456]{0:T(1024)(128)(4,1)} %bitcast.67), calls=%async_computation.8 | async-start | bytes 4194304
  240.2 11.7 %copy-start.1 = (bf16[96,4096]{1,0:T(8,128)(2,1)S(1)}, bf16[96,4096]{1,0:T(8,128)(2,1)}, u32[]{:S(2)}) copy-start(bf16[96,4096]{1,0:T(8,128)(2,1)} %param.7) | copy-start | bytes 2359300
  240.2 193.6 %all-to-all-start.1 = ((bf16[128,6,4096]{2,1,0:T(8,128)(2,1)}), bf16[128,6,4096]{2,1,0:T(8,128)(2,1)}, u32[]{:S(2)}, u32[]{:S(2)}) async-start(bf16[128,6,4096]{2,1,0:T(8,128)(2,1)} %copy.101), calls=%async_computation.1 | async-start | bytes 16777216 | tf_op jit(solution)/shard_map/return/all_to_all | solution.py:141
  251.8 3.1 collective-permute-start.3
  255.0 164.8 %copy-start = (bf16[192,4096]{1,0:T(8,128)(2,1)}, bf16[192,4096]{1,0:T(8,128)(2,1)S(1)}, u32[]{:S(2)}) copy-start(bf16[192,4096]{1,0:T(8,128)(2,1)S(1)} %constant_dynamic-update-slice_fusion) | copy-start | bytes 4718596
  426.8 17.4 %collective-permute-start.4 = (f32[96,4096]{1,0:T(8,128)}, f32[96,4096]{1,0:T(8,128)}, u32[]{:S(2)}, u32[]{:S(2)}) collective-permute-start(f32[96,4096]{1,0:T(8,128)} %slice.54), channel_id=1, source_target_pairs={{0,1},{1,0},{2,3},{3,2},{4,5},{5,4},{6,7},{7,6},{8,9},{9,8},{10,11... | collective-permute-start | bytes 4718600 | tf_op jit(solution)/shard_map/hot_expert/ppermute | solution.py:161
  433.8 10.4 %copy-start.6 = (f32[96]{0:T(128)S(1)}, f32[96]{0:T(128)}, u32[]{:S(2)}) copy-start(f32[96]{0:T(128)} %get-tuple-element.18) | copy-start | bytes 1156
Sparse Core Ops, SparseCore 0:
  84.7 332.0 all-reduce.2

commit v5 on v3

--- a/solution.py
+++ b/solution.py
@@ -154,6 +154,7 @@
 
     with jax.named_scope("hot_expert"):
         pair = jnp.concatenate([tokens, lax.ppermute(tokens, "dp", swap)], axis=0)
+        cold_sum, pair = lax.optimization_barrier((cold_sum, pair))
         gate_val = jnp.dot(pair, hot_w[0], preferred_element_type=jnp.float32)
         up_val = jnp.dot(pair, hot_w[1], preferred_element_type=jnp.float32)
         hidden = (jax.nn.silu(gate_val) * up_val).astype(jnp.bfloat16)

time: 450 us -> 411 us (0.913)
  waiting for transfers between devices: 264 us -> 224 us
    psum x1, waiting for transfers between devices: 161 us -> 52.1 us  [on_device(): hot_w = tuple((lax.psum(w, 'expert') for w in held))]
    all_to_all x1, waiting for transfers between devices: 0.01 us -> 96.9 us  [on_device(): returned = lax.all_to_all(results, ('expert', 'dp'), 0, 0, tiled=True)]
    all_to_all x1, waiting for transfers between devices: 102 us -> 71.9 us  [on_device(): arrived = lax.all_to_all(outgoing, ('expert', 'dp'), 0, 0, tiled=True)]
    unnamed x22 -> x19, local copies, waits for them, and re-layouts: 17.6 us -> 17.4 us
  transfers between devices with their start and end apart: 8 -> 8, of which waited for: 3 -> 4; matrix products, arithmetic and copies ran while one was open for 24% -> 29% of each run, Pallas kernels for 0% -> 0%
where the time goes in v5:
time: 411 us; the launch traced here: 403 us
  waiting for transfers between devices  224 us (55%)
  matrix products  67.6 us (16%)
  other arithmetic  34.5 us (8%)
  local copies, waits for them, and re-layouts  33.3 us (8%)
  starting transfers between devices  29 us (7%)
  between operations  14.5 us (4%)
    all_to_all x1, waiting for transfers between devices, on_device(): returned = lax.all_to_all(results, ('expert', 'dp'), 0, 0, tiled=True)  96.9 us
    all_to_all x1, waiting for transfers between devices, on_device(): arrived = lax.all_to_all(outgoing, ('expert', 'dp'), 0, 0, tiled=True)  71.9 us
    psum x1, waiting for transfers between devices, on_device(): hot_w = tuple((lax.psum(w, 'expert') for w in held))  52.1 us
    dot_general x1, matrix products, on_device(): jnp.einsum('esd,dh->esh', arrived, own[1], preferred_element_type=jnp.flo...  18.7 us
    dot_general x1, matrix products, on_device(): jnp.einsum('esd,dh->esh', arrived, own[0], preferred_element_type=jnp.flo...  18.2 us
    unnamed x19, local copies, waits for them, and re-layouts  17.4 us
    dot_general x1, matrix products, on_device(): jnp.einsum('esp,esd->pd', combine, returned.astype(jnp.float32), precisio...  13.6 us
    all_to_all x1, starting transfers between devices, on_device(): returned = lax.all_to_all(results, ('expert', 'dp'), 0, 0, tiled=True)  11.6 us
  transfers between devices with their start and end apart: 8, of which 4 were waited for; matrix products, arithmetic and copies ran while one was open for 29% of the time, Pallas kernels for 0%

profile of v5, /device:TPU:1, one launch (start us, length us, event | category | flops | bytes accessed | tf_op | source)
XLA Modules:
  0.0 402.8 jit_solution(12692434477712089960)
XLA Ops:
  6.5 4.8 %select_bitcast_fusion = bf16[384,4096]{1,0:T(8,128)(2,1)} fusion(pred[]{:T(512)S(6)} %eq.102, bf16[1,768,4096]{2,1,0:T(8,128)(2,1)} %param.10), kind=kLoop, calls=%fused_computation.15 | loop fusion | flops 1572864 | bytes 9437185 | tf_op jit(solution)/shard_map/hot_weight_broadcast/jit(_where)/select_n | solution.py:121
  15.0 2.9 fusion.12
  19.8 6.7 %copy.92 = bf16[128,6,4096]{2,1,0:T(8,128)(2,1)} copy(bf16[128,6,4096]{2,0,1:T(8,128)(2,1)S(1)} %convolution_convert_fusion) | data formatting | bytes 12582912 | tf_op jit(solution)/shard_map/dispatch/convert_element_type | solution.py:103
  26.5 10.7 %all-to-all-start = ((bf16[128,6,4096]{2,1,0:T(8,128)(2,1)}), bf16[128,6,4096]{2,1,0:T(8,128)(2,1)}, u32[]{:S(2)}, u32[]{:S(2)}) async-start(bf16[128,6,4096]{2,1,0:T(8,128)(2,1)} %copy.92), calls=%async_computation | async-start | bytes 16777216 | tf_op jit(solution)/shard_map/dispatch/all_to_all | solution.py:104
  37.2 8.6 %copy.97 = bf16[1,4096,768]{1,2,0:T(8,128)(2,1)} copy(bf16[1,4096,768]{2,1,0:T(8,128)(2,1)} %param.8) | data formatting | bytes 12582912 | tf_op args[1]
  45.8 4.9 %select_bitcast_fusion.2 = bf16[4096,384]{0,1:T(8,128)(2,1)} fusion(pred[]{:T(512)S(6)} %eq.102, bf16[4096,2,384]{0,2,1:T(8,128)(2,1)} %bitcast.58), kind=kLoop, calls=%fused_computation.17 | loop fusion | flops 1572864 | bytes 9437185 | tf_op jit(solution)/shard_map/hot_weight_broadcast/jit(_where)/select_n | solution.py:119
  51.8 8.7 %copy.98 = bf16[1,4096,768]{1,2,0:T(8,128)(2,1)} copy(bf16[1,4096,768]{2,1,0:T(8,128)(2,1)} %param.9) | data formatting | bytes 12582912 | tf_op args[2]
  60.5 5.0 %select_bitcast_fusion.1 = bf16[4096,384]{0,1:T(8,128)(2,1)} fusion(pred[]{:T(512)S(6)} %eq.102, bf16[4096,2,384]{0,2,1:T(8,128)(2,1)} %bitcast.54), kind=kLoop, calls=%fused_computation.16 | loop fusion | flops 1572864 | bytes 9437185 | tf_op jit(solution)/shard_map/hot_weight_broadcast/jit(_where)/select_n | solution.py:120
  66.0 4.4 %bitcast_select_fusion = bf16[384,4096]{1,0:T(8,128)(2,1)} fusion(bf16[384,4096]{1,0:T(8,128)(2,1)} %collective-permute-done.3, pred[]{:T(512)S(6)} %eq.103, pred[]{:T(512)S(6)} %eq.102, pred[]{:T(512)S(6)} %eq.101, bf16[1,768,4096]{2,1,0:T(8,128)(2,1)} %param.10), kind=kLoop, calls=%fused_computation.12 | loop fusion | flops 4718592 | bytes 12582915 | tf_op jit(solution)/shard_map/hot_weight_broadcast/jit(_where)/select_n | solution.py:126
  70.4 4.2 %bitcast_select_fusion.2 = bf16[4096,384]{0,1:T(8,128)(2,1)} fusion(bf16[4096,384]{0,1:T(8,128)(2,1)} %collective-permute-done.1, pred[]{:T(512)S(6)} %eq.103, pred[]{:T(512)S(6)} %eq.102, pred[]{:T(512)S(6)} %eq.101, bf16[4096,2,384]{0,2,1:T(8,128)(2,1)} %bitcast.59), kind=kLoop, calls=%fused_computation.14 | loop fusion | flops 4718592 | bytes 12582915 | tf_op jit(solution)/shard_map/hot_weight_broadcast/jit(_where)/select_n | solution.py:126
  76.6 71.9 %all-to-all-done = bf16[128,6,4096]{2,1,0:T(8,128)(2,1)} async-done(((bf16[128,6,4096]{2,1,0:T(8,128)(2,1)}), bf16[128,6,4096]{2,1,0:T(8,128)(2,1)}, u32[]{:S(2)}, u32[]{:S(2)}) %all-to-all-start) | async-done | bytes 6291488 | tf_op jit(solution)/shard_map/dispatch/all_to_all | solution.py:104
  148.6 18.7 %fusion.1 = f32[128,6,768]{2,0,1:T(8,128)S(1)} fusion(bf16[1,4096,768]{2,1,0:T(8,128)(2,1)} %param.9, bf16[128,6,4096]{2,1,0:T(8,128)(2,1)} %all-to-all-done), kind=kOutput, calls=%fused_computation.3 | convolution fusion | flops 4831838208 | bytes 14942208 | tf_op jit(solution)/shard_map/expert_ffn/esd,dh->esh/dot_general | solution.py:133
  167.3 18.2 %multiply_convert_fusion = bf16[128,6,768]{2,0,1:T(8,128)(2,1)S(1)} fusion(f32[128,6,768]{2,0,1:T(8,128)S(1)} %fusion.1, bf16[1,4096,768]{2,1,0:T(8,128)(2,1)} %param.8, bf16[128,6,4096]{2,1,0:T(8,128)(2,1)} %all-to-all-done), kind=kOutput, calls=%fused_computation.18 | convolution fusion | flops 4835377152 | bytes 16121856 | tf_op jit(solution)/shard_map/expert_ffn/esd,dh->esh/dot_general | solution.py:132
  185.5 5.3 %convolution_convert_fusion.1 = bf16[128,6,4096]{2,0,1:T(8,128)(2,1)S(1)} fusion(bf16[128,6,768]{2,0,1:T(8,128)(2,1)S(1)} %multiply_convert_fusion, bf16[1,768,4096]{2,1,0:T(8,128)(2,1)S(1)} %bitcast.61), kind=kOutput, calls=%fused_computation.1 | convolution fusion | flops 4834983936 | bytes 13762560 | tf_op jit(solution)/shard_map/expert_ffn/esh,hd->esd/dot_general | solution.py:135
  190.8 6.7 %copy.95 = bf16[128,6,4096]{2,1,0:T(8,128)(2,1)} copy(bf16[128,6,4096]{2,0,1:T(8,128)(2,1)S(1)} %convolution_convert_fusion.1) | data formatting | bytes 12582912 | tf_op jit(solution)/shard_map/expert_ffn/convert_element_type | solution.py:137
  197.6 11.6 %all-to-all-start.1 = ((bf16[128,6,4096]{2,1,0:T(8,128)(2,1)}), bf16[128,6,4096]{2,1,0:T(8,128)(2,1)}, u32[]{:S(2)}, u32[]{:S(2)}) async-start(bf16[128,6,4096]{2,1,0:T(8,128)(2,1)} %copy.95), calls=%async_computation.1 | async-start | bytes 16777216 | tf_op jit(solution)/shard_map/return/all_to_all | solution.py:140
  210.5 3.1 select_reduce_fusion
  214.9 96.9 %all-to-all-done.1 = bf16[128,6,4096]{2,1,0:T(8,128)(2,1)} async-done(((bf16[128,6,4096]{2,1,0:T(8,128)(2,1)}), bf16[128,6,4096]{2,1,0:T(8,128)(2,1)}, u32[]{:S(2)}, u32[]{:S(2)}) %all-to-all-start.1) | async-done | bytes 6291488 | tf_op jit(solution)/shard_map/return/all_to_all | solution.py:140
  311.7 13.6 %fusion.7 = f32[96,4096]{1,0:T(8,128)S(1)} fusion(f32[128,6,96]{0,2,1:T(8,128)S(1)} %select_reduce_fusion, bf16[128,6,4096]{2,1,0:T(8,128)(2,1)} %all-to-all-done.1), kind=kOutput, calls=%fused_computation.9 | convolution fusion | flops 3623878656 | bytes 8159232 | tf_op jit(solution)/shard_map/combine/esp,esd->pd/dot_general | solution.py:147
  325.3 52.1 %all-reduce.3.cloned.1.call-done = (bf16[384,4096]{1,0:T(8,128)(2,1)}, bf16[4096,384]{0,1:T(8,128)(2,1)}, bf16[4096,384]{0,1:T(8,128)(2,1)}) async-done(((bf16[384,4096]{1,0:T(8,128)(2,1)}, bf16[4096,384]{0,1:T(8,128)(2,1)}, bf16[4096,384]{0,1:T(8,128)(2,1)}), (bf16[384,4096]{1,0:T(8,128)(2,1)}, bf16[4096,384]{0,1:T(8,128)(2,1)}, bf16[4096,384]{0,1:T(8,128)(2,1)})) %all-reduce.3.cloned.1.call-update) | async-done | bytes 9437200 | tf_op jit(solution)/shard_map/hot_weight_broadcast/psum | solution.py:129
  377.4 3.1 fusion.28
  380.5 6.9 %fusion.23 = f32[192,4096]{1,0:T(8,128)} fusion(bf16[384,4096]{1,0:T(8,128)(2,1)} %get-tuple-element.9, f32[192,384]{1,0:T(8,128)S(1)} %fusion.28, bf16[192,4096]{1,0:T(8,128)(2,1)S(1)} %pad_maximum_fusion, bf16[4096,384]{0,1:T(8,128)(2,1)} %get-tuple-element.10), kind=kOutput, calls=%fused_computation.38 | convolution fusion | flops 1208401920 | bytes 11304960 | tf_op jit(solution)/shard_map/hot_expert/dot_general | solution.py:161
  389.0 2.5 collective-permute-start.4
  391.5 3.0 collective-permute-done.4
  (50 shorter events, 13.9 us)
Async XLA Ops:
  6.5 6.3 %copy-start.2 = (s32[96,8]{0,1:T(8,128)S(1)}, s32[96,8]{0,1:T(8,128)}, u32[]{:S(2)}) copy-start(s32[96,8]{0,1:T(8,128)} %param.11) | copy-start | bytes 9220
  11.4 3.5 copy-start.3
  11.4 6.6 %copy-start.1 = (bf16[96,4096]{1,0:T(8,128)(2,1)S(1)}, bf16[96,4096]{1,0:T(8,128)(2,1)}, u32[]{:S(2)}) copy-start(bf16[96,4096]{1,0:T(8,128)(2,1)} %param.7) | copy-start | bytes 2359300
  11.4 54.6 %collective-permute-start.3 = (bf16[384,4096]{1,0:T(8,128)(2,1)}, bf16[384,4096]{1,0:T(8,128)(2,1)}, u32[]{:S(2)}, u32[]{:S(2)}) collective-permute-start(bf16[384,4096]{1,0:T(8,128)(2,1)} %select_bitcast_fusion), channel_id=1, source_target_pairs={{0,1},{1,0},{2,3},{3,2},{4,5},{5,4},{6,7},{7,6},{8,9},{9,8},{10,11... | collective-permute-start | bytes 9437192 | tf_op jit(solution)/shard_map/hot_weight_broadcast/ppermute | solution.py:124
  26.5 122.1 %all-to-all-start = ((bf16[128,6,4096]{2,1,0:T(8,128)(2,1)}), bf16[128,6,4096]{2,1,0:T(8,128)(2,1)}, u32[]{:S(2)}, u32[]{:S(2)}) async-start(bf16[128,6,4096]{2,1,0:T(8,128)(2,1)} %copy.92), calls=%async_computation | async-start | bytes 16777216 | tf_op jit(solution)/shard_map/dispatch/all_to_all | solution.py:104
  37.2 340.3 %all-reduce.3.cloned.1.call-start = ((), (), s32[]{:S(2)}) async-start(), calls=%async_computation.2 | async-start | bytes 18874368 | tf_op jit(solution)/shard_map/hot_weight_broadcast/psum | solution.py:129
  50.7 19.7 %collective-permute-start.1 = (bf16[4096,384]{0,1:T(8,128)(2,1)}, bf16[4096,384]{0,1:T(8,128)(2,1)}, u32[]{:S(2)}, u32[]{:S(2)}) collective-permute-start(bf16[4096,384]{0,1:T(8,128)(2,1)} %select_bitcast_fusion.2), channel_id=1, source_target_pairs={{0,1},{1,0},{2,3},{3,2},{4,5},{5,4},{6,7},{7,6},{8,9},{9,8},{10,11... | collective-permute-start | bytes 9437192 | tf_op jit(solution)/shard_map/hot_weight_broadcast/ppermute | solution.py:124
  60.5 14.1 %slice-start = ((s8[6291456]{0:T(1024)(128)(4,1)}), s8[2097152]{0:T(1024)(128)(4,1)S(1)}, s32[]{:S(2)}) async-start(s8[6291456]{0:T(1024)(128)(4,1)} %bitcast.55), calls=%async_computation.3 | async-start | bytes 4194304
  65.5 9.1 %collective-permute-start.2 = (bf16[4096,384]{0,1:T(8,128)(2,1)}, bf16[4096,384]{0,1:T(8,128)(2,1)}, u32[]{:S(2)}, u32[]{:S(2)}) collective-permute-start(bf16[4096,384]{0,1:T(8,128)(2,1)} %select_bitcast_fusion.1), channel_id=1, source_target_pairs={{0,1},{1,0},{2,3},{3,2},{4,5},{5,4},{6,7},{7,6},{8,9},{9,8},{10,11... | collective-permute-start | bytes 9437192 | tf_op jit(solution)/shard_map/hot_weight_broadcast/ppermute | solution.py:124
  66.0 8.6 %slice-start.1 = ((s8[6291456]{0:T(1024)(128)(4,1)}), s8[4194304]{0:T(1024)(128)(4,1)S(1)}, s32[]{:S(2)}) async-start(s8[6291456]{0:T(1024)(128)(4,1)} %bitcast.55), calls=%async_computation.4 | async-start | bytes 8388608
  148.6 36.9 %slice-start.2 = ((s8[6291456]{0:T(1024)(128)(4,1)}), s8[4194304]{0:T(1024)(128)(4,1)S(1)}, s32[]{:S(2)}) async-start(s8[6291456]{0:T(1024)(128)(4,1)} %bitcast.60), calls=%async_computation.5 | async-start | bytes 8388608
  167.3 18.2 %slice-start.3 = ((s8[6291456]{0:T(1024)(128)(4,1)}), s8[2097152]{0:T(1024)(128)(4,1)S(1)}, s32[]{:S(2)}) async-start(s8[6291456]{0:T(1024)(128)(4,1)} %bitcast.60), calls=%async_computation.6 | async-start | bytes 4194304
  197.6 114.2 %all-to-all-start.1 = ((bf16[128,6,4096]{2,1,0:T(8,128)(2,1)}), bf16[128,6,4096]{2,1,0:T(8,128)(2,1)}, u32[]{:S(2)}, u32[]{:S(2)}) async-start(bf16[128,6,4096]{2,1,0:T(8,128)(2,1)} %copy.95), calls=%async_computation.1 | async-start | bytes 16777216 | tf_op jit(solution)/shard_map/return/all_to_all | solution.py:140
  209.2 4.4 %collective-permute-start = (bf16[96,4096]{1,0:T(8,128)(2,1)S(1)}, bf16[96,4096]{1,0:T(8,128)(2,1)}, u32[]{:S(2)}, u32[]{:S(2)}) collective-permute-start(bf16[96,4096]{1,0:T(8,128)(2,1)S(1)} %copy-done.1), channel_id=1, source_target_pairs={{0,1},{1,0},{2,3},{3,2},{4,5},{5,4},{6,7},{7,6},{8,9},{9,8},{10,11... | collective-permute-start | bytes 2359304 | tf_op jit(solution)/shard_map/hot_expert/ppermute | solution.py:156
  387.4 7.2 %copy-start = (f32[192,4096]{1,0:T(8,128)S(1)}, f32[192,4096]{1,0:T(8,128)}, u32[]{:S(2)}) copy-start(f32[192,4096]{1,0:T(8,128)} %fusion.23) | copy-start | bytes 9437188
  389.0 5.5 %collective-permute-start.4 = (f32[96,4096]{1,0:T(8,128)S(1)}, f32[96,4096]{1,0:T(8,128)S(1)}, u32[]{:S(2)}, u32[]{:S(2)}) collective-permute-start(f32[96,4096]{1,0:T(8,128)S(1)} %slice.54), channel_id=1, source_target_pairs={{0,1},{1,0},{2,3},{3,2},{4,5},{5,4},{6,7},{7,6},{8,9},{9,8},{10,11... | collective-permute-start | bytes 4718600 | tf_op jit(solution)/shard_map/hot_expert/ppermute | solution.py:163
Sparse Core Ops, SparseCore 0:
  76.7 300.6 all-reduce.2

commit v6 on v5

--- a/solution.py
+++ b/solution.py
@@ -107,17 +107,18 @@
         core = lax.axis_index("dp")
         partner = me + 1 - 2 * core
         half = own[0].shape[1] // 2
-        split_g = own[0].reshape(own[0].shape[0], 2, half)
-        split_u = own[1].reshape(own[1].shape[0], 2, half)
+        rows = own[0].shape[0] // 2
+        split_g = own[0].reshape(2, rows, own[0].shape[1])
+        split_u = own[1].reshape(2, rows, own[1].shape[1])
         split_d = own[2].reshape(2, half, own[2].shape[1])
         mine = (
-            jnp.where(core == 0, split_g[:, 0], split_g[:, 1]),
-            jnp.where(core == 0, split_u[:, 0], split_u[:, 1]),
+            jnp.where(core == 0, split_g[0], split_g[1]),
+            jnp.where(core == 0, split_u[0], split_u[1]),
             jnp.where(core == 0, split_d[0], split_d[1]),
         )
         theirs = (
-            jnp.where(core == 0, split_g[:, 1], split_g[:, 0]),
-            jnp.where(core == 0, split_u[:, 1], split_u[:, 0]),
+            jnp.where(core == 0, split_g[1], split_g[0]),
+            jnp.where(core == 0, split_u[1], split_u[0]),
             jnp.where(core == 0, split_d[1], split_d[0]),
         )
         swap = [(0, 1), (1, 0)]
@@ -153,15 +154,27 @@
         )
 
     with jax.named_scope("hot_expert"):
-        pair = jnp.concatenate([tokens, lax.ppermute(tokens, "dp", swap)], axis=0)
+        other_tokens = lax.ppermute(tokens, "dp", swap)
+        pair = jnp.where(
+            core == 0,
+            jnp.concatenate([tokens, other_tokens], axis=0),
+            jnp.concatenate([other_tokens, tokens], axis=0),
+        )
         cold_sum, pair = lax.optimization_barrier((cold_sum, pair))
-        gate_val = jnp.dot(pair, hot_w[0], preferred_element_type=jnp.float32)
-        up_val = jnp.dot(pair, hot_w[1], preferred_element_type=jnp.float32)
-        hidden = (jax.nn.silu(gate_val) * up_val).astype(jnp.bfloat16)
+        cols = pair.reshape(pair.shape[0], 2, rows)
+        pair_part = jnp.where(core == 0, cols[:, 0], cols[:, 1])
+        gate_part = jnp.dot(pair_part, hot_w[0], preferred_element_type=jnp.float32)
+        up_part = jnp.dot(pair_part, hot_w[1], preferred_element_type=jnp.float32)
+        both = jnp.stack([gate_part, up_part]).reshape(2, pair.shape[0], 2, half)
+        keep_part = jnp.where(core == 0, both[:, :, 0], both[:, :, 1])
+        send_part = jnp.where(core == 0, both[:, :, 1], both[:, :, 0])
+        full = keep_part + lax.ppermute(send_part, "dp", swap)
+        hidden = (jax.nn.silu(full[0]) * full[1]).astype(jnp.bfloat16)
         partial = jnp.dot(hidden, hot_w[2], preferred_element_type=jnp.float32)
-        hot_out = (
-            partial[:tok_rows] + lax.ppermute(partial[tok_rows:], "dp", swap)
-        ).astype(jnp.bfloat16)
+        by_core = partial.reshape(2, tok_rows, partial.shape[1])
+        own_rows = jnp.where(core == 0, by_core[0], by_core[1])
+        other_rows = jnp.where(core == 0, by_core[1], by_core[0])
+        hot_out = (own_rows + lax.ppermute(other_rows, "dp", swap)).astype(jnp.bfloat16)
         hot_weight = jnp.sum(
             jnp.where(route_ids == hot_id, route_gates, jnp.zeros_like(route_gates)), axis=1
         )

time: 411 us -> 403 us (0.981)
  local copies, waits for them, and re-layouts: 33.3 us -> 24.5 us
  waiting for transfers between devices: 224 us -> 230 us
  matrix products: 67.6 us -> 63.3 us
    unnamed x19 -> x25, local copies, waits for them, and re-layouts: 17.4 us -> 0.91 us
    all_to_all x1, waiting for transfers between devices: 71.9 us -> 84.2 us  [on_device(): arrived = lax.all_to_all(outgoing, ('expert', 'dp'), 0, 0, tiled=True)]
    psum x1, waiting for transfers between devices: 52.1 us -> 43.9 us  [on_device(): hot_w = tuple((lax.psum(w, 'expert') for w in held))]
    select_n x3 -> x1, other arithmetic: 10.6 us -> 4.29 us  [on_device(): jnp.where(me == hot_id, a, jnp.where(partner == hot_id, b, jnp.zeros_like...]
    dot_general x0 -> x2, other arithmetic: none -> 6.18 us  [the longest x1 3.09 us: on_device(): up_part = jnp.dot(pair_part, hot_w[1], preferred_element_type=jnp.float32)]
    dot_general x0 -> x2, local copies, waits for them, and re-layouts: none -> 5.94 us  [the longest x1 2.99 us: on_device(): up_part = jnp.dot(pair_part, hot_w[1], preferred_element_type=jnp.float32)]
    dot_general x1, matrix products: 6.86 us -> 1.01 us  [on_device(): partial = jnp.dot(hidden, hot_w[2], preferred_element_type=jnp.float32)]
    select_n x2 -> x5, other arithmetic: 9.84 us -> 8.7 us  [the longest x1 4.85 us: on_device(): jnp.where(core == 0, split_u[1], split_u[0])]
  transfers between devices with their start and end apart: 8 -> 9, of which waited for: 4 -> 5; matrix products, arithmetic and copies ran while one was open for 29% -> 25% of each run, Pallas kernels for 0% -> 0%
where the time goes in v6:
time: 403 us; the launch traced here: 396 us
  waiting for transfers between devices  230 us (57%)
  matrix products  63.3 us (16%)
  starting transfers between devices  31.8 us (8%)
  other arithmetic  31 us (8%)
  local copies, waits for them, and re-layouts  24.5 us (6%)
  between operations  14.6 us (4%)
    all_to_all x1, waiting for transfers between devices, on_device(): returned = lax.all_to_all(results, ('expert', 'dp'), 0, 0, tiled=True)  97.6 us
    all_to_all x1, waiting for transfers between devices, on_device(): arrived = lax.all_to_all(outgoing, ('expert', 'dp'), 0, 0, tiled=True)  84.2 us
    psum x1, waiting for transfers between devices, on_device(): hot_w = tuple((lax.psum(w, 'expert') for w in held))  43.9 us
    dot_general x1, matrix products, on_device(): jnp.einsum('esd,dh->esh', arrived, own[0], preferred_element_type=jnp.flo...  18.2 us
    dot_general x1, matrix products, on_device(): jnp.einsum('esd,dh->esh', arrived, own[1], preferred_element_type=jnp.flo...  18 us
    dot_general x1, matrix products, on_device(): jnp.einsum('esp,esd->pd', combine, returned.astype(jnp.float32), precisio...  14.5 us
    all_to_all x1, starting transfers between devices, on_device(): returned = lax.all_to_all(results, ('expert', 'dp'), 0, 0, tiled=True)  13.5 us
    all_to_all x1, starting transfers between devices, on_device(): arrived = lax.all_to_all(outgoing, ('expert', 'dp'), 0, 0, tiled=True)  12 us
  transfers between devices with their start and end apart: 9, of which 5 were waited for; matrix products, arithmetic and copies ran while one was open for 25% of the time, Pallas kernels for 0%

profile of v6, /device:TPU:1, one launch (start us, length us, event | category | flops | bytes accessed | tf_op | source)
XLA Modules:
  0.0 395.6 jit_solution(611456419219684926)
XLA Ops:
  9.6 2.9 fusion.14
  14.3 6.7 %copy.95 = bf16[128,6,4096]{2,1,0:T(8,128)(2,1)} copy(bf16[128,6,4096]{2,0,1:T(8,128)(2,1)S(1)} %convolution_convert_fusion) | data formatting | bytes 12582912 | tf_op jit(solution)/shard_map/dispatch/convert_element_type | solution.py:103
  21.0 12.0 %all-to-all-start = ((bf16[128,6,4096]{2,1,0:T(8,128)(2,1)}), bf16[128,6,4096]{2,1,0:T(8,128)(2,1)}, u32[]{:S(2)}, u32[]{:S(2)}) async-start(bf16[128,6,4096]{2,1,0:T(8,128)(2,1)} %copy.95), calls=%async_computation | async-start | bytes 16777216 | tf_op jit(solution)/shard_map/dispatch/all_to_all | solution.py:104
  33.1 3.3 select_bitcast_fusion.2
  37.6 4.9 %select_bitcast_fusion.1 = bf16[2048,768]{1,0:T(8,128)(2,1)} fusion(pred[]{:T(512)S(6)} %eq.106, bf16[1,4096,768]{2,1,0:T(8,128)(2,1)} %param.9), kind=kLoop, calls=%fused_computation.18 | loop fusion | flops 1572864 | bytes 9437185 | tf_op jit(solution)/shard_map/hot_weight_broadcast/jit(_where)/select_n | solution.py:121
  45.5 3.1 fusion.13
  48.6 2.9 copy.102
  51.5 3.1 fusion.12
  54.6 3.0 copy.103
  57.6 4.3 %bitcast_select_fusion = bf16[384,4096]{1,0:T(8,128)(2,1)} fusion(bf16[384,4096]{1,0:T(8,128)(2,1)} %collective-permute-done.4, pred[]{:T(512)S(6)} %eq.109, pred[]{:T(512)S(6)} %eq.106, pred[]{:T(512)S(6)} %eq.108, bf16[1,768,4096]{2,1,0:T(8,128)(2,1)} %param.10), kind=kLoop, calls=%fused_computation.12 | loop fusion | flops 4718592 | bytes 12582915 | tf_op jit(solution)/shard_map/hot_weight_broadcast/jit(_where)/select_n | solution.py:127
  61.9 84.2 %all-to-all-done = bf16[128,6,4096]{2,1,0:T(8,128)(2,1)} async-done(((bf16[128,6,4096]{2,1,0:T(8,128)(2,1)}), bf16[128,6,4096]{2,1,0:T(8,128)(2,1)}, u32[]{:S(2)}, u32[]{:S(2)}) %all-to-all-start) | async-done | bytes 6291488 | tf_op jit(solution)/shard_map/dispatch/all_to_all | solution.py:104
  146.1 18.0 %fusion.1 = f32[128,6,768]{2,0,1:T(8,128)S(1)} fusion(bf16[1,4096,768]{2,1,0:T(8,128)(2,1)} %param.9, bf16[128,6,4096]{2,1,0:T(8,128)(2,1)} %all-to-all-done), kind=kOutput, calls=%fused_computation.3 | convolution fusion | flops 4831838208 | bytes 14942208 | tf_op jit(solution)/shard_map/expert_ffn/esd,dh->esh/dot_general | solution.py:134
  164.1 18.2 %multiply_convert_fusion = bf16[128,6,768]{2,0,1:T(8,128)(2,1)S(1)} fusion(f32[128,6,768]{2,0,1:T(8,128)S(1)} %fusion.1, bf16[1,4096,768]{2,1,0:T(8,128)(2,1)} %param.8, bf16[128,6,4096]{2,1,0:T(8,128)(2,1)} %all-to-all-done), kind=kOutput, calls=%fused_computation.20 | convolution fusion | flops 4835377152 | bytes 16121856 | tf_op jit(solution)/shard_map/expert_ffn/esd,dh->esh/dot_general | solution.py:133
  182.4 5.3 %convolution_convert_fusion.1 = bf16[128,6,4096]{2,0,1:T(8,128)(2,1)S(1)} fusion(bf16[128,6,768]{2,0,1:T(8,128)(2,1)S(1)} %multiply_convert_fusion, bf16[1,768,4096]{2,1,0:T(8,128)(2,1)S(1)} %bitcast.102), kind=kOutput, calls=%fused_computation.1 | convolution fusion | flops 4834983936 | bytes 13762560 | tf_op jit(solution)/shard_map/expert_ffn/esh,hd->esd/dot_general | solution.py:136
  187.7 6.7 %copy.98 = bf16[128,6,4096]{2,1,0:T(8,128)(2,1)} copy(bf16[128,6,4096]{2,0,1:T(8,128)(2,1)S(1)} %convolution_convert_fusion.1) | data formatting | bytes 12582912 | tf_op jit(solution)/shard_map/expert_ffn/convert_element_type | solution.py:138
  194.4 13.5 %all-to-all-start.1 = ((bf16[128,6,4096]{2,1,0:T(8,128)(2,1)}), bf16[128,6,4096]{2,1,0:T(8,128)(2,1)}, u32[]{:S(2)}, u32[]{:S(2)}) async-start(bf16[128,6,4096]{2,1,0:T(8,128)(2,1)} %copy.98), calls=%async_computation.1 | async-start | bytes 16777216 | tf_op jit(solution)/shard_map/return/all_to_all | solution.py:141
  209.3 3.8 select_reduce_fusion
  213.4 97.6 %all-to-all-done.1 = bf16[128,6,4096]{2,1,0:T(8,128)(2,1)} async-done(((bf16[128,6,4096]{2,1,0:T(8,128)(2,1)}), bf16[128,6,4096]{2,1,0:T(8,128)(2,1)}, u32[]{:S(2)}, u32[]{:S(2)}) %all-to-all-start.1) | async-done | bytes 6291488 | tf_op jit(solution)/shard_map/return/all_to_all | solution.py:141
  311.0 14.5 %fusion.7 = f32[96,4096]{1,0:T(8,128)} fusion(f32[128,6,96]{0,2,1:T(8,128)S(1)} %copy-done.5, bf16[128,6,4096]{2,1,0:T(8,128)(2,1)} %all-to-all-done.1), kind=kOutput, calls=%fused_computation.9 | convolution fusion | flops 3623878656 | bytes 8159232 | tf_op jit(solution)/shard_map/combine/esp,esd->pd/dot_general | solution.py:148
  326.7 2.2 fusion.34
  329.9 43.9 %all-reduce.3.cloned.1.call-done = (bf16[384,4096]{1,0:T(8,128)(2,1)}, bf16[2,384,2048]{2,1,0:T(8,128)(2,1)}, bf16[2,384,2048]{2,1,0:T(8,128)(2,1)}) async-done(((bf16[384,4096]{1,0:T(8,128)(2,1)}, bf16[2,384,2048]{2,1,0:T(8,128)(2,1)}, bf16[2,384,2048]{2,1,0:T(8,128)(2,1)}), (bf16[384,4096]{1,0:T(8,128)(2,1)}, bf16[2,384,2048]{2,1,0:T(8,128)(2,1)}, ...) | async-done | bytes 9437200 | tf_op jit(solution)/shard_map/hot_weight_broadcast/psum | solution.py:130
  373.8 3.2 convolution_bitcast_fusion.1
  378.3 2.5 collective-permute-start.3
  384.2 3.0 collective-permute-done.5
  (66 shorter events, 18.1 us)
Async XLA Ops:
  6.5 2.9 copy-start.6
  6.5 2.9 copy-start.7
  6.5 5.9 %copy-start.2 = (bf16[96,4096]{1,0:T(8,128)(2,1)S(1)}, bf16[96,4096]{1,0:T(8,128)(2,1)}, u32[]{:S(2)}) copy-start(bf16[96,4096]{1,0:T(8,128)(2,1)} %param.7) | copy-start | bytes 2359300
  21.0 125.1 %all-to-all-start = ((bf16[128,6,4096]{2,1,0:T(8,128)(2,1)}), bf16[128,6,4096]{2,1,0:T(8,128)(2,1)}, u32[]{:S(2)}, u32[]{:S(2)}) async-start(bf16[128,6,4096]{2,1,0:T(8,128)(2,1)} %copy.95), calls=%async_computation | async-start | bytes 16777216 | tf_op jit(solution)/shard_map/dispatch/all_to_all | solution.py:104
  33.0 340.8 %all-reduce.3.cloned.1.call-start = ((), (), s32[]{:S(2)}) async-start(), calls=%async_computation.2 | async-start | bytes 18874368 | tf_op jit(solution)/shard_map/hot_weight_broadcast/psum | solution.py:130
  33.1 9.6 %slice-start = ((s8[6291456]{0:T(1024)(128)(4,1)}), s8[4194304]{0:T(1024)(128)(4,1)S(1)}, s32[]{:S(2)}) async-start(s8[6291456]{0:T(1024)(128)(4,1)} %bitcast.99), calls=%async_computation.3 | async-start | bytes 8388608
  36.4 6.2 %slice-start.1 = ((s8[6291456]{0:T(1024)(128)(4,1)}), s8[2097152]{0:T(1024)(128)(4,1)S(1)}, s32[]{:S(2)}) async-start(s8[6291456]{0:T(1024)(128)(4,1)} %bitcast.99), calls=%async_computation.4 | async-start | bytes 4194304
  36.4 9.1 %collective-permute-start.1 = (bf16[2048,768]{1,0:T(8,128)(2,1)S(1)}, bf16[2048,768]{1,0:T(8,128)(2,1)}, u32[]{:S(2)}, u32[]{:S(2)}) collective-permute-start(bf16[2048,768]{1,0:T(8,128)(2,1)S(1)} %select_bitcast_fusion.2), channel_id=1, source_target_pairs={{0,1},{1,0},{2,3},{3,2},{4,5},{5,4},{6,7},{7,6},{8,9},{9,8},{10,11... | collective-permute-start | bytes 9437192 | tf_op jit(solution)/shard_map/hot_weight_broadcast/ppermute | solution.py:125
  42.5 9.0 %collective-permute-start.2 = (bf16[2048,768]{1,0:T(8,128)(2,1)}, bf16[2048,768]{1,0:T(8,128)(2,1)}, u32[]{:S(2)}, u32[]{:S(2)}) collective-permute-start(bf16[2048,768]{1,0:T(8,128)(2,1)} %select_bitcast_fusion.1), channel_id=1, source_target_pairs={{0,1},{1,0},{2,3},{3,2},{4,5},{5,4},{6,7},{7,6},{8,9},{9,8},{10,11... | collective-permute-start | bytes 9437192 | tf_op jit(solution)/shard_map/hot_weight_broadcast/ppermute | solution.py:125
  44.7 13.0 %collective-permute-start.4 = (bf16[384,4096]{1,0:T(8,128)(2,1)}, bf16[384,4096]{1,0:T(8,128)(2,1)}, u32[]{:S(2)}, u32[]{:S(2)}) collective-permute-start(bf16[384,4096]{1,0:T(8,128)(2,1)} %select_bitcast_fusion), channel_id=1, source_target_pairs={{0,1},{1,0},{2,3},{3,2},{4,5},{5,4},{6,7},{7,6},{8,9},{9,8},{10,11... | collective-permute-start | bytes 9437192 | tf_op jit(solution)/shard_map/hot_weight_broadcast/ppermute | solution.py:125
  146.1 36.2 %slice-start.2 = ((s8[6291456]{0:T(1024)(128)(4,1)}), s8[4194304]{0:T(1024)(128)(4,1)S(1)}, s32[]{:S(2)}) async-start(s8[6291456]{0:T(1024)(128)(4,1)} %bitcast.101), calls=%async_computation.5 | async-start | bytes 8388608
  164.1 18.2 %slice-start.3 = ((s8[6291456]{0:T(1024)(128)(4,1)}), s8[2097152]{0:T(1024)(128)(4,1)S(1)}, s32[]{:S(2)}) async-start(s8[6291456]{0:T(1024)(128)(4,1)} %bitcast.101), calls=%async_computation.6 | async-start | bytes 4194304
  194.4 13.5 %copy-start.3 = (bf16[96,4096]{1,0:T(8,128)(2,1)S(1)}, bf16[96,4096]{1,0:T(8,128)(2,1)}, u32[]{:S(2)}) copy-start(bf16[96,4096]{1,0:T(8,128)(2,1)} %param.7) | copy-start | bytes 2359300
  194.4 116.6 %all-to-all-start.1 = ((bf16[128,6,4096]{2,1,0:T(8,128)(2,1)}), bf16[128,6,4096]{2,1,0:T(8,128)(2,1)}, u32[]{:S(2)}, u32[]{:S(2)}) async-start(bf16[128,6,4096]{2,1,0:T(8,128)(2,1)} %copy.98), calls=%async_computation.1 | async-start | bytes 16777216 | tf_op jit(solution)/shard_map/return/all_to_all | solution.py:141
  208.0 5.1 %collective-permute-start = (bf16[96,4096]{1,0:T(8,128)(2,1)S(1)}, bf16[96,4096]{1,0:T(8,128)(2,1)S(1)}, u32[]{:S(2)}, u32[]{:S(2)}) collective-permute-start(bf16[96,4096]{1,0:T(8,128)(2,1)S(1)} %copy-done.3), channel_id=1, source_target_pairs={{0,1},{1,0},{2,3},{3,2},{4,5},{5,4},{6,7},{7,6},{8,9},{9,8},{10,11... | collective-permute-start | bytes 2359304 | tf_op jit(solution)/shard_map/hot_expert/ppermute | solution.py:157
  213.1 97.9 %copy-start.5 = (f32[128,6,96]{0,2,1:T(8,128)S(1)}, f32[128,6,96]{0,2,1:T(8,128)}, u32[]{:S(2)}) copy-start(f32[128,6,96]{0,2,1:T(8,128)} %select_reduce_fusion) | copy-start | bytes 884740
  373.8 3.2 copy-start.1
  378.2 4.3 %copy-start = (bf16[384,4096]{1,0:T(8,128)(2,1)S(1)}, bf16[384,4096]{1,0:T(8,128)(2,1)}, u32[]{:S(2)}) copy-start(bf16[384,4096]{1,0:T(8,128)(2,1)} %get-tuple-element.9) | copy-start | bytes 9437188
  378.3 4.1 %collective-permute-start.3 = (f32[2,192,384]{2,1,0:T(8,128)S(1)}, f32[2,192,384]{2,1,0:T(8,128)S(1)}, u32[]{:S(2)}, u32[]{:S(2)}) collective-permute-start(f32[2,192,384]{2,1,0:T(8,128)S(1)} %select_bitcast_fusion.3), channel_id=1, source_target_pairs={{0,1},{1,0},{2,3},{3,2},{4,5},{5,4},{6,7},{7,6},{8,9},{9,8},{10,11... | collective-permute-start | bytes 1769480 | tf_op jit(solution)/shard_map/hot_expert/ppermute | solution.py:171
  383.6 3.7 copy-start.4
  383.7 3.5 collective-permute-start.5
Sparse Core Ops, SparseCore 0:
  62.1 311.6 all-reduce.2

commit v7 on v6

--- a/solution.py
+++ b/solution.py
@@ -8,6 +8,7 @@
 
 
 CAP = 6
+SLOTS = 8
 MESH = pl.DeviceIdType.MESH
 
 
@@ -97,11 +98,14 @@
         dispatch = jnp.any(hit.reshape(experts, CAP, tok_rows, top_k), axis=3)
 
     with jax.named_scope("dispatch"):
-        outgoing = jnp.einsum(
-            "esp,pd->esd", dispatch.astype(tokens.dtype), tokens,
+        padded = jnp.pad(dispatch, ((0, 0), (0, SLOTS - CAP), (0, 0)))
+        outgoing = jnp.dot(
+            padded.reshape(experts * SLOTS, tok_rows).astype(tokens.dtype), tokens,
             preferred_element_type=jnp.float32,
         ).astype(tokens.dtype)
-        arrived = lax.all_to_all(outgoing, ("expert", "dp"), 0, 0, tiled=True)
+        arrived = lax.all_to_all(
+            outgoing.reshape(experts, SLOTS, -1), ("expert", "dp"), 0, 0, tiled=True
+        )
 
     with jax.named_scope("hot_weight_broadcast"):
         core = lax.axis_index("dp")
@@ -130,24 +134,22 @@
         hot_w = tuple(lax.psum(w, "expert") for w in held)
 
     with jax.named_scope("expert_ffn"):
-        gate_val = jnp.einsum("esd,dh->esh", arrived, own[0], preferred_element_type=jnp.float32)
-        up_val = jnp.einsum("esd,dh->esh", arrived, own[1], preferred_element_type=jnp.float32)
-        hidden = (jax.nn.silu(gate_val) * up_val).astype(jnp.bfloat16)
-        results = jnp.einsum(
-            "esh,hd->esd", hidden, own[2], preferred_element_type=jnp.float32
-        ).astype(jnp.bfloat16)
+        results = expert_ffn(arrived.reshape(experts * SLOTS, -1), *own)
 
     with jax.named_scope("return"):
-        returned = lax.all_to_all(results, ("expert", "dp"), 0, 0, tiled=True)
+        returned = lax.all_to_all(
+            results.reshape(experts, SLOTS, -1), ("expert", "dp"), 0, 0, tiled=True
+        ).reshape(experts * SLOTS, -1)
 
     with jax.named_scope("combine"):
         gate_flat = route_gates.reshape(-1)
         cold_weight = jnp.where(is_kept, gate_flat, jnp.zeros_like(gate_flat))
         weight_of_slot = jnp.where(hit, cold_weight[None, None, :], 0.0)
         combine = jnp.sum(weight_of_slot.reshape(experts, CAP, tok_rows, top_k), axis=3)
+        combine = jnp.pad(combine, ((0, 0), (0, SLOTS - CAP), (0, 0)))
         cold_sum = jnp.einsum(
-            "esp,esd->pd",
-            combine,
+            "sp,sd->pd",
+            combine.reshape(experts * SLOTS, tok_rows),
             returned.astype(jnp.float32),
             precision=lax.Precision.HIGHEST,
             preferred_element_type=jnp.float32,

time: 403 us -> 455 us (1.13); the launches traced: 396 us -> 455 us
  waiting for transfers between devices: 230 us -> 309 us
  local copies, waits for them, and re-layouts: 24.5 us -> 12.7 us
    psum x1, waiting for transfers between devices: 43.9 us -> 123 us  [on_device(): hot_w = tuple((lax.psum(w, 'expert') for w in held))]
    convert_element_type x2 -> x0, local copies, waits for them, and re-layouts: 13.5 us -> none  [the longest x1 6.74 us: on_device(): outgoing = jnp.einsum('esp,pd->esd', dispatch.astype(tokens.dtype), token...]
  transfers between devices with their start and end apart: 9 -> 9, of which waited for: 5 -> 5; matrix products, arithmetic and copies ran while one was open for 25% -> 19% of each run, Pallas kernels for 0% -> 0%
where the time goes in v7:
time: 455 us
  waiting for transfers between devices  309 us (68%)
  matrix products  60.3 us (13%)
  other arithmetic  31.5 us (7%)
  starting transfers between devices  27.8 us (6%)
  between operations  14.4 us (3%)
  local copies, waits for them, and re-layouts  12.7 us (3%)
    psum x1, waiting for transfers between devices, on_device(): hot_w = tuple((lax.psum(w, 'expert') for w in held))  123 us
    all_to_all x1, waiting for transfers between devices, on_device(): lax.all_to_all(results.reshape(experts, SLOTS, -1), ('expert', 'dp'), 0,...  102 us
    all_to_all x1, waiting for transfers between devices, on_device(): lax.all_to_all(outgoing.reshape(experts, SLOTS, -1), ('expert', 'dp'), 0,...  78.5 us
    dot_general x1, matrix products, on_device(): jnp.einsum('sp,sd->pd', combine.reshape(experts * SLOTS, tok_rows), retur...  18.1 us
    all_to_all x1, starting transfers between devices, on_device(): lax.all_to_all(outgoing.reshape(experts, SLOTS, -1), ('expert', 'dp'), 0,...  12 us
    dot_general x1, matrix products, expert_ffn(): gate_val = jnp.dot(in_rows, gate_w, preferred_element_type=jnp.float32)  11.4 us
    dot_general x1, matrix products, expert_ffn(): up_val = jnp.dot(in_rows, up_w, preferred_element_type=jnp.float32)  11 us
    all_to_all x1, starting transfers between devices, on_device(): lax.all_to_all(results.reshape(experts, SLOTS, -1), ('expert', 'dp'), 0,...  9.99 us
  transfers between devices with their start and end apart: 9, of which 5 were waited for; matrix products, arithmetic and copies ran while one was open for 19% of the time, Pallas kernels for 0%

profile of v7, /device:TPU:1, one launch (start us, length us, event | category | flops | bytes accessed | tf_op | source)
XLA Modules:
  0.0 455.1 jit_solution(1690570519580410811)
XLA Ops:
  9.6 2.9 fusion.14
  12.7 5.6 %convert_bitcast_fusion.1 = bf16[128,8,4096]{2,1,0:T(8,128)(2,1)} fusion(bf16[96,4096]{1,0:T(8,128)(2,1)S(1)} %copy-done.3, pred[128,6,96]{2,1,0:T(8,128)(4,1)S(1)} %copy.123), kind=kOutput, calls=%fused_computation.7 | convolution fusion | flops 809500672 | bytes 9248768 | tf_op jit(solution)/shard_map/dispatch/dot_general | solution.py:102
  18.3 12.0 %all-to-all-start = ((bf16[128,8,4096]{2,1,0:T(8,128)(2,1)}), bf16[128,8,4096]{2,1,0:T(8,128)(2,1)}, u32[]{:S(2)}, u32[]{:S(2)}) async-start(bf16[128,8,4096]{2,1,0:T(8,128)(2,1)} %convert_bitcast_fusion.1), calls=%async_computation | async-start | bytes 16777216 | tf_op jit(solution)/shard_map/dispatch/all_to_all | solution.py:106
  30.3 3.3 select_bitcast_fusion.2
  34.8 4.9 %select_bitcast_fusion.1 = bf16[2048,768]{1,0:T(8,128)(2,1)} fusion(pred[]{:T(512)S(6)} %eq.106, bf16[1,4096,768]{2,1,0:T(8,128)(2,1)} %param.9), kind=kLoop, calls=%fused_computation.18 | loop fusion | flops 1572864 | bytes 9437185 | tf_op jit(solution)/shard_map/hot_weight_broadcast/jit(_where)/select_n | solution.py:125
  39.8 2.0 select_bitcast_fusion
  42.2 3.1 fusion.13
  45.3 3.0 copy.114
  48.3 3.1 fusion.12
  51.4 3.0 copy.115
  54.4 78.5 %all-to-all-done = bf16[128,8,4096]{2,1,0:T(8,128)(2,1)} async-done(((bf16[128,8,4096]{2,1,0:T(8,128)(2,1)}), bf16[128,8,4096]{2,1,0:T(8,128)(2,1)}, u32[]{:S(2)}, u32[]{:S(2)}) %all-to-all-start) | async-done | bytes 8388640 | tf_op jit(solution)/shard_map/dispatch/all_to_all | solution.py:106
  132.9 11.0 %fusion = f32[1024,768]{1,0:T(8,128)S(1)} fusion(bf16[128,8,4096]{2,1,0:T(8,128)(2,1)} %all-to-all-done, bf16[1,4096,768]{2,1,0:T(8,128)(2,1)} %param.9), kind=kOutput, calls=%fused_computation | convolution fusion | flops 6442450944 | bytes 17825792 | tf_op jit(solution)/shard_map/expert_ffn/dot_general | solution.py:74
  143.9 11.4 %multiply_convert_fusion = bf16[1024,768]{1,0:T(8,128)(2,1)S(1)} fusion(f32[1024,768]{1,0:T(8,128)S(1)} %fusion, bf16[1,4096,768]{2,1,0:T(8,128)(2,1)} %param.8, bf16[128,8,4096]{2,1,0:T(8,128)(2,1)} %all-to-all-done), kind=kOutput, calls=%fused_computation.20 | convolution fusion | flops 6447169536 | bytes 19398656 | tf_op jit(solution)/shard_map/expert_ffn/dot_general | solution.py:73
  155.3 8.8 %convert_bitcast_fusion = bf16[128,8,4096]{2,1,0:T(8,128)(2,1)} fusion(bf16[1024,768]{1,0:T(8,128)(2,1)S(1)} %multiply_convert_fusion, bf16[1,768,4096]{2,1,0:T(8,128)(2,1)S(1)} %bitcast.110), kind=kOutput, calls=%fused_computation.6 | convolution fusion | flops 6446645248 | bytes 16252928 | tf_op jit(solution)/shard_map/expert_ffn/dot_general | solution.py:76
  164.2 10.0 %all-to-all-start.1 = ((bf16[128,8,4096]{2,1,0:T(8,128)(2,1)}), bf16[128,8,4096]{2,1,0:T(8,128)(2,1)}, u32[]{:S(2)}, u32[]{:S(2)}) async-start(bf16[128,8,4096]{2,1,0:T(8,128)(2,1)} %convert_bitcast_fusion), calls=%async_computation.1 | async-start | bytes 16777216 | tf_op jit(solution)/shard_map/return/all_to_all | solution.py:140
  174.2 4.2 bitcast_select_fusion
  180.8 2.9 select_reduce_fusion
  185.5 102.3 %all-to-all-done.1 = bf16[128,8,4096]{2,1,0:T(8,128)(2,1)} async-done(((bf16[128,8,4096]{2,1,0:T(8,128)(2,1)}), bf16[128,8,4096]{2,1,0:T(8,128)(2,1)}, u32[]{:S(2)}, u32[]{:S(2)}) %all-to-all-start.1) | async-done | bytes 8388640 | tf_op jit(solution)/shard_map/return/all_to_all | solution.py:140
  287.8 18.1 %fusion.9 = f32[96,4096]{1,0:T(8,128)} fusion(f32[128,6,96]{0,2,1:T(8,128)S(1)} %select_reduce_fusion, bf16[128,8,4096]{2,1,0:T(8,128)(2,1)} %all-to-all-done.1), kind=kOutput, calls=%fused_computation.11 | convolution fusion | flops 3623878656 | bytes 10256384 | tf_op jit(solution)/shard_map/combine/sp,sd->pd/dot_general | solution.py:150
  307.1 2.5 fusion.34
  310.5 123.0 %all-reduce.5.cloned.1.call-done = (bf16[384,4096]{1,0:T(8,128)(2,1)}, bf16[2,384,2048]{2,1,0:T(8,128)(2,1)}, bf16[2,384,2048]{2,1,0:T(8,128)(2,1)}) async-done(((bf16[384,4096]{1,0:T(8,128)(2,1)}, bf16[2,384,2048]{2,1,0:T(8,128)(2,1)}, bf16[2,384,2048]{2,1,0:T(8,128)(2,1)}), (bf16[384,4096]{1,0:T(8,128)(2,1)}, bf16[2,384,2048]{2,1,0:T(8,128)(2,1)}, ...) | async-done | bytes 9437200 | tf_op jit(solution)/shard_map/hot_weight_broadcast/psum | solution.py:134
  433.5 3.2 convolution_bitcast_fusion.1
  438.0 2.5 collective-permute-start.3
  443.9 3.0 collective-permute-done.5
  (63 shorter events, 16.5 us)
Async XLA Ops:
  6.5 2.9 copy-start.5
  6.5 2.9 copy-start.6
  6.5 6.2 %copy-start.3 = (bf16[96,4096]{1,0:T(8,128)(2,1)S(1)}, bf16[96,4096]{1,0:T(8,128)(2,1)}, u32[]{:S(2)}) copy-start(bf16[96,4096]{1,0:T(8,128)(2,1)} %param.7) | copy-start | bytes 2359300
  18.3 114.6 %all-to-all-start = ((bf16[128,8,4096]{2,1,0:T(8,128)(2,1)}), bf16[128,8,4096]{2,1,0:T(8,128)(2,1)}, u32[]{:S(2)}, u32[]{:S(2)}) async-start(bf16[128,8,4096]{2,1,0:T(8,128)(2,1)} %convert_bitcast_fusion.1), calls=%async_computation | async-start | bytes 16777216 | tf_op jit(solution)/shard_map/dispatch/all_to_all | solution.py:106
  30.3 9.6 %slice-start = ((s8[6291456]{0:T(1024)(128)(4,1)}), s8[4194304]{0:T(1024)(128)(4,1)S(1)}, s32[]{:S(2)}) async-start(s8[6291456]{0:T(1024)(128)(4,1)} %bitcast.107), calls=%async_computation.3 | async-start | bytes 8388608
  33.6 6.2 %slice-start.1 = ((s8[6291456]{0:T(1024)(128)(4,1)}), s8[2097152]{0:T(1024)(128)(4,1)S(1)}, s32[]{:S(2)}) async-start(s8[6291456]{0:T(1024)(128)(4,1)} %bitcast.107), calls=%async_computation.4 | async-start | bytes 4194304
  33.6 8.6 %collective-permute-start.1 = (bf16[2048,768]{1,0:T(8,128)(2,1)S(1)}, bf16[2048,768]{1,0:T(8,128)(2,1)}, u32[]{:S(2)}, u32[]{:S(2)}) collective-permute-start(bf16[2048,768]{1,0:T(8,128)(2,1)S(1)} %select_bitcast_fusion.2), channel_id=1, source_target_pairs={{0,1},{1,0},{2,3},{3,2},{4,5},{5,4},{6,7},{7,6},{8,9},{9,8},{10,11... | collective-permute-start | bytes 9437192 | tf_op jit(solution)/shard_map/hot_weight_broadcast/ppermute | solution.py:129
  39.7 8.6 %collective-permute-start.2 = (bf16[2048,768]{1,0:T(8,128)(2,1)}, bf16[2048,768]{1,0:T(8,128)(2,1)}, u32[]{:S(2)}, u32[]{:S(2)}) collective-permute-start(bf16[2048,768]{1,0:T(8,128)(2,1)} %select_bitcast_fusion.1), channel_id=1, source_target_pairs={{0,1},{1,0},{2,3},{3,2},{4,5},{5,4},{6,7},{7,6},{8,9},{9,8},{10,11... | collective-permute-start | bytes 9437192 | tf_op jit(solution)/shard_map/hot_weight_broadcast/ppermute | solution.py:129
  41.8 132.4 %collective-permute-start.4 = (bf16[384,4096]{1,0:T(8,128)(2,1)}, bf16[384,4096]{1,0:T(8,128)(2,1)}, u32[]{:S(2)}, u32[]{:S(2)}) collective-permute-start(bf16[384,4096]{1,0:T(8,128)(2,1)} %select_bitcast_fusion), channel_id=1, source_target_pairs={{0,1},{1,0},{2,3},{3,2},{4,5},{5,4},{6,7},{7,6},{8,9},{9,8},{10,11... | collective-permute-start | bytes 9437192 | tf_op jit(solution)/shard_map/hot_weight_broadcast/ppermute | solution.py:129
  132.9 22.4 %slice-start.2 = ((s8[6291456]{0:T(1024)(128)(4,1)}), s8[4194304]{0:T(1024)(128)(4,1)S(1)}, s32[]{:S(2)}) async-start(s8[6291456]{0:T(1024)(128)(4,1)} %bitcast.109), calls=%async_computation.5 | async-start | bytes 8388608
  143.9 11.4 %slice-start.3 = ((s8[6291456]{0:T(1024)(128)(4,1)}), s8[2097152]{0:T(1024)(128)(4,1)S(1)}, s32[]{:S(2)}) async-start(s8[6291456]{0:T(1024)(128)(4,1)} %bitcast.109), calls=%async_computation.6 | async-start | bytes 4194304
  164.2 123.7 %all-to-all-start.1 = ((bf16[128,8,4096]{2,1,0:T(8,128)(2,1)}), bf16[128,8,4096]{2,1,0:T(8,128)(2,1)}, u32[]{:S(2)}, u32[]{:S(2)}) async-start(bf16[128,8,4096]{2,1,0:T(8,128)(2,1)} %convert_bitcast_fusion), calls=%async_computation.1 | async-start | bytes 16777216 | tf_op jit(solution)/shard_map/return/all_to_all | solution.py:140
  174.2 259.3 %all-reduce.5.cloned.1.call-start = ((), (), s32[]{:S(2)}) async-start(), calls=%async_computation.2 | async-start | bytes 18874368 | tf_op jit(solution)/shard_map/hot_weight_broadcast/psum | solution.py:134
  178.5 1.1 copy-start.4
  179.6 4.1 collective-permute-start
  433.5 3.2 copy-start.2
  437.9 4.3 copy-start.1
  438.0 4.1 collective-permute-start.3
  443.3 3.7 copy-start
  443.4 3.5 collective-permute-start.5
Sparse Core Ops, SparseCore 0:
  181.0 252.4 all-reduce.4

commit v8 on v6

--- a/solution.py
+++ b/solution.py
@@ -127,7 +127,8 @@
             jnp.where(me == hot_id, a, jnp.where(partner == hot_id, b, jnp.zeros_like(a)))
             for a, b in zip(mine, from_partner)
         )
-        hot_w = tuple(lax.psum(w, "expert") for w in held)
+        held = lax.optimization_barrier(held)
+        hot_w = lax.optimization_barrier(tuple(lax.psum(w, "expert") for w in held))
 
     with jax.named_scope("expert_ffn"):
         gate_val = jnp.einsum("esd,dh->esh", arrived, own[0], preferred_element_type=jnp.float32)

time: 403 us -> 410 us (1.017)
  waiting for transfers between devices: 230 us -> 237 us
    all_to_all x1, waiting for transfers between devices: 84.2 us -> 90.8 us  [on_device(): arrived = lax.all_to_all(outgoing, ('expert', 'dp'), 0, 0, tiled=True)]
    dot_general x2 -> x0, other arithmetic: 6.18 us -> none  [the longest x1 3.09 us: on_device(): up_part = jnp.dot(pair_part, hot_w[1], preferred_element_type=jnp.float32)]
  transfers between devices with their start and end apart: 9 -> 9, of which waited for: 5 -> 6; matrix products, arithmetic and copies ran while one was open for 25% -> 23% of each run, Pallas kernels for 0% -> 0%
where the time goes in v8:
time: 410 us; the launch traced here: 403 us
  waiting for transfers between devices  237 us (58%)
  matrix products  63.9 us (16%)
  other arithmetic  30.5 us (7%)
  starting transfers between devices  29.1 us (7%)
  local copies, waits for them, and re-layouts  28.2 us (7%)
  between operations  14.6 us (4%)
    all_to_all x1, waiting for transfers between devices, on_device(): returned = lax.all_to_all(results, ('expert', 'dp'), 0, 0, tiled=True)  98.2 us
    all_to_all x1, waiting for transfers between devices, on_device(): arrived = lax.all_to_all(outgoing, ('expert', 'dp'), 0, 0, tiled=True)  90.8 us
    psum x1, waiting for transfers between devices, on_device(): lax.psum(w, 'expert')  42.5 us
    dot_general x1, matrix products, on_device(): jnp.einsum('esd,dh->esh', arrived, own[0], preferred_element_type=jnp.flo...  18.6 us
    dot_general x1, matrix products, on_device(): jnp.einsum('esd,dh->esh', arrived, own[1], preferred_element_type=jnp.flo...  18.1 us
    dot_general x1, matrix products, on_device(): jnp.einsum('esp,esd->pd', combine, returned.astype(jnp.float32), precisio...  14.5 us
    all_to_all x1, starting transfers between devices, on_device(): arrived = lax.all_to_all(outgoing, ('expert', 'dp'), 0, 0, tiled=True)  12 us
    all_to_all x1, starting transfers between devices, on_device(): returned = lax.all_to_all(results, ('expert', 'dp'), 0, 0, tiled=True)  10.8 us
  transfers between devices with their start and end apart: 9, of which 6 were waited for; matrix products, arithmetic and copies ran while one was open for 23% of the time, Pallas kernels for 0%

profile of v8, /device:TPU:1, one launch (start us, length us, event | category | flops | bytes accessed | tf_op | source)
XLA Modules:
  0.0 402.8 jit_solution(5024810192724964080)
XLA Ops:
  9.6 2.9 fusion.12
  14.3 6.7 %copy.95 = bf16[128,6,4096]{2,1,0:T(8,128)(2,1)} copy(bf16[128,6,4096]{2,0,1:T(8,128)(2,1)S(1)} %convolution_convert_fusion) | data formatting | bytes 12582912 | tf_op jit(solution)/shard_map/dispatch/convert_element_type | solution.py:103
  21.0 12.0 %all-to-all-start = ((bf16[128,6,4096]{2,1,0:T(8,128)(2,1)}), bf16[128,6,4096]{2,1,0:T(8,128)(2,1)}, u32[]{:S(2)}, u32[]{:S(2)}) async-start(bf16[128,6,4096]{2,1,0:T(8,128)(2,1)} %copy.95), calls=%async_computation | async-start | bytes 16777216 | tf_op jit(solution)/shard_map/dispatch/all_to_all | solution.py:104
  33.1 5.0 %select_bitcast_fusion.1 = bf16[2048,768]{1,0:T(8,128)(2,1)} fusion(pred[]{:T(512)S(6)} %eq.106, bf16[1,4096,768]{2,1,0:T(8,128)(2,1)} %param.9), kind=kLoop, calls=%fused_computation.16 | loop fusion | flops 1572864 | bytes 9437185 | tf_op jit(solution)/shard_map/hot_weight_broadcast/jit(_where)/select_n | solution.py:121
  39.2 4.9 %select_bitcast_fusion.2 = bf16[2048,768]{1,0:T(8,128)(2,1)} fusion(pred[]{:T(512)S(6)} %eq.106, bf16[1,4096,768]{2,1,0:T(8,128)(2,1)} %param.8), kind=kLoop, calls=%fused_computation.17 | loop fusion | flops 1572864 | bytes 9437185 | tf_op jit(solution)/shard_map/hot_weight_broadcast/jit(_where)/select_n | solution.py:120
  44.2 2.0 select_bitcast_fusion
  47.0 4.3 %bitcast_select_fusion.1 = bf16[2048,768]{1,0:T(8,128)(2,1)} fusion(bf16[2048,768]{1,0:T(8,128)(2,1)} %collective-permute-done.2, pred[]{:T(512)S(6)} %eq.109, pred[]{:T(512)S(6)} %eq.106, pred[]{:T(512)S(6)} %eq.108, bf16[1,4096,768]{2,1,0:T(8,128)(2,1)} %param.9), kind=kLoop, calls=%fused_computation.13 | loop fusion | flops 4718592 | bytes 12582915 | tf_op jit(solution)/shard_map/hot_weight_broadcast/jit(_where)/select_n | solution.py:127
  52.2 1.9 bitcast_select_fusion.2
  57.3 90.8 %all-to-all-done = bf16[128,6,4096]{2,1,0:T(8,128)(2,1)} async-done(((bf16[128,6,4096]{2,1,0:T(8,128)(2,1)}), bf16[128,6,4096]{2,1,0:T(8,128)(2,1)}, u32[]{:S(2)}, u32[]{:S(2)}) %all-to-all-start) | async-done | bytes 6291488 | tf_op jit(solution)/shard_map/dispatch/all_to_all | solution.py:104
  148.1 18.1 %fusion.1 = f32[128,6,768]{2,0,1:T(8,128)S(1)} fusion(bf16[1,4096,768]{2,1,0:T(8,128)(2,1)} %param.9, bf16[128,6,4096]{2,1,0:T(8,128)(2,1)} %all-to-all-done), kind=kOutput, calls=%fused_computation.3 | convolution fusion | flops 4831838208 | bytes 14942208 | tf_op jit(solution)/shard_map/expert_ffn/esd,dh->esh/dot_general | solution.py:135
  166.1 18.6 %multiply_convert_fusion = bf16[128,6,768]{2,0,1:T(8,128)(2,1)S(1)} fusion(f32[128,6,768]{2,0,1:T(8,128)S(1)} %fusion.1, bf16[1,4096,768]{2,1,0:T(8,128)(2,1)} %param.8, bf16[128,6,4096]{2,1,0:T(8,128)(2,1)} %all-to-all-done), kind=kOutput, calls=%fused_computation.18 | convolution fusion | flops 4835377152 | bytes 16121856 | tf_op jit(solution)/shard_map/expert_ffn/esd,dh->esh/dot_general | solution.py:134
  184.8 5.3 %convolution_convert_fusion.1 = bf16[128,6,4096]{2,0,1:T(8,128)(2,1)S(1)} fusion(bf16[128,6,768]{2,0,1:T(8,128)(2,1)S(1)} %multiply_convert_fusion, bf16[1,768,4096]{2,1,0:T(8,128)(2,1)S(1)} %bitcast.100), kind=kOutput, calls=%fused_computation.1 | convolution fusion | flops 4834983936 | bytes 13762560 | tf_op jit(solution)/shard_map/expert_ffn/esh,hd->esd/dot_general | solution.py:137
  190.1 6.7 %copy.98 = bf16[128,6,4096]{2,1,0:T(8,128)(2,1)} copy(bf16[128,6,4096]{2,0,1:T(8,128)(2,1)S(1)} %convolution_convert_fusion.1) | data formatting | bytes 12582912 | tf_op jit(solution)/shard_map/expert_ffn/convert_element_type | solution.py:139
  196.8 10.8 %all-to-all-start.1 = ((bf16[128,6,4096]{2,1,0:T(8,128)(2,1)}), bf16[128,6,4096]{2,1,0:T(8,128)(2,1)}, u32[]{:S(2)}, u32[]{:S(2)}) async-start(bf16[128,6,4096]{2,1,0:T(8,128)(2,1)} %copy.98), calls=%async_computation.1 | async-start | bytes 16777216 | tf_op jit(solution)/shard_map/return/all_to_all | solution.py:142
  209.0 3.1 select_reduce_fusion
  212.4 98.2 %all-to-all-done.1 = bf16[128,6,4096]{2,1,0:T(8,128)(2,1)} async-done(((bf16[128,6,4096]{2,1,0:T(8,128)(2,1)}), bf16[128,6,4096]{2,1,0:T(8,128)(2,1)}, u32[]{:S(2)}, u32[]{:S(2)}) %all-to-all-start.1) | async-done | bytes 6291488 | tf_op jit(solution)/shard_map/return/all_to_all | solution.py:142
  310.7 14.5 %fusion.7 = f32[96,4096]{1,0:T(8,128)} fusion(f32[128,6,96]{0,2,1:T(8,128)S(1)} %select_reduce_fusion, bf16[128,6,4096]{2,1,0:T(8,128)(2,1)} %all-to-all-done.1), kind=kOutput, calls=%fused_computation.9 | convolution fusion | flops 3623878656 | bytes 8159232 | tf_op jit(solution)/shard_map/combine/esp,esd->pd/dot_general | solution.py:149
  326.4 2.2 fusion.32
  330.4 42.5 %all-reduce.3.cloned.1.call-done = (bf16[2048,768]{1,0:T(8,128)(2,1)}, bf16[2048,768]{1,0:T(8,128)(2,1)}, bf16[384,4096]{1,0:T(8,128)(2,1)}) async-done(((bf16[2048,768]{1,0:T(8,128)(2,1)}, bf16[2048,768]{1,0:T(8,128)(2,1)}, bf16[384,4096]{1,0:T(8,128)(2,1)}), (bf16[2048,768]{1,0:T(8,128)(2,1)}, bf16[2048,768]{1,0:T(8,128)(2,1)}, bf16[384,4096]{1,0:T(8,128)(2,1)})) %all-reduce.3.cloned.1.call-update) | async-done | bytes 9437200 | tf_op jit(solution)/shard_map/hot_weight_broadcast/psum | solution.py:131
  372.8 4.8 %copy.108 = bf16[768,2048]{1,0:T(8,128)(2,1)} copy(bf16[768,2048]{0,1:T(8,128)(2,1)} %bitcast.104) | data formatting | bytes 6291456 | tf_op jit(solution)/shard_map/hot_expert/dot_general | solution.py:167
  377.6 3.2 copy.109
  380.8 3.4 convolution_bitcast_fusion.1
  385.5 2.5 collective-permute-start.4
  391.3 3.0 collective-permute-done.5
  (74 shorter events, 20.9 us)
Async XLA Ops:
  6.5 2.9 copy-start.5
  6.5 2.9 copy-start.6
  6.5 5.9 %copy-start.2 = (bf16[96,4096]{1,0:T(8,128)(2,1)S(1)}, bf16[96,4096]{1,0:T(8,128)(2,1)}, u32[]{:S(2)}) copy-start(bf16[96,4096]{1,0:T(8,128)(2,1)} %param.7) | copy-start | bytes 2359300
  21.0 127.0 %all-to-all-start = ((bf16[128,6,4096]{2,1,0:T(8,128)(2,1)}), bf16[128,6,4096]{2,1,0:T(8,128)(2,1)}, u32[]{:S(2)}, u32[]{:S(2)}) async-start(bf16[128,6,4096]{2,1,0:T(8,128)(2,1)} %copy.95), calls=%async_computation | async-start | bytes 16777216 | tf_op jit(solution)/shard_map/dispatch/all_to_all | solution.py:104
  33.0 339.8 %all-reduce.3.cloned.1.call-start = ((), (), s32[]{:S(2)}) async-start(), calls=%async_computation.2 | async-start | bytes 18874368 | tf_op jit(solution)/shard_map/hot_weight_broadcast/psum | solution.py:131
  33.1 11.1 %slice-start.2 = ((s8[6291456]{0:T(1024)(128)(4,1)}), s8[4194304]{0:T(1024)(128)(4,1)S(1)}, s32[]{:S(2)}) async-start(s8[6291456]{0:T(1024)(128)(4,1)} %bitcast.95), calls=%async_computation.5 | async-start | bytes 8388608
  38.0 6.2 %slice-start.3 = ((s8[6291456]{0:T(1024)(128)(4,1)}), s8[2097152]{0:T(1024)(128)(4,1)S(1)}, s32[]{:S(2)}) async-start(s8[6291456]{0:T(1024)(128)(4,1)} %bitcast.95), calls=%async_computation.6 | async-start | bytes 4194304
  38.0 9.0 %collective-permute-start.2 = (bf16[2048,768]{1,0:T(8,128)(2,1)}, bf16[2048,768]{1,0:T(8,128)(2,1)}, u32[]{:S(2)}, u32[]{:S(2)}) collective-permute-start(bf16[2048,768]{1,0:T(8,128)(2,1)} %select_bitcast_fusion.1), channel_id=1, source_target_pairs={{0,1},{1,0},{2,3},{3,2},{4,5},{5,4},{6,7},{7,6},{8,9},{9,8},{10,11... | collective-permute-start | bytes 9437192 | tf_op jit(solution)/shard_map/hot_weight_broadcast/ppermute | solution.py:125
  44.0 7.3 %collective-permute-start.1 = (bf16[2048,768]{1,0:T(8,128)(2,1)}, bf16[2048,768]{1,0:T(8,128)(2,1)}, u32[]{:S(2)}, u32[]{:S(2)}) collective-permute-start(bf16[2048,768]{1,0:T(8,128)(2,1)} %select_bitcast_fusion.2), channel_id=1, source_target_pairs={{0,1},{1,0},{2,3},{3,2},{4,5},{5,4},{6,7},{7,6},{8,9},{9,8},{10,11... | collective-permute-start | bytes 9437192 | tf_op jit(solution)/shard_map/hot_weight_broadcast/ppermute | solution.py:125
  44.2 7.1 %slice-start = ((s8[6291456]{0:T(1024)(128)(4,1)}), s8[2097152]{0:T(1024)(128)(4,1)S(1)}, s32[]{:S(2)}) async-start(s8[6291456]{0:T(1024)(128)(4,1)} %bitcast.93), calls=%async_computation.3 | async-start | bytes 4194304
  46.2 8.4 %collective-permute-start.3 = (bf16[384,4096]{1,0:T(8,128)(2,1)}, bf16[384,4096]{1,0:T(8,128)(2,1)}, u32[]{:S(2)}, u32[]{:S(2)}) collective-permute-start(bf16[384,4096]{1,0:T(8,128)(2,1)} %select_bitcast_fusion), channel_id=1, source_target_pairs={{0,1},{1,0},{2,3},{3,2},{4,5},{5,4},{6,7},{7,6},{8,9},{9,8},{10,11... | collective-permute-start | bytes 9437192 | tf_op jit(solution)/shard_map/hot_weight_broadcast/ppermute | solution.py:125
  47.0 5.2 %slice-start.1 = ((s8[6291456]{0:T(1024)(128)(4,1)}), s8[4194304]{0:T(1024)(128)(4,1)S(1)}, s32[]{:S(2)}) async-start(s8[6291456]{0:T(1024)(128)(4,1)} %bitcast.93), calls=%async_computation.4 | async-start | bytes 8388608
  47.0 7.6 %slice-start.4 = ((s8[6291456]{0:T(1024)(128)(4,1)}), s8[4194304]{0:T(1024)(128)(4,1)S(1)}, s32[]{:S(2)}) async-start(s8[6291456]{0:T(1024)(128)(4,1)} %bitcast.97), calls=%async_computation.7 | async-start | bytes 8388608
  51.3 4.1 %slice-start.5 = ((s8[6291456]{0:T(1024)(128)(4,1)}), s8[2097152]{0:T(1024)(128)(4,1)S(1)}, s32[]{:S(2)}) async-start(s8[6291456]{0:T(1024)(128)(4,1)} %bitcast.97), calls=%async_computation.8 | async-start | bytes 4194304
  148.1 36.7 %slice-start.6 = ((s8[6291456]{0:T(1024)(128)(4,1)}), s8[4194304]{0:T(1024)(128)(4,1)S(1)}, s32[]{:S(2)}) async-start(s8[6291456]{0:T(1024)(128)(4,1)} %bitcast.99), calls=%async_computation.9 | async-start | bytes 8388608
  166.1 18.6 %slice-start.7 = ((s8[6291456]{0:T(1024)(128)(4,1)}), s8[2097152]{0:T(1024)(128)(4,1)S(1)}, s32[]{:S(2)}) async-start(s8[6291456]{0:T(1024)(128)(4,1)} %bitcast.99), calls=%async_computation.10 | async-start | bytes 4194304
  196.8 15.3 %copy-start.3 = (bf16[96,4096]{1,0:T(8,128)(2,1)S(1)}, bf16[96,4096]{1,0:T(8,128)(2,1)}, u32[]{:S(2)}) copy-start(bf16[96,4096]{1,0:T(8,128)(2,1)} %param.7) | copy-start | bytes 2359300
  196.8 113.8 %all-to-all-start.1 = ((bf16[128,6,4096]{2,1,0:T(8,128)(2,1)}), bf16[128,6,4096]{2,1,0:T(8,128)(2,1)}, u32[]{:S(2)}, u32[]{:S(2)}) async-start(bf16[128,6,4096]{2,1,0:T(8,128)(2,1)} %copy.98), calls=%async_computation.1 | async-start | bytes 16777216 | tf_op jit(solution)/shard_map/return/all_to_all | solution.py:142
  207.7 4.4 %collective-permute-start = (bf16[96,4096]{1,0:T(8,128)(2,1)S(1)}, bf16[96,4096]{1,0:T(8,128)(2,1)S(1)}, u32[]{:S(2)}, u32[]{:S(2)}) collective-permute-start(bf16[96,4096]{1,0:T(8,128)(2,1)S(1)} %copy-done.2), channel_id=1, source_target_pairs={{0,1},{1,0},{2,3},{3,2},{4,5},{5,4},{6,7},{7,6},{8,9},{9,8},{10,11... | collective-permute-start | bytes 2359304 | tf_op jit(solution)/shard_map/hot_expert/ppermute | solution.py:158
  380.8 3.4 copy-start
  385.4 4.3 %copy-start.1 = (bf16[384,4096]{1,0:T(8,128)(2,1)S(1)}, bf16[384,4096]{1,0:T(8,128)(2,1)}, u32[]{:S(2)}) copy-start(bf16[384,4096]{1,0:T(8,128)(2,1)} %get-tuple-element.20) | copy-start | bytes 9437188
  385.5 4.1 %collective-permute-start.4 = (f32[2,192,384]{2,1,0:T(8,128)S(1)}, f32[2,192,384]{2,1,0:T(8,128)S(1)}, u32[]{:S(2)}, u32[]{:S(2)}) collective-permute-start(f32[2,192,384]{2,1,0:T(8,128)S(1)} %select_bitcast_fusion.3), channel_id=1, source_target_pairs={{0,1},{1,0},{2,3},{3,2},{4,5},{5,4},{6,7},{7,6},{8,9},{9,8},{10,11... | collective-permute-start | bytes 1769480 | tf_op jit(solution)/shard_map/hot_expert/ppermute | solution.py:172
  390.7 3.7 copy-start.4
  390.9 3.5 collective-permute-start.5
Sparse Core Ops, SparseCore 0:
  57.4 315.3 all-reduce.2

commit v9 on v6

--- a/solution.py
+++ b/solution.py
@@ -130,12 +130,7 @@
         hot_w = tuple(lax.psum(w, "expert") for w in held)
 
     with jax.named_scope("expert_ffn"):
-        gate_val = jnp.einsum("esd,dh->esh", arrived, own[0], preferred_element_type=jnp.float32)
-        up_val = jnp.einsum("esd,dh->esh", arrived, own[1], preferred_element_type=jnp.float32)
-        hidden = (jax.nn.silu(gate_val) * up_val).astype(jnp.bfloat16)
-        results = jnp.einsum(
-            "esh,hd->esd", hidden, own[2], preferred_element_type=jnp.float32
-        ).astype(jnp.bfloat16)
+        results = expert_ffn(arrived.reshape(experts * CAP, -1), *own).reshape(arrived.shape)
 
     with jax.named_scope("return"):
         returned = lax.all_to_all(results, ("expert", "dp"), 0, 0, tiled=True)

time: 403 us -> 394 us (0.978); the launches traced: 396 us -> 395 us
  matrix products: 63.3 us -> 46.1 us
  local copies, waits for them, and re-layouts: 24.5 us -> 38.6 us
    reshape x0 -> x2, local copies, waits for them, and re-layouts: none -> 20.8 us  [the longest x1 10.6 us: on_device(): arrived.reshape(experts * CAP, -1)]
    dot_general x3, matrix products: 41.5 us -> 24.3 us  [the longest x1 9.79 us: expert_ffn(): jnp.dot(hidden, down_w, preferred_element_type=jnp.float32)]
    convert_element_type x1 -> x0, local copies, waits for them, and re-layouts: 6.74 us -> none  [on_device(): results = jnp.einsum('esh,hd->esd', hidden, own[2], preferred_element_typ...]
  transfers between devices with their start and end apart: 9 -> 9, of which waited for: 5 -> 5; matrix products, arithmetic and copies ran while one was open for 25% -> 24% of each run, Pallas kernels for 0% -> 0%
where the time goes in v9:
time: 394 us; the launch traced here: 395 us
  waiting for transfers between devices  234 us (59%)
  matrix products  46.1 us (12%)
  local copies, waits for them, and re-layouts  38.6 us (10%)
  starting transfers between devices  30.9 us (8%)
  other arithmetic  30.8 us (8%)
  between operations  14.4 us (4%)
    all_to_all x1, waiting for transfers between devices, on_device(): returned = lax.all_to_all(results, ('expert', 'dp'), 0, 0, tiled=True)  98.3 us
    all_to_all x1, waiting for transfers between devices, on_device(): arrived = lax.all_to_all(outgoing, ('expert', 'dp'), 0, 0, tiled=True)  84.4 us
    psum x1, waiting for transfers between devices, on_device(): hot_w = tuple((lax.psum(w, 'expert') for w in held))  46.5 us
    dot_general x1, matrix products, on_device(): jnp.einsum('esp,esd->pd', combine, returned.astype(jnp.float32), precisio...  14.5 us
    all_to_all x1, starting transfers between devices, on_device(): returned = lax.all_to_all(results, ('expert', 'dp'), 0, 0, tiled=True)  12.8 us
    all_to_all x1, starting transfers between devices, on_device(): arrived = lax.all_to_all(outgoing, ('expert', 'dp'), 0, 0, tiled=True)  12 us
    reshape x1, local copies, waits for them, and re-layouts, on_device(): arrived.reshape(experts * CAP, -1)  10.6 us
    reshape x1, local copies, waits for them, and re-layouts, on_device(): expert_ffn(arrived.reshape(experts * CAP, -1), *own).reshape(arrived.shape)  10.1 us
  transfers between devices with their start and end apart: 9, of which 5 were waited for; matrix products, arithmetic and copies ran while one was open for 24% of the time, Pallas kernels for 0%

profile of v9, /device:TPU:1, one launch (start us, length us, event | category | flops | bytes accessed | tf_op | source)
XLA Modules:
  0.0 394.6 jit_solution(14316305268438261335)
XLA Ops:
  9.6 2.9 fusion.12
  14.3 6.7 %copy.92 = bf16[128,6,4096]{2,1,0:T(8,128)(2,1)} copy(bf16[128,6,4096]{2,0,1:T(8,128)(2,1)S(1)} %convolution_convert_fusion) | data formatting | bytes 12582912 | tf_op jit(solution)/shard_map/dispatch/convert_element_type | solution.py:103
  21.0 12.0 %all-to-all-start = ((bf16[128,6,4096]{2,1,0:T(8,128)(2,1)}), bf16[128,6,4096]{2,1,0:T(8,128)(2,1)}, u32[]{:S(2)}, u32[]{:S(2)}) async-start(bf16[128,6,4096]{2,1,0:T(8,128)(2,1)} %copy.92), calls=%async_computation | async-start | bytes 16777216 | tf_op jit(solution)/shard_map/dispatch/all_to_all | solution.py:104
  33.1 3.3 select_bitcast_fusion.2
  37.6 4.8 %select_bitcast_fusion.1 = bf16[2048,768]{1,0:T(8,128)(2,1)} fusion(pred[]{:T(512)S(6)} %eq.106, bf16[1,4096,768]{2,1,0:T(8,128)(2,1)} %param.9), kind=kLoop, calls=%fused_computation.16 | loop fusion | flops 1572864 | bytes 9437185 | tf_op jit(solution)/shard_map/hot_weight_broadcast/jit(_where)/select_n | solution.py:121
  45.0 3.1 fusion.11
  48.1 3.0 copy.96
  51.2 3.1 fusion.10
  54.2 3.0 copy.97
  57.3 4.3 %bitcast_select_fusion = bf16[384,4096]{1,0:T(8,128)(2,1)} fusion(bf16[384,4096]{1,0:T(8,128)(2,1)} %collective-permute-done.4, pred[]{:T(512)S(6)} %eq.109, pred[]{:T(512)S(6)} %eq.106, pred[]{:T(512)S(6)} %eq.108, bf16[1,768,4096]{2,1,0:T(8,128)(2,1)} %param.10), kind=kLoop, calls=%fused_computation.10 | loop fusion | flops 4718592 | bytes 12582915 | tf_op jit(solution)/shard_map/hot_weight_broadcast/jit(_where)/select_n | solution.py:127
  61.6 84.4 %all-to-all-done = bf16[128,6,4096]{2,1,0:T(8,128)(2,1)} async-done(((bf16[128,6,4096]{2,1,0:T(8,128)(2,1)}), bf16[128,6,4096]{2,1,0:T(8,128)(2,1)}, u32[]{:S(2)}, u32[]{:S(2)}) %all-to-all-start) | async-done | bytes 6291488 | tf_op jit(solution)/shard_map/dispatch/all_to_all | solution.py:104
  146.0 10.6 %reshape.175 = bf16[768,4096]{1,0:T(8,128)(2,1)} reshape(bf16[128,6,4096]{2,1,0:T(8,128)(2,1)} %all-to-all-done) | data formatting | bytes 12582912 | tf_op jit(solution)/shard_map/expert_ffn/reshape | solution.py:133
  156.6 9.2 %fusion.3 = f32[768,768]{1,0:T(8,128)S(1)} fusion(bf16[768,4096]{1,0:T(8,128)(2,1)} %reshape.175, bf16[1,4096,768]{2,1,0:T(8,128)(2,1)} %param.8), kind=kOutput, calls=%fused_computation.5 | convolution fusion | flops 4831838208 | bytes 14942208 | tf_op jit(solution)/shard_map/expert_ffn/dot_general | solution.py:72
  165.9 5.2 %multiply_convert_fusion = bf16[768,768]{1,0:T(8,128)(2,1)S(1)} fusion(f32[768,768]{1,0:T(8,128)S(1)} %fusion.3, bf16[768,4096]{1,0:T(8,128)(2,1)S(1)} %copy-done, bf16[1,4096,768]{2,1,0:T(8,128)(2,1)S(1)} %bitcast.99), kind=kOutput, calls=%fused_computation.18 | convolution fusion | flops 4835377152 | bytes 16121856 | tf_op jit(solution)/shard_map/expert_ffn/dot_general | solution.py:73
  171.2 9.8 %convolution_convert_fusion.1 = bf16[768,4096]{1,0:T(8,128)(2,1)} fusion(bf16[768,768]{1,0:T(8,128)(2,1)S(1)} %multiply_convert_fusion, bf16[1,768,4096]{2,1,0:T(8,128)(2,1)} %param.10), kind=kOutput, calls=%fused_computation.1 | convolution fusion | flops 4834983936 | bytes 13762560 | tf_op jit(solution)/shard_map/expert_ffn/dot_general | solution.py:75
  180.9 10.1 %reshape.176 = bf16[128,6,4096]{2,1,0:T(8,128)(2,1)} reshape(bf16[768,4096]{1,0:T(8,128)(2,1)} %convolution_convert_fusion.1) | data formatting | bytes 12582912 | tf_op jit(solution)/shard_map/expert_ffn/reshape | solution.py:133
  191.1 12.8 %all-to-all-start.1 = ((bf16[128,6,4096]{2,1,0:T(8,128)(2,1)}), bf16[128,6,4096]{2,1,0:T(8,128)(2,1)}, u32[]{:S(2)}, u32[]{:S(2)}) async-start(bf16[128,6,4096]{2,1,0:T(8,128)(2,1)} %reshape.176), calls=%async_computation.1 | async-start | bytes 16777216 | tf_op jit(solution)/shard_map/return/all_to_all | solution.py:136
  205.5 3.6 select_reduce_fusion
  209.4 98.3 %all-to-all-done.1 = bf16[128,6,4096]{2,1,0:T(8,128)(2,1)} async-done(((bf16[128,6,4096]{2,1,0:T(8,128)(2,1)}), bf16[128,6,4096]{2,1,0:T(8,128)(2,1)}, u32[]{:S(2)}, u32[]{:S(2)}) %all-to-all-start.1) | async-done | bytes 6291488 | tf_op jit(solution)/shard_map/return/all_to_all | solution.py:136
  307.7 14.5 %fusion.7 = f32[96,4096]{1,0:T(8,128)} fusion(f32[128,6,96]{0,2,1:T(8,128)S(1)} %copy-done.6, bf16[128,6,4096]{2,1,0:T(8,128)(2,1)} %all-to-all-done.1), kind=kOutput, calls=%fused_computation.9 | convolution fusion | flops 3623878656 | bytes 8159232 | tf_op jit(solution)/shard_map/combine/esp,esd->pd/dot_general | solution.py:143
  326.5 46.5 %all-reduce.3.cloned.1.call-done = (bf16[384,4096]{1,0:T(8,128)(2,1)}, bf16[2,384,2048]{2,1,0:T(8,128)(2,1)}, bf16[2,384,2048]{2,1,0:T(8,128)(2,1)}) async-done(((bf16[384,4096]{1,0:T(8,128)(2,1)}, bf16[2,384,2048]{2,1,0:T(8,128)(2,1)}, bf16[2,384,2048]{2,1,0:T(8,128)(2,1)}), (bf16[384,4096]{1,0:T(8,128)(2,1)}, bf16[2,384,2048]{2,1,0:T(8,128)(2,1)}, ...) | async-done | bytes 9437200 | tf_op jit(solution)/shard_map/hot_weight_broadcast/psum | solution.py:130
  373.0 3.2 convolution_bitcast_fusion.1
  377.6 2.5 collective-permute-start.3
  383.4 3.0 collective-permute-done.5
  (69 shorter events, 20.1 us)
Async XLA Ops:
  6.5 2.9 copy-start.7
  6.5 2.9 copy-start.8
  6.5 5.9 %copy-start.3 = (bf16[96,4096]{1,0:T(8,128)(2,1)S(1)}, bf16[96,4096]{1,0:T(8,128)(2,1)}, u32[]{:S(2)}) copy-start(bf16[96,4096]{1,0:T(8,128)(2,1)} %param.7) | copy-start | bytes 2359300
  21.0 124.9 %all-to-all-start = ((bf16[128,6,4096]{2,1,0:T(8,128)(2,1)}), bf16[128,6,4096]{2,1,0:T(8,128)(2,1)}, u32[]{:S(2)}, u32[]{:S(2)}) async-start(bf16[128,6,4096]{2,1,0:T(8,128)(2,1)} %copy.92), calls=%async_computation | async-start | bytes 16777216 | tf_op jit(solution)/shard_map/dispatch/all_to_all | solution.py:104
  33.0 340.0 %all-reduce.3.cloned.1.call-start = ((), (), s32[]{:S(2)}) async-start(), calls=%async_computation.2 | async-start | bytes 18874368 | tf_op jit(solution)/shard_map/hot_weight_broadcast/psum | solution.py:130
  33.1 9.6 %slice-start.2 = ((s8[6291456]{0:T(1024)(128)(4,1)}), s8[4194304]{0:T(1024)(128)(4,1)S(1)}, s32[]{:S(2)}) async-start(s8[6291456]{0:T(1024)(128)(4,1)} %bitcast.100), calls=%async_computation.5 | async-start | bytes 8388608
  36.4 6.2 %slice-start.3 = ((s8[6291456]{0:T(1024)(128)(4,1)}), s8[2097152]{0:T(1024)(128)(4,1)S(1)}, s32[]{:S(2)}) async-start(s8[6291456]{0:T(1024)(128)(4,1)} %bitcast.100), calls=%async_computation.6 | async-start | bytes 4194304
  36.4 8.6 %collective-permute-start.1 = (bf16[2048,768]{1,0:T(8,128)(2,1)S(1)}, bf16[2048,768]{1,0:T(8,128)(2,1)}, u32[]{:S(2)}, u32[]{:S(2)}) collective-permute-start(bf16[2048,768]{1,0:T(8,128)(2,1)S(1)} %select_bitcast_fusion.2), channel_id=1, source_target_pairs={{0,1},{1,0},{2,3},{3,2},{4,5},{5,4},{6,7},{7,6},{8,9},{9,8},{10,11... | collective-permute-start | bytes 9437192 | tf_op jit(solution)/shard_map/hot_weight_broadcast/ppermute | solution.py:125
  42.5 8.7 %collective-permute-start.2 = (bf16[2048,768]{1,0:T(8,128)(2,1)}, bf16[2048,768]{1,0:T(8,128)(2,1)}, u32[]{:S(2)}, u32[]{:S(2)}) collective-permute-start(bf16[2048,768]{1,0:T(8,128)(2,1)} %select_bitcast_fusion.1), channel_id=1, source_target_pairs={{0,1},{1,0},{2,3},{3,2},{4,5},{5,4},{6,7},{7,6},{8,9},{9,8},{10,11... | collective-permute-start | bytes 9437192 | tf_op jit(solution)/shard_map/hot_weight_broadcast/ppermute | solution.py:125
  44.7 12.6 %collective-permute-start.4 = (bf16[384,4096]{1,0:T(8,128)(2,1)}, bf16[384,4096]{1,0:T(8,128)(2,1)}, u32[]{:S(2)}, u32[]{:S(2)}) collective-permute-start(bf16[384,4096]{1,0:T(8,128)(2,1)} %select_bitcast_fusion), channel_id=1, source_target_pairs={{0,1},{1,0},{2,3},{3,2},{4,5},{5,4},{6,7},{7,6},{8,9},{9,8},{10,11... | collective-permute-start | bytes 9437192 | tf_op jit(solution)/shard_map/hot_weight_broadcast/ppermute | solution.py:125
  146.0 19.9 %slice-start = ((s8[6291456]{0:T(1024)(128)(4,1)}), s8[2097152]{0:T(1024)(128)(4,1)S(1)}, s32[]{:S(2)}) async-start(s8[6291456]{0:T(1024)(128)(4,1)} %bitcast.98), calls=%async_computation.3 | async-start | bytes 4194304
  156.6 9.3 %slice-start.1 = ((s8[6291456]{0:T(1024)(128)(4,1)}), s8[4194304]{0:T(1024)(128)(4,1)S(1)}, s32[]{:S(2)}) async-start(s8[6291456]{0:T(1024)(128)(4,1)} %bitcast.98), calls=%async_computation.4 | async-start | bytes 8388608
  156.6 9.3 %copy-start = (bf16[768,4096]{1,0:T(8,128)(2,1)S(1)}, bf16[768,4096]{1,0:T(8,128)(2,1)}, u32[]{:S(2)}) copy-start(bf16[768,4096]{1,0:T(8,128)(2,1)} %reshape.175) | copy-start | bytes 18874372
  191.1 12.8 %copy-start.4 = (bf16[96,4096]{1,0:T(8,128)(2,1)S(1)}, bf16[96,4096]{1,0:T(8,128)(2,1)}, u32[]{:S(2)}) copy-start(bf16[96,4096]{1,0:T(8,128)(2,1)} %param.7) | copy-start | bytes 2359300
  191.1 116.6 %all-to-all-start.1 = ((bf16[128,6,4096]{2,1,0:T(8,128)(2,1)}), bf16[128,6,4096]{2,1,0:T(8,128)(2,1)}, u32[]{:S(2)}, u32[]{:S(2)}) async-start(bf16[128,6,4096]{2,1,0:T(8,128)(2,1)} %reshape.176), calls=%async_computation.1 | async-start | bytes 16777216 | tf_op jit(solution)/shard_map/return/all_to_all | solution.py:136
  203.9 5.1 %collective-permute-start = (bf16[96,4096]{1,0:T(8,128)(2,1)S(1)}, bf16[96,4096]{1,0:T(8,128)(2,1)S(1)}, u32[]{:S(2)}, u32[]{:S(2)}) collective-permute-start(bf16[96,4096]{1,0:T(8,128)(2,1)S(1)} %copy-done.4), channel_id=1, source_target_pairs={{0,1},{1,0},{2,3},{3,2},{4,5},{5,4},{6,7},{7,6},{8,9},{9,8},{10,11... | collective-permute-start | bytes 2359304 | tf_op jit(solution)/shard_map/hot_expert/ppermute | solution.py:152
  209.1 98.6 %copy-start.6 = (f32[128,6,96]{0,2,1:T(8,128)S(1)}, f32[128,6,96]{0,2,1:T(8,128)}, u32[]{:S(2)}) copy-start(f32[128,6,96]{0,2,1:T(8,128)} %select_reduce_fusion) | copy-start | bytes 884740
  373.0 3.2 copy-start.2
  377.5 4.3 %copy-start.1 = (bf16[384,4096]{1,0:T(8,128)(2,1)S(1)}, bf16[384,4096]{1,0:T(8,128)(2,1)}, u32[]{:S(2)}) copy-start(bf16[384,4096]{1,0:T(8,128)(2,1)} %get-tuple-element.9) | copy-start | bytes 9437188
  377.6 4.1 %collective-permute-start.3 = (f32[2,192,384]{2,1,0:T(8,128)S(1)}, f32[2,192,384]{2,1,0:T(8,128)S(1)}, u32[]{:S(2)}, u32[]{:S(2)}) collective-permute-start(f32[2,192,384]{2,1,0:T(8,128)S(1)} %select_bitcast_fusion.3), channel_id=1, source_target_pairs={{0,1},{1,0},{2,3},{3,2},{4,5},{5,4},{6,7},{7,6},{8,9},{9,8},{10,11... | collective-permute-start | bytes 1769480 | tf_op jit(solution)/shard_map/hot_expert/ppermute | solution.py:166
  382.8 3.7 copy-start.5
  383.0 3.5 collective-permute-start.5
Sparse Core Ops, SparseCore 0:
  61.7 311.2 all-reduce.2

commit v10 on v9

--- a/solution.py
+++ b/solution.py
@@ -97,10 +97,10 @@
         dispatch = jnp.any(hit.reshape(experts, CAP, tok_rows, top_k), axis=3)
 
     with jax.named_scope("dispatch"):
-        outgoing = jnp.einsum(
-            "esp,pd->esd", dispatch.astype(tokens.dtype), tokens,
+        outgoing = jnp.dot(
+            dispatch.reshape(experts * CAP, tok_rows).astype(tokens.dtype), tokens,
             preferred_element_type=jnp.float32,
-        ).astype(tokens.dtype)
+        ).astype(tokens.dtype).reshape(experts, CAP, -1)
         arrived = lax.all_to_all(outgoing, ("expert", "dp"), 0, 0, tiled=True)
 
     with jax.named_scope("hot_weight_broadcast"):

time: 394 us -> 404 us (1.025)
    reshape x0 -> x2, local copies, waits for them, and re-layouts: none -> 10.2 us  [the longest x1 10.1 us: on_device(): outgoing = jnp.dot(dispatch.reshape(experts * CAP, tok_rows).astype(token...]
    convert_element_type x1 -> x0, local copies, waits for them, and re-layouts: 6.74 us -> none  [on_device(): outgoing = jnp.einsum('esp,pd->esd', dispatch.astype(tokens.dtype), token...]
  transfers between devices with their start and end apart: 9 -> 9, of which waited for: 5 -> 5; matrix products, arithmetic and copies ran while one was open for 24% -> 23% of each run, Pallas kernels for 0% -> 0%
where the time goes in v10:
time: 404 us
  waiting for transfers between devices  234 us (58%)
  matrix products  48.9 us (12%)
  local copies, waits for them, and re-layouts  42.1 us (10%)
  starting transfers between devices  32.8 us (8%)
  other arithmetic  30.8 us (8%)
  between operations  14.4 us (4%)
    all_to_all x1, waiting for transfers between devices, on_device(): returned = lax.all_to_all(results, ('expert', 'dp'), 0, 0, tiled=True)  98.3 us
    all_to_all x1, waiting for transfers between devices, on_device(): arrived = lax.all_to_all(outgoing, ('expert', 'dp'), 0, 0, tiled=True)  84.7 us
    psum x1, waiting for transfers between devices, on_device(): hot_w = tuple((lax.psum(w, 'expert') for w in held))  46.7 us
    all_to_all x1, starting transfers between devices, on_device(): returned = lax.all_to_all(results, ('expert', 'dp'), 0, 0, tiled=True)  14.7 us
    dot_general x1, matrix products, on_device(): jnp.einsum('esp,esd->pd', combine, returned.astype(jnp.float32), precisio...  14.5 us
    all_to_all x1, starting transfers between devices, on_device(): arrived = lax.all_to_all(outgoing, ('expert', 'dp'), 0, 0, tiled=True)  12 us
    reshape x1, local copies, waits for them, and re-layouts, on_device(): arrived.reshape(experts * CAP, -1)  10.4 us
    reshape x1, local copies, waits for them, and re-layouts, on_device(): expert_ffn(arrived.reshape(experts * CAP, -1), *own).reshape(arrived.shape)  10.1 us
  transfers between devices with their start and end apart: 9, of which 5 were waited for; matrix products, arithmetic and copies ran while one was open for 23% of the time, Pallas kernels for 0%

profile of v10, /device:TPU:1, one launch (start us, length us, event | category | flops | bytes accessed | tf_op | source)
XLA Modules:
  0.0 403.5 jit_solution(12224334489458552056)
XLA Ops:
  9.6 2.9 fusion.12
  12.9 4.4 %convolution_convert_fusion = bf16[768,4096]{1,0:T(8,128)(2,1)} fusion(pred[768,96]{1,0:T(32,128)(4,1)S(1)} %reshape.181, bf16[96,4096]{1,0:T(8,128)(2,1)S(1)} %copy-done.3), kind=kOutput, calls=%fused_computation | convolution fusion | flops 607125504 | bytes 7151616 | tf_op jit(solution)/shard_map/dispatch/dot_general | solution.py:100
  17.3 10.1 %reshape.182 = bf16[128,6,4096]{2,1,0:T(8,128)(2,1)} reshape(bf16[768,4096]{1,0:T(8,128)(2,1)} %convolution_convert_fusion) | data formatting | bytes 12582912 | tf_op jit(solution)/shard_map/dispatch/reshape | solution.py:103
  27.4 12.0 %all-to-all-start = ((bf16[128,6,4096]{2,1,0:T(8,128)(2,1)}), bf16[128,6,4096]{2,1,0:T(8,128)(2,1)}, u32[]{:S(2)}, u32[]{:S(2)}) async-start(bf16[128,6,4096]{2,1,0:T(8,128)(2,1)} %reshape.182), calls=%async_computation | async-start | bytes 16777216 | tf_op jit(solution)/shard_map/dispatch/all_to_all | solution.py:104
  39.4 3.3 select_bitcast_fusion.2
  44.0 4.8 %select_bitcast_fusion.1 = bf16[2048,768]{1,0:T(8,128)(2,1)} fusion(pred[]{:T(512)S(6)} %eq.106, bf16[1,4096,768]{2,1,0:T(8,128)(2,1)} %param.9), kind=kLoop, calls=%fused_computation.16 | loop fusion | flops 1572864 | bytes 9437185 | tf_op jit(solution)/shard_map/hot_weight_broadcast/jit(_where)/select_n | solution.py:121
  51.4 3.1 fusion.11
  54.5 3.0 copy.94
  57.5 3.1 fusion.10
  60.6 3.0 copy.95
  63.6 4.3 %bitcast_select_fusion = bf16[384,4096]{1,0:T(8,128)(2,1)} fusion(bf16[384,4096]{1,0:T(8,128)(2,1)} %collective-permute-done.4, pred[]{:T(512)S(6)} %eq.109, pred[]{:T(512)S(6)} %eq.106, pred[]{:T(512)S(6)} %eq.108, bf16[1,768,4096]{2,1,0:T(8,128)(2,1)} %param.10), kind=kLoop, calls=%fused_computation.10 | loop fusion | flops 4718592 | bytes 12582915 | tf_op jit(solution)/shard_map/hot_weight_broadcast/jit(_where)/select_n | solution.py:127
  68.0 84.7 %all-to-all-done = bf16[128,6,4096]{2,1,0:T(8,128)(2,1)} async-done(((bf16[128,6,4096]{2,1,0:T(8,128)(2,1)}), bf16[128,6,4096]{2,1,0:T(8,128)(2,1)}, u32[]{:S(2)}, u32[]{:S(2)}) %all-to-all-start) | async-done | bytes 6291488 | tf_op jit(solution)/shard_map/dispatch/all_to_all | solution.py:104
  152.7 10.4 %reshape.183 = bf16[768,4096]{1,0:T(8,128)(2,1)} reshape(bf16[128,6,4096]{2,1,0:T(8,128)(2,1)} %all-to-all-done) | data formatting | bytes 12582912 | tf_op jit(solution)/shard_map/expert_ffn/reshape | solution.py:133
  163.1 9.4 %fusion.3 = f32[768,768]{1,0:T(8,128)S(1)} fusion(bf16[768,4096]{1,0:T(8,128)(2,1)} %reshape.183, bf16[1,4096,768]{2,1,0:T(8,128)(2,1)} %param.8), kind=kOutput, calls=%fused_computation.5 | convolution fusion | flops 4831838208 | bytes 14942208 | tf_op jit(solution)/shard_map/expert_ffn/dot_general | solution.py:72
  172.5 5.2 %multiply_convert_fusion = bf16[768,768]{1,0:T(8,128)(2,1)S(1)} fusion(f32[768,768]{1,0:T(8,128)S(1)} %fusion.3, bf16[768,4096]{1,0:T(8,128)(2,1)S(1)} %copy-done, bf16[1,4096,768]{2,1,0:T(8,128)(2,1)S(1)} %bitcast.97), kind=kOutput, calls=%fused_computation.18 | convolution fusion | flops 4835377152 | bytes 16121856 | tf_op jit(solution)/shard_map/expert_ffn/dot_general | solution.py:73
  177.7 9.9 %convolution_convert_fusion.1 = bf16[768,4096]{1,0:T(8,128)(2,1)} fusion(bf16[768,768]{1,0:T(8,128)(2,1)S(1)} %multiply_convert_fusion, bf16[1,768,4096]{2,1,0:T(8,128)(2,1)} %param.10), kind=kOutput, calls=%fused_computation.1 | convolution fusion | flops 4834983936 | bytes 13762560 | tf_op jit(solution)/shard_map/expert_ffn/dot_general | solution.py:75
  187.7 10.1 %reshape.184 = bf16[128,6,4096]{2,1,0:T(8,128)(2,1)} reshape(bf16[768,4096]{1,0:T(8,128)(2,1)} %convolution_convert_fusion.1) | data formatting | bytes 12582912 | tf_op jit(solution)/shard_map/expert_ffn/reshape | solution.py:133
  197.8 14.7 %all-to-all-start.1 = ((bf16[128,6,4096]{2,1,0:T(8,128)(2,1)}), bf16[128,6,4096]{2,1,0:T(8,128)(2,1)}, u32[]{:S(2)}, u32[]{:S(2)}) async-start(bf16[128,6,4096]{2,1,0:T(8,128)(2,1)} %reshape.184), calls=%async_computation.1 | async-start | bytes 16777216 | tf_op jit(solution)/shard_map/return/all_to_all | solution.py:136
  214.1 3.6 select_reduce_fusion
  218.0 98.3 %all-to-all-done.1 = bf16[128,6,4096]{2,1,0:T(8,128)(2,1)} async-done(((bf16[128,6,4096]{2,1,0:T(8,128)(2,1)}), bf16[128,6,4096]{2,1,0:T(8,128)(2,1)}, u32[]{:S(2)}, u32[]{:S(2)}) %all-to-all-start.1) | async-done | bytes 6291488 | tf_op jit(solution)/shard_map/return/all_to_all | solution.py:136
  316.4 14.5 %fusion.7 = f32[96,4096]{1,0:T(8,128)} fusion(f32[128,6,96]{0,2,1:T(8,128)S(1)} %copy-done.6, bf16[128,6,4096]{2,1,0:T(8,128)(2,1)} %all-to-all-done.1), kind=kOutput, calls=%fused_computation.9 | convolution fusion | flops 3623878656 | bytes 8159232 | tf_op jit(solution)/shard_map/combine/esp,esd->pd/dot_general | solution.py:143
  335.2 46.7 %all-reduce.3.cloned.1.call-done = (bf16[384,4096]{1,0:T(8,128)(2,1)}, bf16[2,384,2048]{2,1,0:T(8,128)(2,1)}, bf16[2,384,2048]{2,1,0:T(8,128)(2,1)}) async-done(((bf16[384,4096]{1,0:T(8,128)(2,1)}, bf16[2,384,2048]{2,1,0:T(8,128)(2,1)}, bf16[2,384,2048]{2,1,0:T(8,128)(2,1)}), (bf16[384,4096]{1,0:T(8,128)(2,1)}, bf16[2,384,2048]{2,1,0:T(8,128)(2,1)}, ...) | async-done | bytes 9437200 | tf_op jit(solution)/shard_map/hot_weight_broadcast/psum | solution.py:130
  381.9 3.2 convolution_bitcast_fusion.1
  392.3 3.0 collective-permute-done.5
  (71 shorter events, 21.1 us)
Async XLA Ops:
  6.5 2.9 copy-start.7
  6.5 2.9 copy-start.8
  6.5 6.3 %copy-start.3 = (bf16[96,4096]{1,0:T(8,128)(2,1)S(1)}, bf16[96,4096]{1,0:T(8,128)(2,1)}, u32[]{:S(2)}) copy-start(bf16[96,4096]{1,0:T(8,128)(2,1)} %param.7) | copy-start | bytes 2359300
  27.4 125.3 %all-to-all-start = ((bf16[128,6,4096]{2,1,0:T(8,128)(2,1)}), bf16[128,6,4096]{2,1,0:T(8,128)(2,1)}, u32[]{:S(2)}, u32[]{:S(2)}) async-start(bf16[128,6,4096]{2,1,0:T(8,128)(2,1)} %reshape.182), calls=%async_computation | async-start | bytes 16777216 | tf_op jit(solution)/shard_map/dispatch/all_to_all | solution.py:104
  39.4 342.6 %all-reduce.3.cloned.1.call-start = ((), (), s32[]{:S(2)}) async-start(), calls=%async_computation.2 | async-start | bytes 18874368 | tf_op jit(solution)/shard_map/hot_weight_broadcast/psum | solution.py:130
  39.4 9.6 %slice-start.2 = ((s8[6291456]{0:T(1024)(128)(4,1)}), s8[4194304]{0:T(1024)(128)(4,1)S(1)}, s32[]{:S(2)}) async-start(s8[6291456]{0:T(1024)(128)(4,1)} %bitcast.98), calls=%async_computation.5 | async-start | bytes 8388608
  42.8 6.2 %slice-start.3 = ((s8[6291456]{0:T(1024)(128)(4,1)}), s8[2097152]{0:T(1024)(128)(4,1)S(1)}, s32[]{:S(2)}) async-start(s8[6291456]{0:T(1024)(128)(4,1)} %bitcast.98), calls=%async_computation.6 | async-start | bytes 4194304
  42.8 8.6 %collective-permute-start.1 = (bf16[2048,768]{1,0:T(8,128)(2,1)S(1)}, bf16[2048,768]{1,0:T(8,128)(2,1)}, u32[]{:S(2)}, u32[]{:S(2)}) collective-permute-start(bf16[2048,768]{1,0:T(8,128)(2,1)S(1)} %select_bitcast_fusion.2), channel_id=1, source_target_pairs={{0,1},{1,0},{2,3},{3,2},{4,5},{5,4},{6,7},{7,6},{8,9},{9,8},{10,11... | collective-permute-start | bytes 9437192 | tf_op jit(solution)/shard_map/hot_weight_broadcast/ppermute | solution.py:125
  48.8 8.7 %collective-permute-start.2 = (bf16[2048,768]{1,0:T(8,128)(2,1)}, bf16[2048,768]{1,0:T(8,128)(2,1)}, u32[]{:S(2)}, u32[]{:S(2)}) collective-permute-start(bf16[2048,768]{1,0:T(8,128)(2,1)} %select_bitcast_fusion.1), channel_id=1, source_target_pairs={{0,1},{1,0},{2,3},{3,2},{4,5},{5,4},{6,7},{7,6},{8,9},{9,8},{10,11... | collective-permute-start | bytes 9437192 | tf_op jit(solution)/shard_map/hot_weight_broadcast/ppermute | solution.py:125
  51.0 12.6 %collective-permute-start.4 = (bf16[384,4096]{1,0:T(8,128)(2,1)}, bf16[384,4096]{1,0:T(8,128)(2,1)}, u32[]{:S(2)}, u32[]{:S(2)}) collective-permute-start(bf16[384,4096]{1,0:T(8,128)(2,1)} %select_bitcast_fusion), channel_id=1, source_target_pairs={{0,1},{1,0},{2,3},{3,2},{4,5},{5,4},{6,7},{7,6},{8,9},{9,8},{10,11... | collective-permute-start | bytes 9437192 | tf_op jit(solution)/shard_map/hot_weight_broadcast/ppermute | solution.py:125
  152.7 19.8 %slice-start = ((s8[6291456]{0:T(1024)(128)(4,1)}), s8[2097152]{0:T(1024)(128)(4,1)S(1)}, s32[]{:S(2)}) async-start(s8[6291456]{0:T(1024)(128)(4,1)} %bitcast.96), calls=%async_computation.3 | async-start | bytes 4194304
  163.1 9.4 %slice-start.1 = ((s8[6291456]{0:T(1024)(128)(4,1)}), s8[4194304]{0:T(1024)(128)(4,1)S(1)}, s32[]{:S(2)}) async-start(s8[6291456]{0:T(1024)(128)(4,1)} %bitcast.96), calls=%async_computation.4 | async-start | bytes 8388608
  163.1 9.4 %copy-start = (bf16[768,4096]{1,0:T(8,128)(2,1)S(1)}, bf16[768,4096]{1,0:T(8,128)(2,1)}, u32[]{:S(2)}) copy-start(bf16[768,4096]{1,0:T(8,128)(2,1)} %reshape.183) | copy-start | bytes 18874372
  197.8 14.8 %copy-start.4 = (bf16[96,4096]{1,0:T(8,128)(2,1)S(1)}, bf16[96,4096]{1,0:T(8,128)(2,1)}, u32[]{:S(2)}) copy-start(bf16[96,4096]{1,0:T(8,128)(2,1)} %param.7) | copy-start | bytes 2359300
  197.8 118.6 %all-to-all-start.1 = ((bf16[128,6,4096]{2,1,0:T(8,128)(2,1)}), bf16[128,6,4096]{2,1,0:T(8,128)(2,1)}, u32[]{:S(2)}, u32[]{:S(2)}) async-start(bf16[128,6,4096]{2,1,0:T(8,128)(2,1)} %reshape.184), calls=%async_computation.1 | async-start | bytes 16777216 | tf_op jit(solution)/shard_map/return/all_to_all | solution.py:136
  212.6 5.1 %collective-permute-start = (bf16[96,4096]{1,0:T(8,128)(2,1)S(1)}, bf16[96,4096]{1,0:T(8,128)(2,1)S(1)}, u32[]{:S(2)}, u32[]{:S(2)}) collective-permute-start(bf16[96,4096]{1,0:T(8,128)(2,1)S(1)} %copy-done.4), channel_id=1, source_target_pairs={{0,1},{1,0},{2,3},{3,2},{4,5},{5,4},{6,7},{7,6},{8,9},{9,8},{10,11... | collective-permute-start | bytes 2359304 | tf_op jit(solution)/shard_map/hot_expert/ppermute | solution.py:152
  217.7 98.7 %copy-start.6 = (f32[128,6,96]{0,2,1:T(8,128)S(1)}, f32[128,6,96]{0,2,1:T(8,128)}, u32[]{:S(2)}) copy-start(f32[128,6,96]{0,2,1:T(8,128)} %select_reduce_fusion) | copy-start | bytes 884740
  381.9 3.2 copy-start.2
  386.4 4.3 %copy-start.1 = (bf16[384,4096]{1,0:T(8,128)(2,1)S(1)}, bf16[384,4096]{1,0:T(8,128)(2,1)}, u32[]{:S(2)}) copy-start(bf16[384,4096]{1,0:T(8,128)(2,1)} %get-tuple-element.9) | copy-start | bytes 9437188
  386.4 4.1 %collective-permute-start.3 = (f32[2,192,384]{2,1,0:T(8,128)S(1)}, f32[2,192,384]{2,1,0:T(8,128)S(1)}, u32[]{:S(2)}, u32[]{:S(2)}) collective-permute-start(f32[2,192,384]{2,1,0:T(8,128)S(1)} %select_bitcast_fusion.3), channel_id=1, source_target_pairs={{0,1},{1,0},{2,3},{3,2},{4,5},{5,4},{6,7},{7,6},{8,9},{9,8},{10,11... | collective-permute-start | bytes 1769480 | tf_op jit(solution)/shard_map/hot_expert/ppermute | solution.py:166
  391.7 3.7 copy-start.5
  391.9 3.5 collective-permute-start.5
Sparse Core Ops, SparseCore 0:
  68.1 313.7 all-reduce.2

commit v11 on v9

--- a/solution.py
+++ b/solution.py
@@ -169,7 +169,8 @@
         by_core = partial.reshape(2, tok_rows, partial.shape[1])
         own_rows = jnp.where(core == 0, by_core[0], by_core[1])
         other_rows = jnp.where(core == 0, by_core[1], by_core[0])
-        hot_out = (own_rows + lax.ppermute(other_rows, "dp", swap)).astype(jnp.bfloat16)
+        other_half = lax.ppermute(other_rows.astype(jnp.bfloat16), "dp", swap)
+        hot_out = (own_rows + other_half.astype(jnp.float32)).astype(jnp.bfloat16)
         hot_weight = jnp.sum(
             jnp.where(route_ids == hot_id, route_gates, jnp.zeros_like(route_gates)), axis=1
         )

time: 394 us -> 393 us (level)
  waiting for transfers between devices: 234 us -> 230 us
where the time goes in v11:
time: 393 us; the launch traced here: 391 us
  waiting for transfers between devices  230 us (59%)
  matrix products  46 us (12%)
  local copies, waits for them, and re-layouts  38.5 us (10%)
  starting transfers between devices  31 us (8%)
  other arithmetic  30.8 us (8%)
  between operations  14.4 us (4%)
    all_to_all x1, waiting for transfers between devices, on_device(): returned = lax.all_to_all(results, ('expert', 'dp'), 0, 0, tiled=True)  98.6 us
    all_to_all x1, waiting for transfers between devices, on_device(): arrived = lax.all_to_all(outgoing, ('expert', 'dp'), 0, 0, tiled=True)  84.3 us
    psum x1, waiting for transfers between devices, on_device(): hot_w = tuple((lax.psum(w, 'expert') for w in held))  43.9 us
    dot_general x1, matrix products, on_device(): jnp.einsum('esp,esd->pd', combine, returned.astype(jnp.float32), precisio...  14.5 us
    all_to_all x1, starting transfers between devices, on_device(): returned = lax.all_to_all(results, ('expert', 'dp'), 0, 0, tiled=True)  13 us
    all_to_all x1, starting transfers between devices, on_device(): arrived = lax.all_to_all(outgoing, ('expert', 'dp'), 0, 0, tiled=True)  12 us
    reshape x1, local copies, waits for them, and re-layouts, on_device(): arrived.reshape(experts * CAP, -1)  10.6 us
    reshape x1, local copies, waits for them, and re-layouts, on_device(): expert_ffn(arrived.reshape(experts * CAP, -1), *own).reshape(arrived.shape)  10.1 us
  transfers between devices with their start and end apart: 9, of which 5 were waited for; matrix products, arithmetic and copies ran while one was open for 24% of the time, Pallas kernels for 0%

profile of v11, /device:TPU:1, one launch (start us, length us, event | category | flops | bytes accessed | tf_op | source)
XLA Modules:
  0.0 391.1 jit_solution(6954789371460848513)
XLA Ops:
  9.6 2.9 fusion.12
  14.3 6.7 %copy.92 = bf16[128,6,4096]{2,1,0:T(8,128)(2,1)} copy(bf16[128,6,4096]{2,0,1:T(8,128)(2,1)S(1)} %convolution_convert_fusion) | data formatting | bytes 12582912 | tf_op jit(solution)/shard_map/dispatch/convert_element_type | solution.py:103
  21.0 12.0 %all-to-all-start = ((bf16[128,6,4096]{2,1,0:T(8,128)(2,1)}), bf16[128,6,4096]{2,1,0:T(8,128)(2,1)}, u32[]{:S(2)}, u32[]{:S(2)}) async-start(bf16[128,6,4096]{2,1,0:T(8,128)(2,1)} %copy.92), calls=%async_computation | async-start | bytes 16777216 | tf_op jit(solution)/shard_map/dispatch/all_to_all | solution.py:104
  33.1 3.3 select_bitcast_fusion.2
  37.6 4.8 %select_bitcast_fusion.1 = bf16[2048,768]{1,0:T(8,128)(2,1)} fusion(pred[]{:T(512)S(6)} %eq.106, bf16[1,4096,768]{2,1,0:T(8,128)(2,1)} %param.9), kind=kLoop, calls=%fused_computation.16 | loop fusion | flops 1572864 | bytes 9437185 | tf_op jit(solution)/shard_map/hot_weight_broadcast/jit(_where)/select_n | solution.py:121
  45.0 3.1 fusion.11
  48.1 3.0 copy.96
  51.2 3.1 fusion.10
  54.2 3.0 copy.97
  57.3 4.3 %bitcast_select_fusion = bf16[384,4096]{1,0:T(8,128)(2,1)} fusion(bf16[384,4096]{1,0:T(8,128)(2,1)} %collective-permute-done.4, pred[]{:T(512)S(6)} %eq.109, pred[]{:T(512)S(6)} %eq.106, pred[]{:T(512)S(6)} %eq.108, bf16[1,768,4096]{2,1,0:T(8,128)(2,1)} %param.10), kind=kLoop, calls=%fused_computation.10 | loop fusion | flops 4718592 | bytes 12582915 | tf_op jit(solution)/shard_map/hot_weight_broadcast/jit(_where)/select_n | solution.py:127
  61.6 84.3 %all-to-all-done = bf16[128,6,4096]{2,1,0:T(8,128)(2,1)} async-done(((bf16[128,6,4096]{2,1,0:T(8,128)(2,1)}), bf16[128,6,4096]{2,1,0:T(8,128)(2,1)}, u32[]{:S(2)}, u32[]{:S(2)}) %all-to-all-start) | async-done | bytes 6291488 | tf_op jit(solution)/shard_map/dispatch/all_to_all | solution.py:104
  145.9 10.6 %reshape.175 = bf16[768,4096]{1,0:T(8,128)(2,1)} reshape(bf16[128,6,4096]{2,1,0:T(8,128)(2,1)} %all-to-all-done) | data formatting | bytes 12582912 | tf_op jit(solution)/shard_map/expert_ffn/reshape | solution.py:133
  156.5 9.2 %fusion.3 = f32[768,768]{1,0:T(8,128)S(1)} fusion(bf16[768,4096]{1,0:T(8,128)(2,1)} %reshape.175, bf16[1,4096,768]{2,1,0:T(8,128)(2,1)} %param.8), kind=kOutput, calls=%fused_computation.5 | convolution fusion | flops 4831838208 | bytes 14942208 | tf_op jit(solution)/shard_map/expert_ffn/dot_general | solution.py:72
  165.8 5.2 %multiply_convert_fusion = bf16[768,768]{1,0:T(8,128)(2,1)S(1)} fusion(f32[768,768]{1,0:T(8,128)S(1)} %fusion.3, bf16[768,4096]{1,0:T(8,128)(2,1)S(1)} %copy-done, bf16[1,4096,768]{2,1,0:T(8,128)(2,1)S(1)} %bitcast.99), kind=kOutput, calls=%fused_computation.18 | convolution fusion | flops 4835377152 | bytes 16121856 | tf_op jit(solution)/shard_map/expert_ffn/dot_general | solution.py:73
  171.0 9.8 %convolution_convert_fusion.1 = bf16[768,4096]{1,0:T(8,128)(2,1)} fusion(bf16[768,768]{1,0:T(8,128)(2,1)S(1)} %multiply_convert_fusion, bf16[1,768,4096]{2,1,0:T(8,128)(2,1)} %param.10), kind=kOutput, calls=%fused_computation.1 | convolution fusion | flops 4834983936 | bytes 13762560 | tf_op jit(solution)/shard_map/expert_ffn/dot_general | solution.py:75
  180.8 10.1 %reshape.176 = bf16[128,6,4096]{2,1,0:T(8,128)(2,1)} reshape(bf16[768,4096]{1,0:T(8,128)(2,1)} %convolution_convert_fusion.1) | data formatting | bytes 12582912 | tf_op jit(solution)/shard_map/expert_ffn/reshape | solution.py:133
  191.0 13.0 %all-to-all-start.1 = ((bf16[128,6,4096]{2,1,0:T(8,128)(2,1)}), bf16[128,6,4096]{2,1,0:T(8,128)(2,1)}, u32[]{:S(2)}, u32[]{:S(2)}) async-start(bf16[128,6,4096]{2,1,0:T(8,128)(2,1)} %reshape.176), calls=%async_computation.1 | async-start | bytes 16777216 | tf_op jit(solution)/shard_map/return/all_to_all | solution.py:136
  205.5 3.6 select_reduce_fusion
  209.4 98.6 %all-to-all-done.1 = bf16[128,6,4096]{2,1,0:T(8,128)(2,1)} async-done(((bf16[128,6,4096]{2,1,0:T(8,128)(2,1)}), bf16[128,6,4096]{2,1,0:T(8,128)(2,1)}, u32[]{:S(2)}, u32[]{:S(2)}) %all-to-all-start.1) | async-done | bytes 6291488 | tf_op jit(solution)/shard_map/return/all_to_all | solution.py:136
  308.0 14.5 %fusion.7 = f32[96,4096]{1,0:T(8,128)} fusion(f32[128,6,96]{0,2,1:T(8,128)S(1)} %copy-done.6, bf16[128,6,4096]{2,1,0:T(8,128)(2,1)} %all-to-all-done.1), kind=kOutput, calls=%fused_computation.9 | convolution fusion | flops 3623878656 | bytes 8159232 | tf_op jit(solution)/shard_map/combine/esp,esd->pd/dot_general | solution.py:143
  323.7 2.2 fusion.30
  326.9 43.9 %all-reduce.3.cloned.1.call-done = (bf16[384,4096]{1,0:T(8,128)(2,1)}, bf16[2,384,2048]{2,1,0:T(8,128)(2,1)}, bf16[2,384,2048]{2,1,0:T(8,128)(2,1)}) async-done(((bf16[384,4096]{1,0:T(8,128)(2,1)}, bf16[2,384,2048]{2,1,0:T(8,128)(2,1)}, bf16[2,384,2048]{2,1,0:T(8,128)(2,1)}), (bf16[384,4096]{1,0:T(8,128)(2,1)}, bf16[2,384,2048]{2,1,0:T(8,128)(2,1)}, ...) | async-done | bytes 9437200 | tf_op jit(solution)/shard_map/hot_weight_broadcast/psum | solution.py:130
  370.7 3.2 convolution_bitcast_fusion.1
  375.3 2.5 collective-permute-start.3
  (69 shorter events, 19.7 us)
Async XLA Ops:
  6.5 2.9 copy-start.7
  6.5 2.9 copy-start.8
  6.5 5.9 %copy-start.3 = (bf16[96,4096]{1,0:T(8,128)(2,1)S(1)}, bf16[96,4096]{1,0:T(8,128)(2,1)}, u32[]{:S(2)}) copy-start(bf16[96,4096]{1,0:T(8,128)(2,1)} %param.7) | copy-start | bytes 2359300
  21.0 124.9 %all-to-all-start = ((bf16[128,6,4096]{2,1,0:T(8,128)(2,1)}), bf16[128,6,4096]{2,1,0:T(8,128)(2,1)}, u32[]{:S(2)}, u32[]{:S(2)}) async-start(bf16[128,6,4096]{2,1,0:T(8,128)(2,1)} %copy.92), calls=%async_computation | async-start | bytes 16777216 | tf_op jit(solution)/shard_map/dispatch/all_to_all | solution.py:104
  33.0 337.7 %all-reduce.3.cloned.1.call-start = ((), (), s32[]{:S(2)}) async-start(), calls=%async_computation.2 | async-start | bytes 18874368 | tf_op jit(solution)/shard_map/hot_weight_broadcast/psum | solution.py:130
  33.1 9.6 %slice-start.2 = ((s8[6291456]{0:T(1024)(128)(4,1)}), s8[4194304]{0:T(1024)(128)(4,1)S(1)}, s32[]{:S(2)}) async-start(s8[6291456]{0:T(1024)(128)(4,1)} %bitcast.100), calls=%async_computation.5 | async-start | bytes 8388608
  36.4 6.2 %slice-start.3 = ((s8[6291456]{0:T(1024)(128)(4,1)}), s8[2097152]{0:T(1024)(128)(4,1)S(1)}, s32[]{:S(2)}) async-start(s8[6291456]{0:T(1024)(128)(4,1)} %bitcast.100), calls=%async_computation.6 | async-start | bytes 4194304
  36.4 8.6 %collective-permute-start.1 = (bf16[2048,768]{1,0:T(8,128)(2,1)S(1)}, bf16[2048,768]{1,0:T(8,128)(2,1)}, u32[]{:S(2)}, u32[]{:S(2)}) collective-permute-start(bf16[2048,768]{1,0:T(8,128)(2,1)S(1)} %select_bitcast_fusion.2), channel_id=1, source_target_pairs={{0,1},{1,0},{2,3},{3,2},{4,5},{5,4},{6,7},{7,6},{8,9},{9,8},{10,11... | collective-permute-start | bytes 9437192 | tf_op jit(solution)/shard_map/hot_weight_broadcast/ppermute | solution.py:125
  42.5 8.7 %collective-permute-start.2 = (bf16[2048,768]{1,0:T(8,128)(2,1)}, bf16[2048,768]{1,0:T(8,128)(2,1)}, u32[]{:S(2)}, u32[]{:S(2)}) collective-permute-start(bf16[2048,768]{1,0:T(8,128)(2,1)} %select_bitcast_fusion.1), channel_id=1, source_target_pairs={{0,1},{1,0},{2,3},{3,2},{4,5},{5,4},{6,7},{7,6},{8,9},{9,8},{10,11... | collective-permute-start | bytes 9437192 | tf_op jit(solution)/shard_map/hot_weight_broadcast/ppermute | solution.py:125
  44.7 12.6 %collective-permute-start.4 = (bf16[384,4096]{1,0:T(8,128)(2,1)}, bf16[384,4096]{1,0:T(8,128)(2,1)}, u32[]{:S(2)}, u32[]{:S(2)}) collective-permute-start(bf16[384,4096]{1,0:T(8,128)(2,1)} %select_bitcast_fusion), channel_id=1, source_target_pairs={{0,1},{1,0},{2,3},{3,2},{4,5},{5,4},{6,7},{7,6},{8,9},{9,8},{10,11... | collective-permute-start | bytes 9437192 | tf_op jit(solution)/shard_map/hot_weight_broadcast/ppermute | solution.py:125
  145.9 19.9 %slice-start = ((s8[6291456]{0:T(1024)(128)(4,1)}), s8[2097152]{0:T(1024)(128)(4,1)S(1)}, s32[]{:S(2)}) async-start(s8[6291456]{0:T(1024)(128)(4,1)} %bitcast.98), calls=%async_computation.3 | async-start | bytes 4194304
  156.5 9.3 %slice-start.1 = ((s8[6291456]{0:T(1024)(128)(4,1)}), s8[4194304]{0:T(1024)(128)(4,1)S(1)}, s32[]{:S(2)}) async-start(s8[6291456]{0:T(1024)(128)(4,1)} %bitcast.98), calls=%async_computation.4 | async-start | bytes 8388608
  156.5 9.3 %copy-start = (bf16[768,4096]{1,0:T(8,128)(2,1)S(1)}, bf16[768,4096]{1,0:T(8,128)(2,1)}, u32[]{:S(2)}) copy-start(bf16[768,4096]{1,0:T(8,128)(2,1)} %reshape.175) | copy-start | bytes 18874372
  191.0 13.0 %copy-start.4 = (bf16[96,4096]{1,0:T(8,128)(2,1)S(1)}, bf16[96,4096]{1,0:T(8,128)(2,1)}, u32[]{:S(2)}) copy-start(bf16[96,4096]{1,0:T(8,128)(2,1)} %param.7) | copy-start | bytes 2359300
  191.0 117.1 %all-to-all-start.1 = ((bf16[128,6,4096]{2,1,0:T(8,128)(2,1)}), bf16[128,6,4096]{2,1,0:T(8,128)(2,1)}, u32[]{:S(2)}, u32[]{:S(2)}) async-start(bf16[128,6,4096]{2,1,0:T(8,128)(2,1)} %reshape.176), calls=%async_computation.1 | async-start | bytes 16777216 | tf_op jit(solution)/shard_map/return/all_to_all | solution.py:136
  203.9 5.1 %collective-permute-start = (bf16[96,4096]{1,0:T(8,128)(2,1)S(1)}, bf16[96,4096]{1,0:T(8,128)(2,1)S(1)}, u32[]{:S(2)}, u32[]{:S(2)}) collective-permute-start(bf16[96,4096]{1,0:T(8,128)(2,1)S(1)} %copy-done.4), channel_id=1, source_target_pairs={{0,1},{1,0},{2,3},{3,2},{4,5},{5,4},{6,7},{7,6},{8,9},{9,8},{10,11... | collective-permute-start | bytes 2359304 | tf_op jit(solution)/shard_map/hot_expert/ppermute | solution.py:152
  209.1 99.0 %copy-start.6 = (f32[128,6,96]{0,2,1:T(8,128)S(1)}, f32[128,6,96]{0,2,1:T(8,128)}, u32[]{:S(2)}) copy-start(f32[128,6,96]{0,2,1:T(8,128)} %select_reduce_fusion) | copy-start | bytes 884740
  370.7 3.2 copy-start.2
  375.2 4.3 %copy-start.1 = (bf16[384,4096]{1,0:T(8,128)(2,1)S(1)}, bf16[384,4096]{1,0:T(8,128)(2,1)}, u32[]{:S(2)}) copy-start(bf16[384,4096]{1,0:T(8,128)(2,1)} %get-tuple-element.9) | copy-start | bytes 9437188
  375.3 4.1 %collective-permute-start.3 = (f32[2,192,384]{2,1,0:T(8,128)S(1)}, f32[2,192,384]{2,1,0:T(8,128)S(1)}, u32[]{:S(2)}, u32[]{:S(2)}) collective-permute-start(f32[2,192,384]{2,1,0:T(8,128)S(1)} %select_bitcast_fusion.3), channel_id=1, source_target_pairs={{0,1},{1,0},{2,3},{3,2},{4,5},{5,4},{6,7},{7,6},{8,9},{9,8},{10,11... | collective-permute-start | bytes 1769480 | tf_op jit(solution)/shard_map/hot_expert/ppermute | solution.py:166
  379.5 3.5 copy-start.5
  380.7 2.4 collective-permute-start.5
Sparse Core Ops, SparseCore 0:
  61.7 308.9 all-reduce.2
